TPU v7x, 1024 devices: a whole 4x4x32 slice. The times are simulated.
1024 devices in a mesh: comp: 4 (over y), ty: 8 (over z_lo), tx: 32 (over z_hi, x, core).
Axes of the slice: x: 4, y: 4, z: 32 (z_hi: 4, z_lo: 8; z = z_hi * 8 + z_lo), core: 2. Of those that a mesh axis runs over, the one named last changes fastest.
Arguments:
- ocean: float32 [3, 256, 8192], P(None, 'ty', 'tx'), may hold values from -4 to 4
- tracers: float32 [19, 8, 32, 8192], P(None, 'ty', 'comp', 'tx'), may hold values from 0.05 to 3
- bottom: int32 [256, 128], P('ty', 'tx'), may hold values from 0 to 64, as said below
- stoich: float32 [14], replicated, may hold values from -3 to 3
Outputs:
- ocean_out: float32 [3, 256, 8192], P(None, 'ty', 'tx')
- tracers_out: float32 [19, 8, 32, 8192], P(None, 'ty', 'comp', 'tx')
Inputs may be any that keep to these rules, and one draw needn't show every extreme that they name: bottom counts wet levels from the surface; 0 marks land, 64 a full column.
All inputs are finite; a program needn't handle non-finite values.
Results may differ from a plain program's by a relative error of at most 0.0003.
Values sent between devices are 32-bit elements; how exact they have to be, the bound alone decides.
No kernel may reach another device: no remote copies, remote signals or barrier semaphores. Data moves between devices by JAX's collectives and lax.ppermute only.
A program may use at most 32 MiB of HBM per device.

v0:
```python
import jax
import jax.numpy as jnp
from jax import lax
from jax.sharding import PartitionSpec as P

LEV = 64
STEPS = 2


ATTEN_WATER = 0.04
ATTEN_CHL = 0.03
PRESSURE = 0.05
TIME_STEP = 0.2
CORIOLIS = 1.0
DAMPING = 0.05
HEAT_GAIN = 2.0
DIFFUSE = 0.2
ADVECT = 0.08
GROWTH = 1.0
HALF_LIGHT = 0.2
HALF_NUTRIENT = 0.5
TEMP_COEF = 0.1
GRAZE = 0.8
HALF_PREY = 0.3
MORTAL = 0.1
REMIN = 0.2
CHL_RELAX = 0.3
CHL_RATIO = 0.5
CHL_GAIN = 0.2
ASSIM = 0.3
GRAZER_LOSS = 0.05
REACT_STEP = 0.2


def extended_2(cells, sides, width, closed):
    for axis, dim in sides:
        count = lax.axis_size(axis)
        ends = count if closed else count - 1
        head = lax.slice_in_dim(cells, 0, width, axis=dim)
        tail = lax.slice_in_dim(cells, cells.shape[dim] - width, cells.shape[dim], axis=dim)
        cells = jnp.concatenate(
            [
                lax.ppermute(tail, axis, [(i, (i + 1) % count) for i in range(ends)]),
                cells,
                lax.ppermute(head, axis, [((i + 1) % count, i) for i in range(ends)]),
            ],
            axis=dim,
        )
    return cells


def level_sums(values, inclusive):
    count = values.shape[-1]
    level_ids = jnp.arange(count)
    if inclusive:
        ladder = level_ids[:, None] <= level_ids[None, :]
    else:
        ladder = level_ids[:, None] < level_ids[None, :]
    return jnp.dot(values, ladder.astype(jnp.float32), precision=lax.Precision.HIGHEST)


def optics(chloro, wet_mask):
    absorb = (ATTEN_WATER + ATTEN_CHL * jnp.maximum(chloro, 0.0)) * wet_mask
    sunlight = jnp.exp(-level_sums(absorb, False))
    heating = sunlight * (1.0 - jnp.exp(-absorb)) * wet_mask
    return (sunlight, heating)


def ocean_update(current, row_margin, column_margin, heating, wet_mask):
    east = current[0]
    north = current[1]
    temper = current[2]
    press_rows = PRESSURE * level_sums(row_margin, True)
    press_cols = PRESSURE * level_sums(column_margin, True)
    slope_x = 0.5 * (press_cols[:, 2:] - press_cols[:, :-2])
    slope_y = 0.5 * (press_rows[2:] - press_rows[:-2])
    spread = (
        row_margin[2:]
        + row_margin[:-2]
        + column_margin[:, 2:]
        + column_margin[:, :-2]
        - 4.0 * temper
    )
    new_east = wet_mask * ((1.0 - DAMPING) * east + TIME_STEP * (CORIOLIS * north - slope_x))
    new_north = wet_mask * ((1.0 - DAMPING) * north - TIME_STEP * (CORIOLIS * east + slope_y))
    new_temp = wet_mask * (temper + TIME_STEP * (HEAT_GAIN * heating + DIFFUSE * spread))
    return jnp.stack([new_east, new_north, new_temp])


def minmod(first, second):
    return jnp.where(
        first * second > 0.0, jnp.sign(first) * jnp.minimum(jnp.abs(first), jnp.abs(second)), 0.0
    )


def face_transport(field_wide, speed_wide, wet_wide, along_dim, cell_count):

    def window(values, offset):
        return lax.slice_in_dim(values, offset, offset + cell_count + 1, axis=along_dim)

    far_left = window(field_wide, 0)
    left_cell = window(field_wide, 1)
    right_cell = window(field_wide, 2)
    far_right = window(field_wide, 3)
    speed = (
        0.5
        * (window(speed_wide, 1) + window(speed_wide, 2))
        * window(wet_wide, 1)
        * window(wet_wide, 2)
    )
    from_left = left_cell + 0.5 * minmod(left_cell - far_left, right_cell - left_cell)
    from_right = right_cell - 0.5 * minmod(right_cell - left_cell, far_right - right_cell)
    flux = ADVECT * speed * jnp.where(speed > 0.0, from_left, from_right)
    return lax.slice_in_dim(flux, 1, cell_count + 1, axis=along_dim) - lax.slice_in_dim(
        flux, 0, cell_count, axis=along_dim
    )


def reactions(advected, sunlight, temper, stoich, wet_mask):
    nutrient = jnp.maximum(advected[0], 0.0)
    phyto = jnp.maximum(advected[1], 0.0)
    chloro = jnp.maximum(advected[2], 0.0)
    grazer = jnp.maximum(advected[3], 0.0)
    detritus = jnp.maximum(advected[4], 0.0)
    uptake = (
        GROWTH
        * sunlight
        / (sunlight + HALF_LIGHT)
        * nutrient
        / (nutrient + HALF_NUTRIENT)
        * jnp.exp(TEMP_COEF * temper)
    )
    growth = uptake * phyto
    grazing = GRAZE * grazer * phyto * phyto / (phyto * phyto + HALF_PREY)
    dying = MORTAL * phyto
    remineral = REMIN * detritus
    core = jnp.stack(
        [
            remineral - growth,
            growth - grazing - dying,
            CHL_RELAX * (CHL_RATIO * phyto - chloro) + CHL_GAIN * growth,
            ASSIM * grazing - GRAZER_LOSS * grazer,
            dying + (1.0 - ASSIM) * grazing + GRAZER_LOSS * grazer - remineral,
        ]
    )
    others = stoich.reshape((stoich.shape[0],) + (1,) * growth.ndim) * (growth - remineral)[None]
    change_all = jnp.concatenate([core, others], axis=0)
    return (advected + REACT_STEP * change_all) * wet_mask[None]


def edge_bands(values):
    return extended_2(values, (("ty", 1),), 1, False)


def edge_columns(values, rim_width):
    return extended_2(values, (("tx", 2),), rim_width, False)


def neighbour_rows(values, rim_width, group_id, group_count):
    extended = extended_2(values, (("comp", 1),), rim_width, True)
    lower_side = extended[:, :rim_width]
    upper_side = extended[:, -rim_width:]
    handed = jnp.where(group_id == 0, lower_side, upper_side)[:, None]
    beyond = edge_bands(handed)
    lower_side = jnp.where(group_id == 0, beyond[:, 0], lower_side)
    upper_side = jnp.where(group_id == group_count - 1, beyond[:, 2], upper_side)
    return (lower_side, upper_side)


def shards(ocean, tracers, bottom, stoich):
    group_count = lax.axis_size("comp")
    group_id = lax.axis_index("comp")
    num_tracers = tracers.shape[0]
    sub_rows = tracers.shape[2]
    flat_width = tracers.shape[3]
    levels = LEV
    columns = flat_width // levels
    band_rows = ocean.shape[1]
    level_ids = jnp.arange(levels)
    wet_band = (level_ids[None, None, :] < bottom[:, :, None]).astype(jnp.float32)
    row_start = group_id * sub_rows
    wet_sub = lax.dynamic_slice_in_dim(wet_band, row_start, sub_rows, 0)
    tracer_now = tracers.reshape(num_tracers, sub_rows, columns, levels)
    whole_band = ocean.reshape(3, band_rows, columns, levels)
    current = whole_band
    for step_index in range(STEPS):
        sunlight, heating = optics(tracer_now[2], wet_sub)
        temper = current[2]
        heat_band = lax.all_gather(
            heating.reshape(sub_rows, flat_width), "comp", axis=0, tiled=True
        )
        heat_band = heat_band.reshape(band_rows, columns, levels)
        edge_rows = jnp.stack([temper[:1], temper[-1:]]).reshape(2, 1, 1, flat_width)
        beyond = edge_bands(edge_rows)
        lower_rim = beyond[1, 0].reshape(1, columns, levels)
        upper_rim = beyond[0, 2].reshape(1, columns, levels)
        row_margin = jnp.concatenate([lower_rim, temper, upper_rim], axis=0)
        column_margin = edge_columns(temper.reshape(1, band_rows, flat_width), levels)
        column_margin = column_margin.reshape(band_rows, columns + 2, levels)
        current = ocean_update(current, row_margin, column_margin, heat_band, wet_band)
        moving = lax.dynamic_slice_in_dim(current, row_start, sub_rows, 1)
        packed = jnp.concatenate([tracer_now, moving[0:2], wet_sub[None]], axis=0)
        field_count = num_tracers + 3
        packed = packed.reshape(field_count, sub_rows, flat_width)
        lower_rim, upper_rim = neighbour_rows(packed, 2, group_id, group_count)
        row_wide = jnp.concatenate([lower_rim, packed, upper_rim], axis=1).reshape(
            field_count, sub_rows + 4, columns, levels
        )
        column_wide = edge_columns(packed, 2 * levels).reshape(
            field_count, sub_rows, columns + 4, levels
        )
        column_change = face_transport(
            column_wide[:num_tracers],
            column_wide[num_tracers : num_tracers + 1],
            column_wide[num_tracers + 2 : num_tracers + 3],
            2,
            columns,
        )
        row_change = face_transport(
            row_wide[:num_tracers],
            row_wide[num_tracers + 1 : num_tracers + 2],
            row_wide[num_tracers + 2 : num_tracers + 3],
            1,
            sub_rows,
        )
        advected = tracer_now - column_change - row_change
        tracer_now = reactions(advected, sunlight, moving[2], stoich, wet_sub)
    ocean_final = current.reshape(3, band_rows, flat_width)
    return (ocean_final, tracer_now.reshape(num_tracers, 1, sub_rows, flat_width))


def solution(mesh):
    in_specs = (P(None, "ty", "tx"), P(None, "ty", "comp", "tx"), P("ty", "tx"), P())
    out_specs = (P(None, "ty", "tx"), P(None, "ty", "comp", "tx"))
    return jax.shard_map(shards, mesh=mesh, in_specs=in_specs, out_specs=out_specs, check_vma=False)
```

profile of v0, /device:TPU:39, one launch (start us, length us, event | category | flops | bytes accessed | tf_op | source)
XLA Modules:
  0.0 191.2 jit_solution(17814295461421523981)
XLA Ops:
  1.4 3.5 %collective-permute-start.2 = (f32[2,1,1,256]{3,2,1,0:T(1,128)S(1)}, f32[2,1,1,256]{3,2,1,0:T(1,128)S(1)}, u32[]{:S(2)}, u32[]{:S(2)}) collective-permute-start(f32[2,1,1,256]{3,2,1,0:T(1,128)S(1)} %pad_maximum_fusion.28), channel_id=1, source_target_pairs={{0,32},{32,64},{64,96},{96,128},{128,160},{160,192},{192,224},{1,3... | collective-permute-start | bytes 6152 | tf_op jit(solution)/shard_map/ppermute | solution.py:43
  5.0 1.9 %collective-permute-start.3 = (f32[2,1,1,256]{3,2,1,0:T(1,128)S(1)}, f32[2,1,1,256]{3,2,1,0:T(1,128)S(1)}, u32[]{:S(2)}, u32[]{:S(2)}) collective-permute-start(f32[2,1,1,256]{3,2,1,0:T(1,128)S(1)} %pad_maximum_fusion.28), channel_id=1, source_target_pairs={{32,0},{64,32},{96,64},{128,96},{160,128},{192,160},{224,192},{33,... | collective-permute-start | bytes 6152 | tf_op jit(solution)/shard_map/ppermute | solution.py:45
  7.7 16.3 %collective-permute-start = (f32[1,32,64]{2,1,0:T(8,128)S(1)}, f32[1,32,64]{2,1,0:T(8,128)S(1)}, u32[]{:S(2)}, u32[]{:S(2)}) collective-permute-start(f32[1,32,64]{2,1,0:T(8,128)S(1)} %get-tuple-element.58), channel_id=1, source_target_pairs={{0,1},{1,2},{2,3},{3,4},{4,5},{5,6},{6,7},{7,8},{8,9},{9,10},{10,1... | collective-permute-start | bytes 24584 | tf_op jit(solution)/shard_map/ppermute | solution.py:43
  24.0 1.9 %collective-permute-start.1 = (f32[1,32,64]{2,1,0:T(8,128)S(1)}, f32[1,32,64]{2,1,0:T(8,128)S(1)}, u32[]{:S(2)}, u32[]{:S(2)}) collective-permute-start(f32[1,32,64]{2,1,0:T(8,128)S(1)} %get-tuple-element.59), channel_id=1, source_target_pairs={{1,0},{2,1},{3,2},{4,3},{5,4},{6,5},{7,6},{8,7},{9,8},{10,9},{11,1... | collective-permute-start | bytes 24584 | tf_op jit(solution)/shard_map/ppermute | solution.py:45
  28.4 9.5 %all_gather.6 = f32[32,256]{1,0:T(8,128)S(1)} all-gather(f32[8,256]{1,0:T(8,128)S(1)} %reshape.140), channel_id=1, replica_groups=mesh['comp'=4,'ty'=8,'tx'=32] {'comp'}, dimensions={0}, use_global_device_ids=true | all-gather | bytes 40960 | tf_op jit(solution)/shard_map/all_gather | solution.py:189
  40.6 3.6 %collective-permute-start.6 = (f32[2,1,1,256]{3,2,1,0:T(1,128)S(1)}, f32[2,1,1,256]{3,2,1,0:T(1,128)S(1)}, u32[]{:S(2)}, u32[]{:S(2)}) collective-permute-start(f32[2,1,1,256]{3,2,1,0:T(1,128)S(1)} %constant_dynamic-update-slice_fusion), channel_id=1, source_target_pairs={{0,32},{32,64},{64,96},{96,128},{128,160},{160,192},{192,224},{1,3... | collective-permute-start | bytes 6152 | tf_op jit(solution)/shard_map/ppermute | solution.py:43
  44.2 1.9 %collective-permute-start.7 = (f32[2,1,1,256]{3,2,1,0:T(1,128)S(1)}, f32[2,1,1,256]{3,2,1,0:T(1,128)S(1)}, u32[]{:S(2)}, u32[]{:S(2)}) collective-permute-start(f32[2,1,1,256]{3,2,1,0:T(1,128)S(1)} %constant_dynamic-update-slice_fusion), channel_id=1, source_target_pairs={{32,0},{64,32},{96,64},{128,96},{160,128},{192,160},{224,192},{33,... | collective-permute-start | bytes 6152 | tf_op jit(solution)/shard_map/ppermute | solution.py:45
  46.3 17.0 %collective-permute-start.4 = (f32[1,32,64]{2,1,0:T(8,128)S(1)}, f32[1,32,64]{2,1,0:T(8,128)S(1)}, u32[]{:S(2)}, u32[]{:S(2)}) collective-permute-start(f32[1,32,64]{2,1,0:T(8,128)S(1)} %get-tuple-element.68), channel_id=1, source_target_pairs={{0,1},{1,2},{2,3},{3,4},{4,5},{5,6},{6,7},{7,8},{8,9},{9,10},{10,1... | collective-permute-start | bytes 24584 | tf_op jit(solution)/shard_map/ppermute | solution.py:43
  63.2 1.9 %collective-permute-start.5 = (f32[1,32,64]{2,1,0:T(8,128)S(1)}, f32[1,32,64]{2,1,0:T(8,128)S(1)}, u32[]{:S(2)}, u32[]{:S(2)}) collective-permute-start(f32[1,32,64]{2,1,0:T(8,128)S(1)} %get-tuple-element.69), channel_id=1, source_target_pairs={{1,0},{2,1},{3,2},{4,3},{5,4},{6,5},{7,6},{8,7},{9,8},{10,9},{11,1... | collective-permute-start | bytes 24584 | tf_op jit(solution)/shard_map/ppermute | solution.py:45
  65.4 13.7 %collective-permute-done.5 = f32[1,32,64]{2,1,0:T(8,128)S(1)} collective-permute-done((f32[1,32,64]{2,1,0:T(8,128)S(1)}, f32[1,32,64]{2,1,0:T(8,128)S(1)}, u32[]{:S(2)}, u32[]{:S(2)}) %collective-permute-start.5) | collective-permute-done | bytes 8224 | tf_op jit(solution)/shard_map/ppermute | solution.py:45
  81.4 2.9 %collective-permute-start.10 = (f32[22,2,256]{2,1,0:T(2,128)S(1)}, f32[22,2,256]{2,1,0:T(2,128)S(1)}, u32[]{:S(2)}, u32[]{:S(2)}) collective-permute-start(f32[22,2,256]{2,1,0:T(2,128)S(1)} %get-tuple-element.51), channel_id=1, source_target_pairs={{0,256},{256,512},{512,768},{768,0},{1,257},{257,513},{513,769},{7... | collective-permute-start | bytes 135176 | tf_op jit(solution)/shard_map/ppermute | solution.py:43
  84.4 3.6 %collective-permute-start.11 = (f32[22,2,256]{2,1,0:T(2,128)S(1)}, f32[22,2,256]{2,1,0:T(2,128)S(1)}, u32[]{:S(2)}, u32[]{:S(2)}) collective-permute-start(f32[22,2,256]{2,1,0:T(2,128)S(1)} %get-tuple-element.52), channel_id=1, source_target_pairs={{256,0},{512,256},{768,512},{0,768},{257,1},{513,257},{769,513},{1... | collective-permute-start | bytes 135176 | tf_op jit(solution)/shard_map/ppermute | solution.py:45
  89.2 4.6 %collective-permute-start.12 = (f32[22,1,2,256]{3,2,0,1:T(2,128)S(1)}, f32[22,1,2,256]{3,2,0,1:T(2,128)S(1)}, u32[]{:S(2)}, u32[]{:S(2)}) collective-permute-start(f32[22,1,2,256]{3,2,0,1:T(2,128)S(1)} %select_bitcast_fusion.1), channel_id=1, source_target_pairs={{0,32},{32,64},{64,96},{96,128},{128,160},{160,192},{192,224},{1,3... | collective-permute-start | bytes 135176 | tf_op jit(solution)/shard_map/ppermute | solution.py:43
  93.8 3.6 %collective-permute-start.8 = (f32[22,8,128]{2,1,0:T(8,128)S(1)}, f32[22,8,128]{2,1,0:T(8,128)S(1)}, u32[]{:S(2)}, u32[]{:S(2)}) collective-permute-start(f32[22,8,128]{2,1,0:T(8,128)S(1)} %get-tuple-element.49), channel_id=1, source_target_pairs={{0,1},{1,2},{2,3},{3,4},{4,5},{5,6},{6,7},{7,8},{8,9},{9,10},{10,1... | collective-permute-start | bytes 270344 | tf_op jit(solution)/shard_map/ppermute | solution.py:43
  102.1 4.3 %collective-permute-done.13 = f32[22,1,2,256]{3,2,0,1:T(2,128)S(1)} collective-permute-done((f32[22,1,2,256]{3,2,0,1:T(2,128)S(1)}, f32[22,1,2,256]{3,2,0,1:T(2,128)S(1)}, u32[]{:S(2)}, u32[]{:S(2)}) %collective-permute-start.13) | collective-permute-done | bytes 45088 | tf_op jit(solution)/shard_map/ppermute | solution.py:45
  107.9 6.2 %collective-permute-done.9 = f32[22,8,128]{2,1,0:T(8,128)S(1)} collective-permute-done((f32[22,8,128]{2,1,0:T(8,128)S(1)}, f32[22,8,128]{2,1,0:T(8,128)S(1)}, u32[]{:S(2)}, u32[]{:S(2)}) %collective-permute-start.9) | collective-permute-done | bytes 90144 | tf_op jit(solution)/shard_map/ppermute | solution.py:45
  124.9 9.6 %all_gather.7 = f32[32,256]{1,0:T(8,128)S(1)} all-gather(f32[8,256]{1,0:T(8,128)S(1)} %reshape.143), channel_id=1, replica_groups=mesh['comp'=4,'ty'=8,'tx'=32] {'comp'}, dimensions={0}, use_global_device_ids=true | all-gather | bytes 40960 | tf_op jit(solution)/shard_map/all_gather | solution.py:189
  137.3 3.1 %collective-permute-start.16 = (f32[22,2,256]{2,1,0:T(2,128)S(1)}, f32[22,2,256]{2,1,0:T(2,128)S(1)}, u32[]{:S(2)}, u32[]{:S(2)}) collective-permute-start(f32[22,2,256]{2,1,0:T(2,128)S(1)} %get-tuple-element.47), channel_id=1, source_target_pairs={{0,256},{256,512},{512,768},{768,0},{1,257},{257,513},{513,769},{7... | collective-permute-start | bytes 135176 | tf_op jit(solution)/shard_map/ppermute | solution.py:43
  140.4 3.4 %collective-permute-start.17 = (f32[22,2,256]{2,1,0:T(2,128)S(1)}, f32[22,2,256]{2,1,0:T(2,128)S(1)}, u32[]{:S(2)}, u32[]{:S(2)}) collective-permute-start(f32[22,2,256]{2,1,0:T(2,128)S(1)} %get-tuple-element.48), channel_id=1, source_target_pairs={{256,0},{512,256},{768,512},{0,768},{257,1},{513,257},{769,513},{1... | collective-permute-start | bytes 135176 | tf_op jit(solution)/shard_map/ppermute | solution.py:45
  143.9 17.0 %collective-permute-start.14 = (f32[22,8,128]{2,1,0:T(8,128)S(1)}, f32[22,8,128]{2,1,0:T(8,128)S(1)}, u32[]{:S(2)}, u32[]{:S(2)}) collective-permute-start(f32[22,8,128]{2,1,0:T(8,128)S(1)} %get-tuple-element.45), channel_id=1, source_target_pairs={{0,1},{1,2},{2,3},{3,4},{4,5},{5,6},{6,7},{7,8},{8,9},{9,10},{10,1... | collective-permute-start | bytes 270344 | tf_op jit(solution)/shard_map/ppermute | solution.py:43
  163.1 2.6 %collective-permute-start.18 = (f32[22,1,2,256]{3,2,0,1:T(2,128)S(1)}, f32[22,1,2,256]{3,2,0,1:T(2,128)S(1)}, u32[]{:S(2)}, u32[]{:S(2)}) collective-permute-start(f32[22,1,2,256]{3,2,0,1:T(2,128)S(1)} %select_bitcast_fusion), channel_id=1, source_target_pairs={{0,32},{32,64},{64,96},{96,128},{128,160},{160,192},{192,224},{1,3... | collective-permute-start | bytes 135176 | tf_op jit(solution)/shard_map/ppermute | solution.py:43
  166.4 2.6 %collective-permute-start.19 = (f32[22,1,2,256]{3,2,0,1:T(2,128)S(1)}, f32[22,1,2,256]{3,2,0,1:T(2,128)S(1)}, u32[]{:S(2)}, u32[]{:S(2)}) collective-permute-start(f32[22,1,2,256]{3,2,0,1:T(2,128)S(1)} %select_bitcast_fusion), channel_id=1, source_target_pairs={{32,0},{64,32},{96,64},{128,96},{160,128},{192,160},{224,192},{33,... | collective-permute-start | bytes 135176 | tf_op jit(solution)/shard_map/ppermute | solution.py:45
  169.1 2.2 %collective-permute-done.19 = f32[22,1,2,256]{3,2,0,1:T(2,128)S(1)} collective-permute-done((f32[22,1,2,256]{3,2,0,1:T(2,128)S(1)}, f32[22,1,2,256]{3,2,0,1:T(2,128)S(1)}, u32[]{:S(2)}, u32[]{:S(2)}) %collective-permute-start.19) | collective-permute-done | bytes 45088 | tf_op jit(solution)/shard_map/ppermute | solution.py:45
  172.1 12.2 %collective-permute-done.15 = f32[22,8,128]{2,1,0:T(8,128)S(1)} collective-permute-done((f32[22,8,128]{2,1,0:T(8,128)S(1)}, f32[22,8,128]{2,1,0:T(8,128)S(1)}, u32[]{:S(2)}, u32[]{:S(2)}) %collective-permute-start.15) | collective-permute-done | bytes 90144 | tf_op jit(solution)/shard_map/ppermute | solution.py:45
  (226 shorter events, 40.2 us)
Async XLA Ops:
  0.6 26.9 %copy-start = (f32[19,1,8,256]{3,2,1,0:T(8,128)S(1)}, f32[19,1,8,256]{3,2,1,0:T(8,128)}, u32[]{:S(2)}) copy-start(f32[19,1,8,256]{3,2,1,0:T(8,128)} %param.5) | copy-start | bytes 466948
  1.4 37.3 %collective-permute-start.2 = (f32[2,1,1,256]{3,2,1,0:T(1,128)S(1)}, f32[2,1,1,256]{3,2,1,0:T(1,128)S(1)}, u32[]{:S(2)}, u32[]{:S(2)}) collective-permute-start(f32[2,1,1,256]{3,2,1,0:T(1,128)S(1)} %pad_maximum_fusion.28), channel_id=1, source_target_pairs={{0,32},{32,64},{64,96},{96,128},{128,160},{160,192},{192,224},{1,3... | collective-permute-start | bytes 6152 | tf_op jit(solution)/shard_map/ppermute | solution.py:43
  5.0 33.9 %collective-permute-start.3 = (f32[2,1,1,256]{3,2,1,0:T(1,128)S(1)}, f32[2,1,1,256]{3,2,1,0:T(1,128)S(1)}, u32[]{:S(2)}, u32[]{:S(2)}) collective-permute-start(f32[2,1,1,256]{3,2,1,0:T(1,128)S(1)} %pad_maximum_fusion.28), channel_id=1, source_target_pairs={{32,0},{64,32},{96,64},{128,96},{160,128},{192,160},{224,192},{33,... | collective-permute-start | bytes 6152 | tf_op jit(solution)/shard_map/ppermute | solution.py:45
  7.7 31.4 %collective-permute-start = (f32[1,32,64]{2,1,0:T(8,128)S(1)}, f32[1,32,64]{2,1,0:T(8,128)S(1)}, u32[]{:S(2)}, u32[]{:S(2)}) collective-permute-start(f32[1,32,64]{2,1,0:T(8,128)S(1)} %get-tuple-element.58), channel_id=1, source_target_pairs={{0,1},{1,2},{2,3},{3,4},{4,5},{5,6},{6,7},{7,8},{8,9},{9,10},{10,1... | collective-permute-start | bytes 24584 | tf_op jit(solution)/shard_map/ppermute | solution.py:43
  24.0 15.9 %collective-permute-start.1 = (f32[1,32,64]{2,1,0:T(8,128)S(1)}, f32[1,32,64]{2,1,0:T(8,128)S(1)}, u32[]{:S(2)}, u32[]{:S(2)}) collective-permute-start(f32[1,32,64]{2,1,0:T(8,128)S(1)} %get-tuple-element.59), channel_id=1, source_target_pairs={{1,0},{2,1},{3,2},{4,3},{5,4},{6,5},{7,6},{8,7},{9,8},{10,9},{11,1... | collective-permute-start | bytes 24584 | tf_op jit(solution)/shard_map/ppermute | solution.py:45
  38.7 76.8 %copy-start.8 = (f32[1,8,256]{2,1,0:T(8,128)}, f32[1,8,256]{2,1,0:T(8,128)S(1)}, u32[]{:S(2)}) copy-start(f32[1,8,256]{2,1,0:T(8,128)S(1)} %concatenate.71) | copy-start | bytes 24580
  40.6 24.6 %collective-permute-start.6 = (f32[2,1,1,256]{3,2,1,0:T(1,128)S(1)}, f32[2,1,1,256]{3,2,1,0:T(1,128)S(1)}, u32[]{:S(2)}, u32[]{:S(2)}) collective-permute-start(f32[2,1,1,256]{3,2,1,0:T(1,128)S(1)} %constant_dynamic-update-slice_fusion), channel_id=1, source_target_pairs={{0,32},{32,64},{64,96},{96,128},{128,160},{160,192},{192,224},{1,3... | collective-permute-start | bytes 6152 | tf_op jit(solution)/shard_map/ppermute | solution.py:43
  44.2 21.0 %collective-permute-start.7 = (f32[2,1,1,256]{3,2,1,0:T(1,128)S(1)}, f32[2,1,1,256]{3,2,1,0:T(1,128)S(1)}, u32[]{:S(2)}, u32[]{:S(2)}) collective-permute-start(f32[2,1,1,256]{3,2,1,0:T(1,128)S(1)} %constant_dynamic-update-slice_fusion), channel_id=1, source_target_pairs={{32,0},{64,32},{96,64},{128,96},{160,128},{192,160},{224,192},{33,... | collective-permute-start | bytes 6152 | tf_op jit(solution)/shard_map/ppermute | solution.py:45
  46.3 19.1 %collective-permute-start.4 = (f32[1,32,64]{2,1,0:T(8,128)S(1)}, f32[1,32,64]{2,1,0:T(8,128)S(1)}, u32[]{:S(2)}, u32[]{:S(2)}) collective-permute-start(f32[1,32,64]{2,1,0:T(8,128)S(1)} %get-tuple-element.68), channel_id=1, source_target_pairs={{0,1},{1,2},{2,3},{3,4},{4,5},{5,6},{6,7},{7,8},{8,9},{9,10},{10,1... | collective-permute-start | bytes 24584 | tf_op jit(solution)/shard_map/ppermute | solution.py:43
  63.2 15.9 %collective-permute-start.5 = (f32[1,32,64]{2,1,0:T(8,128)S(1)}, f32[1,32,64]{2,1,0:T(8,128)S(1)}, u32[]{:S(2)}, u32[]{:S(2)}) collective-permute-start(f32[1,32,64]{2,1,0:T(8,128)S(1)} %get-tuple-element.69), channel_id=1, source_target_pairs={{1,0},{2,1},{3,2},{4,3},{5,4},{6,5},{7,6},{8,7},{9,8},{10,9},{11,1... | collective-permute-start | bytes 24584 | tf_op jit(solution)/shard_map/ppermute | solution.py:45
  65.3 22.6 %copy-start.23 = (f32[1,4,64]{2,0,1:T(1,128)}, f32[1,4,64]{2,0,1:T(1,128)S(1)}, u32[]{:S(2)}) copy-start(f32[1,4,64]{2,0,1:T(1,128)S(1)} %reshape_squeeze.15) | copy-start | bytes 3076
  65.4 22.6 %copy-start.25 = (f32[1,4,64]{2,0,1:T(1,128)}, f32[1,4,64]{2,0,1:T(1,128)S(1)}, u32[]{:S(2)}) copy-start(f32[1,4,64]{2,0,1:T(1,128)S(1)} %reshape_squeeze.16) | copy-start | bytes 3076
  81.4 7.4 %collective-permute-start.10 = (f32[22,2,256]{2,1,0:T(2,128)S(1)}, f32[22,2,256]{2,1,0:T(2,128)S(1)}, u32[]{:S(2)}, u32[]{:S(2)}) collective-permute-start(f32[22,2,256]{2,1,0:T(2,128)S(1)} %get-tuple-element.51), channel_id=1, source_target_pairs={{0,256},{256,512},{512,768},{768,0},{1,257},{257,513},{513,769},{7... | collective-permute-start | bytes 135176 | tf_op jit(solution)/shard_map/ppermute | solution.py:43
  84.4 4.8 %collective-permute-start.11 = (f32[22,2,256]{2,1,0:T(2,128)S(1)}, f32[22,2,256]{2,1,0:T(2,128)S(1)}, u32[]{:S(2)}, u32[]{:S(2)}) collective-permute-start(f32[22,2,256]{2,1,0:T(2,128)S(1)} %get-tuple-element.52), channel_id=1, source_target_pairs={{256,0},{512,256},{768,512},{0,768},{257,1},{513,257},{769,513},{1... | collective-permute-start | bytes 135176 | tf_op jit(solution)/shard_map/ppermute | solution.py:45
  89.2 12.9 %collective-permute-start.12 = (f32[22,1,2,256]{3,2,0,1:T(2,128)S(1)}, f32[22,1,2,256]{3,2,0,1:T(2,128)S(1)}, u32[]{:S(2)}, u32[]{:S(2)}) collective-permute-start(f32[22,1,2,256]{3,2,0,1:T(2,128)S(1)} %select_bitcast_fusion.1), channel_id=1, source_target_pairs={{0,32},{32,64},{64,96},{96,128},{128,160},{160,192},{192,224},{1,3... | collective-permute-start | bytes 135176 | tf_op jit(solution)/shard_map/ppermute | solution.py:43
  93.8 14.1 %collective-permute-start.8 = (f32[22,8,128]{2,1,0:T(8,128)S(1)}, f32[22,8,128]{2,1,0:T(8,128)S(1)}, u32[]{:S(2)}, u32[]{:S(2)}) collective-permute-start(f32[22,8,128]{2,1,0:T(8,128)S(1)} %get-tuple-element.49), channel_id=1, source_target_pairs={{0,1},{1,2},{2,3},{3,4},{4,5},{5,6},{6,7},{7,8},{8,9},{9,10},{10,1... | collective-permute-start | bytes 270344 | tf_op jit(solution)/shard_map/ppermute | solution.py:43
  97.4 16.7 %collective-permute-start.9 = (f32[22,8,128]{2,1,0:T(8,128)S(1)}, f32[22,8,128]{2,1,0:T(8,128)S(1)}, u32[]{:S(2)}, u32[]{:S(2)}) collective-permute-start(f32[22,8,128]{2,1,0:T(8,128)S(1)} %get-tuple-element.50), channel_id=1, source_target_pairs={{1,0},{2,1},{3,2},{4,3},{5,4},{6,5},{7,6},{8,7},{9,8},{10,9},{11,1... | collective-permute-start | bytes 270344 | tf_op jit(solution)/shard_map/ppermute | solution.py:45
  100.1 6.3 %collective-permute-start.13 = (f32[22,1,2,256]{3,2,0,1:T(2,128)S(1)}, f32[22,1,2,256]{3,2,0,1:T(2,128)S(1)}, u32[]{:S(2)}, u32[]{:S(2)}) collective-permute-start(f32[22,1,2,256]{3,2,0,1:T(2,128)S(1)} %select_bitcast_fusion.1), channel_id=1, source_target_pairs={{32,0},{64,32},{96,64},{128,96},{160,128},{192,160},{224,192},{33,... | collective-permute-start | bytes 135176 | tf_op jit(solution)/shard_map/ppermute | solution.py:45
  137.3 25.8 %collective-permute-start.16 = (f32[22,2,256]{2,1,0:T(2,128)S(1)}, f32[22,2,256]{2,1,0:T(2,128)S(1)}, u32[]{:S(2)}, u32[]{:S(2)}) collective-permute-start(f32[22,2,256]{2,1,0:T(2,128)S(1)} %get-tuple-element.47), channel_id=1, source_target_pairs={{0,256},{256,512},{512,768},{768,0},{1,257},{257,513},{513,769},{7... | collective-permute-start | bytes 135176 | tf_op jit(solution)/shard_map/ppermute | solution.py:43
  140.4 22.6 %collective-permute-start.17 = (f32[22,2,256]{2,1,0:T(2,128)S(1)}, f32[22,2,256]{2,1,0:T(2,128)S(1)}, u32[]{:S(2)}, u32[]{:S(2)}) collective-permute-start(f32[22,2,256]{2,1,0:T(2,128)S(1)} %get-tuple-element.48), channel_id=1, source_target_pairs={{256,0},{512,256},{768,512},{0,768},{257,1},{513,257},{769,513},{1... | collective-permute-start | bytes 135176 | tf_op jit(solution)/shard_map/ppermute | solution.py:45
  143.9 28.2 %collective-permute-start.14 = (f32[22,8,128]{2,1,0:T(8,128)S(1)}, f32[22,8,128]{2,1,0:T(8,128)S(1)}, u32[]{:S(2)}, u32[]{:S(2)}) collective-permute-start(f32[22,8,128]{2,1,0:T(8,128)S(1)} %get-tuple-element.45), channel_id=1, source_target_pairs={{0,1},{1,2},{2,3},{3,4},{4,5},{5,6},{6,7},{7,8},{8,9},{9,10},{10,1... | collective-permute-start | bytes 270344 | tf_op jit(solution)/shard_map/ppermute | solution.py:43
  160.9 23.4 %collective-permute-start.15 = (f32[22,8,128]{2,1,0:T(8,128)S(1)}, f32[22,8,128]{2,1,0:T(8,128)S(1)}, u32[]{:S(2)}, u32[]{:S(2)}) collective-permute-start(f32[22,8,128]{2,1,0:T(8,128)S(1)} %get-tuple-element.46), channel_id=1, source_target_pairs={{1,0},{2,1},{3,2},{4,3},{5,4},{6,5},{7,6},{8,7},{9,8},{10,9},{11,1... | collective-permute-start | bytes 270344 | tf_op jit(solution)/shard_map/ppermute | solution.py:45
  163.1 5.9 %collective-permute-start.18 = (f32[22,1,2,256]{3,2,0,1:T(2,128)S(1)}, f32[22,1,2,256]{3,2,0,1:T(2,128)S(1)}, u32[]{:S(2)}, u32[]{:S(2)}) collective-permute-start(f32[22,1,2,256]{3,2,0,1:T(2,128)S(1)} %select_bitcast_fusion), channel_id=1, source_target_pairs={{0,32},{32,64},{64,96},{96,128},{128,160},{160,192},{192,224},{1,3... | collective-permute-start | bytes 135176 | tf_op jit(solution)/shard_map/ppermute | solution.py:43
  166.4 4.9 %collective-permute-start.19 = (f32[22,1,2,256]{3,2,0,1:T(2,128)S(1)}, f32[22,1,2,256]{3,2,0,1:T(2,128)S(1)}, u32[]{:S(2)}, u32[]{:S(2)}) collective-permute-start(f32[22,1,2,256]{3,2,0,1:T(2,128)S(1)} %select_bitcast_fusion), channel_id=1, source_target_pairs={{32,0},{64,32},{96,64},{128,96},{160,128},{192,160},{224,192},{33,... | collective-permute-start | bytes 135176 | tf_op jit(solution)/shard_map/ppermute | solution.py:45
  (26 other events, 67.4 us)
where the time goes:
time: 193 us; the launch traced here: 191 us
  starting transfers between devices  97.2 us (50%)
  waiting for transfers between devices  39.8 us (21%)
  local copies, waits for them, and re-layouts  21.7 us (11%)
  blocking collectives  19.2 us (10%)
  other arithmetic  8.76 us (5%)
  matrix products  2.87 us (1%)
    ppermute x10, starting transfers between devices, extended_2(): lax.ppermute(tail, axis, [(i, (i + 1) % count) for i in range(ends)])  74.2 us
    ppermute x10, waiting for transfers between devices, extended_2(): lax.ppermute(head, axis, [((i + 1) % count, i) for i in range(ends)])  39.8 us
    ppermute x10, starting transfers between devices, extended_2(): lax.ppermute(head, axis, [((i + 1) % count, i) for i in range(ends)])  23 us
    all_gather x2, blocking collectives, shards(): lax.all_gather(heating.reshape(sub_rows, flat_width), 'comp', axis=0, til...  19.2 us
    unnamed x63, local copies, waits for them, and re-layouts  9.65 us
  transfers between devices with their start and end apart: 20, of which 7 were waited for; matrix products, arithmetic and copies ran while one was open for 5% of the time, Pallas kernels for 0%

commit v1 on v0

v1 whole, which is shorter than its diff:
```python
import jax
import jax.numpy as jnp
from jax import lax
from jax.experimental import pallas as pl
from jax.experimental.pallas import tpu as pltpu
from jax.sharding import PartitionSpec as P

LEV = 64
NTR = 19
ROWS = 8
WIDE = 256
FIELDS = 22
U, V, T, WET = 19, 20, 21, 22
VMEM = pltpu.VMEM


def next_col(x):
    return pltpu.roll(x, x.shape[1] - LEV, 1)


def prev_col(x):
    return pltpu.roll(x, LEV, 1)


def next_row(x):
    return pltpu.roll(x, x.shape[0] - 1, 0)


def prev_row(x):
    return pltpu.roll(x, 1, 0)


def divergence(q, fac, nxt, prv):
    d = nxt(q) - q
    b = prv(d)
    m = jnp.where(d * b > 0.0, jnp.where(jnp.abs(d) < jnp.abs(b), d, b), 0.0)
    half = 0.5 * m
    flux = fac * jnp.where(fac > 0.0, q + half, nxt(q - half))
    return flux - prv(flux)


def face_factor(vel, wet, nxt):
    return 0.08 * (0.5 * (vel + nxt(vel)) * wet * nxt(wet))


def level_sum(x, ladder):
    rows, lanes = x.shape
    count = lanes // 128
    parts = [x[:, 128 * i : 128 * (i + 1)] for i in range(count)]
    out = jnp.dot(
        jnp.concatenate(parts, axis=0),
        ladder,
        precision=lax.Precision.HIGHEST,
        preferred_element_type=jnp.float32,
    )
    return jnp.concatenate([out[rows * i : rows * (i + 1)] for i in range(count)], axis=1)


def ladders():
    r = lax.broadcasted_iota(jnp.int32, (128, 128), 0)
    c = lax.broadcasted_iota(jnp.int32, (128, 128), 1)
    same = (r // LEV) == (c // LEV)
    incl = jnp.where(same & (r <= c), 1.0, 0.0).astype(jnp.float32)
    excl = jnp.where(same & (r < c), 1.0, 0.0).astype(jnp.float32)
    return incl, excl


def optics(chloro, wet, excl):
    absorb = (0.04 + 0.03 * jnp.maximum(chloro, 0.0)) * wet
    sun = jnp.exp(-level_sum(absorb, excl))
    heat = sun * (1.0 - jnp.exp(-absorb)) * wet
    return sun, heat


def reaction_terms(adv, sun, temp):
    n, p, c, z, d = [jnp.maximum(a, 0.0) for a in adv]
    uptake = sun / (sun + 0.2) * n / (n + 0.5) * jnp.exp(0.1 * temp)
    growth = uptake * p
    grazing = 0.8 * z * p * p / (p * p + 0.3)
    dying = 0.1 * p
    remin = 0.2 * d
    core = [
        remin - growth,
        growth - grazing - dying,
        0.3 * (0.5 * p - c) + 0.2 * growth,
        0.3 * grazing - 0.05 * z,
        dying + 0.7 * grazing + 0.05 * z - remin,
    ]
    return core, growth - remin


def odd(name):
    return lax.rem(lax.axis_index(name), 2) == 1


def pack_kernel(ocean_ref, tr_ref, bot_ref, out_ref):
    rows = pl.ds(pl.multiple_of(lax.axis_index("comp") * ROWS, ROWS), ROWS)
    for f in range(FIELDS):
        x = tr_ref[f, 0] if f < NTR else ocean_ref[f - NTR, rows, :]
        out_ref[2 * f] = x[:, :128]
        out_ref[2 * f + 1] = x[:, 128:]
    out_ref[2 * FIELDS] = jnp.zeros((ROWS, 128), jnp.float32)
    out_ref[2 * FIELDS, :, 0:4] = bot_ref[rows, :].astype(jnp.float32)


def wet_tiles(bottom):
    lane = lax.broadcasted_iota(jnp.int32, (ROWS, 128), 1)
    level = lax.rem(lane, LEV).astype(jnp.float32)
    tiles = []
    for h in range(2):
        b = jnp.where(lane < LEV, bottom[:, 2 * h : 2 * h + 1], bottom[:, 2 * h + 1 : 2 * h + 2])
        tiles.append(jnp.where(level < b, 1.0, 0.0))
    return tiles


def mid_kernel(own_ref, eo_ref, ee_ref, ext_ref, ne_ref, no_ref):
    flip = odd("tx")
    sub = lax.broadcasted_iota(jnp.int32, (ROWS, 128), 0)
    up = (sub < 4) == odd("comp")

    def west(t):
        return jnp.where(flip, ee_ref[t], eo_ref[t])

    def east(t):
        return jnp.where(flip, eo_ref[t], ee_ref[t])

    def put(f, blocks):
        for i, b in enumerate(blocks):
            ext_ref[f, :, 128 * i : 128 * (i + 1)] = b
        for k, (a, b) in enumerate(((blocks[2], blocks[3]), (blocks[1], blocks[4]))):
            swapped = pltpu.roll(b, 4, 0)
            ne_ref[2 * f + k] = jnp.where(up, a, swapped)
            no_ref[2 * f + k] = jnp.where(up, swapped, a)

    for f in range(FIELDS):
        a, b = 2 * f, 2 * f + 1
        put(f, [west(a), west(b), own_ref[a], own_ref[b], east(a), east(b)])
    t = 2 * FIELDS
    put(WET, wet_tiles(west(t)) + wet_tiles(own_ref[t]) + wet_tiles(east(t)))


def main_kernel(ext_ref, te_ref, to_ref, stoich_ref, ocean_ref, out_ref, h_ref, q_ref):
    incl, excl = ladders()
    sub = lax.broadcasted_iota(jnp.int32, (ROWS, 128), 0)
    first = (sub < 4) != odd("comp")

    def fill(f, _):
        for k, (ia, ib) in enumerate(((1, 2), (0, 3))):
            te, to = te_ref[2 * f + k], to_ref[2 * f + k]
            h_ref[f, :, 128 * ia : 128 * (ia + 1)] = jnp.where(first, te, to)
            h_ref[f, :, 128 * ib : 128 * (ib + 1)] = jnp.where(
                first, pltpu.roll(te, 4, 0), pltpu.roll(to, 4, 0)
            )
        return 0

    lax.fori_loop(0, FIELDS + 1, fill, 0)

    def both(o, h):
        return jnp.concatenate([o[:, 128:640], h], axis=0)

    u_o, v_o, t_o, w_o = [ext_ref[f] for f in (U, V, T, WET)]
    u_h, v_h, t_h, w_h = [h_ref[f] for f in (U, V, T, WET)]
    v_b, t_b, w_b = both(v_o, v_h), both(t_o, t_h), both(w_o, w_h)
    u_b = both(u_o, u_h)

    p_o = 0.05 * level_sum(t_o, incl)
    p_h = 0.05 * level_sum(t_h, incl)
    p_b = both(p_o, p_h)
    sun, heat = optics(both(ext_ref[2], h_ref[2]), w_b, excl)

    def east_speed(u, v, p, w):
        slope = 0.5 * (next_col(p) - prev_col(p))
        return w * (0.95 * u + 0.2 * (v - slope))

    def north_speed(u, v, p, w):
        slope = 0.5 * (next_row(p) - prev_row(p))
        return w * (0.95 * v - 0.2 * (u + slope))

    u1_o = east_speed(u_o, v_o, p_o, w_o)
    u1_h = east_speed(u_h, v_h, p_h, w_h)
    v1_b = north_speed(u_b, v_b, p_b, w_b)
    spread = (
        next_row(t_b)
        + prev_row(t_b)
        + both(next_col(t_o), next_col(t_h))
        + both(prev_col(t_o), prev_col(t_h))
        - 4.0 * t_b
    )
    t1_b = w_b * (t_b + 0.2 * (2.0 * heat + 0.2 * spread))

    fc_o = face_factor(u1_o, w_o, next_col)
    fc_h = face_factor(u1_h, w_h, next_col)
    fr_b = face_factor(v1_b, w_b, next_row)

    def advect1(f):
        q_o, q_h = ext_ref[f], h_ref[f]
        q_b = both(q_o, q_h)
        col = both(
            divergence(q_o, fc_o, next_col, prev_col), divergence(q_h, fc_h, next_col, prev_col)
        )
        return q_b - col - divergence(q_b, fr_b, next_row, prev_row)

    def keep1(f, _):
        q_ref[f] = advect1(f)
        return 0

    lax.fori_loop(0, 5, keep1, 0)
    core, gain = reaction_terms([q_ref[f] for f in range(5)], sun, t1_b)
    for f in range(5):
        q_ref[f] = (q_ref[f] + 0.2 * core[f]) * w_b

    def others1(f, _):
        q_ref[f] = (advect1(f) + 0.2 * (stoich_ref[f - 5] * gain)) * w_b
        return 0

    lax.fori_loop(5, NTR, others1, 0)

    own = slice(128, 384)
    w2 = w_b[:ROWS]
    w_own = w2[:, own]
    u1 = both(u1_o, u1_h)
    p1 = 0.05 * level_sum(t1_b, incl)
    sun2, heat2 = optics(q_ref[2, :ROWS, own], w_own, excl)
    u2 = east_speed(u1[:ROWS], v1_b[:ROWS], p1[:ROWS], w2)
    v2 = north_speed(u1[:, own], v1_b[:, own], p1[:, own], w_b[:, own])
    t1 = t1_b[:ROWS, own]
    spread2 = (
        next_row(t1_b)[:ROWS, own]
        + prev_row(t1_b)[:ROWS, own]
        + next_col(t1_b[:ROWS])[:, own]
        + prev_col(t1_b[:ROWS])[:, own]
        - 4.0 * t1
    )
    t2 = w_own * (t1 + 0.2 * (2.0 * heat2 + 0.2 * spread2))
    for peer in range(4):
        ocean_ref[peer, 0] = u2[:, own]
        ocean_ref[peer, 1] = v2[:ROWS]
        ocean_ref[peer, 2] = t2

    fc2 = face_factor(u2, w2, next_col)
    fr2 = face_factor(v2, w_b[:, own], next_row)

    def advect2(f):
        col = divergence(q_ref[f, :ROWS], fc2, next_col, prev_col)[:, own]
        row = divergence(q_ref[f, :, own], fr2, next_row, prev_row)[:ROWS]
        return q_ref[f, :ROWS, own] - col - row

    adv = [advect2(f) for f in range(5)]
    core2, gain2 = reaction_terms(adv, sun2, t2)
    for f in range(5):
        out_ref[f, 0] = (adv[f] + 0.2 * core2[f]) * w_own

    def others2(f, _):
        out_ref[f, 0] = (advect2(f) + 0.2 * (stoich_ref[f - 5] * gain2)) * w_own
        return 0

    lax.fori_loop(5, NTR, others2, 0)


def swaps(count, first, place=lambda i: i):
    pairs = []
    for a in range(first, count - 1, 2):
        pairs += [(place(a), place(a + 1)), (place(a + 1), place(a))]
    return pairs


def shards(ocean, tracers, bottom, stoich):
    comps = lax.axis_size("comp")
    bands = lax.axis_size("ty")
    tiles = lax.axis_size("tx")
    vmem = pl.BlockSpec(memory_space=VMEM)

    def arr(*dims):
        return jax.ShapeDtypeStruct(dims, jnp.float32)

    def place(row):
        return (row % comps) * bands + row // comps

    packed = pl.pallas_call(
        pack_kernel,
        out_shape=arr(2 * FIELDS + 1, ROWS, 128),
        in_specs=[vmem] * 3,
        out_specs=vmem,
    )(ocean, tracers, bottom)
    from_odd = lax.ppermute(packed, "tx", swaps(tiles, 1))
    from_even = lax.ppermute(packed, "tx", swaps(tiles, 0))
    ext, ne, no = pl.pallas_call(
        mid_kernel,
        out_shape=(
            arr(FIELDS + 1, ROWS, 768),
            arr(2 * FIELDS + 2, ROWS, 128),
            arr(2 * FIELDS + 2, ROWS, 128),
        ),
        in_specs=[vmem] * 3,
        out_specs=(vmem,) * 3,
    )(packed, from_odd, from_even)
    axes = ("comp", "ty")
    te = lax.ppermute(ne, axes, swaps(comps * bands, 0, place))
    to = lax.ppermute(no, axes, swaps(comps * bands, 1, place))
    rows, tracers_out = pl.pallas_call(
        main_kernel,
        out_shape=(arr(comps, 3, ROWS, WIDE), arr(NTR, 1, ROWS, WIDE)),
        in_specs=[vmem] * 3 + [pl.BlockSpec(memory_space=pltpu.SMEM)],
        out_specs=(vmem, vmem),
        scratch_shapes=[
            VMEM((FIELDS + 1, ROWS, 512), jnp.float32),
            VMEM((NTR, 2 * ROWS, 512), jnp.float32),
        ],
    )(ext, te, to, stoich)
    gathered = lax.all_to_all(rows, "comp", 0, 0, tiled=True)
    ocean_out = jnp.swapaxes(gathered, 0, 1).reshape(3, comps * ROWS, WIDE)
    return ocean_out, tracers_out


def solution(mesh):
    in_specs = (P(None, "ty", "tx"), P(None, "ty", "comp", "tx"), P("ty", "tx"), P())
    out_specs = (P(None, "ty", "tx"), P(None, "ty", "comp", "tx"))
    return jax.shard_map(shards, mesh=mesh, in_specs=in_specs, out_specs=out_specs, check_vma=False)
```

time: 193 us -> 77.6 us (0.40)
  the two profiles are of different devices: /device:TPU:39 before, /device:TPU:800 now
where the time goes in v1:
time: 77.6 us; the launch traced here: 77.3 us
  waiting for transfers between devices  28.1 us (36%)
  starting transfers between devices  18.9 us (24%)
  Pallas kernels  17 us (22%)
  blocking collectives  9.3 us (12%)
  local copies, waits for them, and re-layouts  3.37 us (4%)
    ppermute x1, waiting for transfers between devices, shards(): from_odd = lax.ppermute(packed, 'tx', swaps(tiles, 1))  21 us
    pallas_call x1, Pallas kernels, shards(): pl.pallas_call(main_kernel, out_shape=(arr(comps, 3, ROWS, WIDE), arr(NTR...  13.2 us
    ppermute x1, starting transfers between devices, shards(): from_odd = lax.ppermute(packed, 'tx', swaps(tiles, 1))  10.7 us
    all_to_all x1, blocking collectives, shards(): gathered = lax.all_to_all(rows, 'comp', 0, 0, tiled=True)  9.3 us
    ppermute x1, waiting for transfers between devices, shards(): to = lax.ppermute(no, axes, swaps(comps * bands, 1, place))  5.6 us
    ppermute x1, starting transfers between devices, shards(): te = lax.ppermute(ne, axes, swaps(comps * bands, 0, place))  3.47 us
    ppermute x1, starting transfers between devices, shards(): to = lax.ppermute(no, axes, swaps(comps * bands, 1, place))  2.74 us
    unnamed x9, local copies, waits for them, and re-layouts  2.72 us
  transfers between devices with their start and end apart: 4, of which 3 were waited for; matrix products, arithmetic and copies ran while one was open for 0% of the time, Pallas kernels for 0%

profile of v1, /device:TPU:800, one launch (start us, length us, event | category | flops | bytes accessed | tf_op | source)
XLA Modules:
  0.0 77.3 jit_solution(1624077216076918533)
XLA Ops:
  0.6 1.4 %copy.7.bot_ref = s32[32,4]{1,0:T(8,128)} copy(s32[32,4]{0,1:T(4,128)} %param.6) | data formatting | bytes 1024 | tf_op args[2]
  2.0 1.6 %shard_map.59.own_ref = f32[45,8,128]{2,1,0:T(8,128)} custom-call(f32[3,32,256]{2,1,0:T(8,128)} %ocean_ref.1, f32[19,1,8,256]{3,2,1,0:T(8,128)} %tr_ref.1, s32[32,4]{1,0:T(8,128)} %copy.7.bot_ref), custom_call_target="tpu_custom_call" | custom-call | tf_op jit(solution)/shard_map/pallas_call | solution.py:279
  3.6 1.9 %collective-permute-start.1 = (f32[45,8,128]{2,1,0:T(8,128)}, f32[45,8,128]{2,1,0:T(8,128)S(1)}, u32[]{:S(2)}, u32[]{:S(2)}) collective-permute-start(f32[45,8,128]{2,1,0:T(8,128)} %shard_map.59.own_ref), channel_id=1, source_target_pairs={{0,1},{1,0},{2,3},{3,2},{4,5},{5,4},{6,7},{7,6},{8,9},{9,8},{10,11... | collective-permute-start | bytes 552968 | tf_op jit(solution)/shard_map/ppermute | solution.py:286
  5.6 10.7 %collective-permute-start = (f32[45,8,128]{2,1,0:T(8,128)}, f32[45,8,128]{2,1,0:T(8,128)S(1)}, u32[]{:S(2)}, u32[]{:S(2)}) collective-permute-start(f32[45,8,128]{2,1,0:T(8,128)} %shard_map.59.own_ref), channel_id=1, source_target_pairs={{1,2},{2,1},{3,4},{4,3},{5,6},{6,5},{7,8},{8,7},{9,10},{10,9},{11,... | collective-permute-start | bytes 552968 | tf_op jit(solution)/shard_map/ppermute | solution.py:285
  16.3 0.0 collective-permute-done.1.ee_ref
  16.3 0.0 copy-start.2
  16.3 21.0 %collective-permute-done.eo_ref = f32[45,8,128]{2,1,0:T(8,128)S(1)} collective-permute-done((f32[45,8,128]{2,1,0:T(8,128)}, f32[45,8,128]{2,1,0:T(8,128)S(1)}, u32[]{:S(2)}, u32[]{:S(2)}) %collective-permute-start) | collective-permute-done | bytes 184352 | tf_op jit(solution)/shard_map/ppermute | solution.py:285
  37.4 0.0 copy-done.2
  37.4 0.0 copy-start.3
  37.4 0.7 copy-done.3
  38.0 2.1 %shard_map.60 = (f32[23,8,768]{2,1,0:T(8,128)}, f32[46,8,128]{2,1,0:T(8,128)}, f32[46,8,128]{2,1,0:T(8,128)}) custom-call(f32[45,8,128]{2,1,0:T(8,128)} %shard_map.59.own_ref, f32[45,8,128]{2,1,0:T(8,128)} %copy-done.3, f32[45,8,128]{2,1,0:T(8,128)} %copy-done.2), custom_call_target="tpu_custom_call" | custom-call | tf_op jit(solution)/shard_map/pallas_call | solution.py:287
  40.2 3.5 %collective-permute-start.2 = (f32[46,8,128]{2,1,0:T(8,128)}, f32[46,8,128]{2,1,0:T(8,128)S(1)}, u32[]{:S(2)}, u32[]{:S(2)}) collective-permute-start(f32[46,8,128]{2,1,0:T(8,128)} %get-tuple-element.8), channel_id=1, source_target_pairs={{0,256},{256,0},{512,768},{768,512},{32,288},{288,32},{544,800},{8... | collective-permute-start | bytes 565256 | tf_op jit(solution)/shard_map/ppermute | solution.py:298
  43.7 2.7 %collective-permute-start.3 = (f32[46,8,128]{2,1,0:T(8,128)}, f32[46,8,128]{2,1,0:T(8,128)S(1)}, u32[]{:S(2)}, u32[]{:S(2)}) collective-permute-start(f32[46,8,128]{2,1,0:T(8,128)} %get-tuple-element.9), channel_id=1, source_target_pairs={{256,512},{512,256},{768,32},{32,768},{288,544},{544,288},{800,64}... | collective-permute-start | bytes 565256 | tf_op jit(solution)/shard_map/ppermute | solution.py:299
  46.4 1.4 %collective-permute-done.2.te_ref = f32[46,8,128]{2,1,0:T(8,128)S(1)} collective-permute-done((f32[46,8,128]{2,1,0:T(8,128)}, f32[46,8,128]{2,1,0:T(8,128)S(1)}, u32[]{:S(2)}, u32[]{:S(2)}) %collective-permute-start.2) | collective-permute-done | bytes 188448 | tf_op jit(solution)/shard_map/ppermute | solution.py:298
  47.9 0.0 copy-start
  47.9 5.6 %collective-permute-done.3.to_ref = f32[46,8,128]{2,1,0:T(8,128)S(1)} collective-permute-done((f32[46,8,128]{2,1,0:T(8,128)}, f32[46,8,128]{2,1,0:T(8,128)S(1)}, u32[]{:S(2)}, u32[]{:S(2)}) %collective-permute-start.3) | collective-permute-done | bytes 188448 | tf_op jit(solution)/shard_map/ppermute | solution.py:299
  53.5 0.0 copy-start.1
  53.5 0.0 copy-done
  53.5 0.7 copy-done.1
  54.1 13.2 %shard_map.61 = (f32[4,3,8,256]{3,2,1,0:T(8,128)}, f32[19,1,8,256]{3,2,1,0:T(8,128)}) custom-call(f32[23,8,768]{2,1,0:T(8,128)} %get-tuple-element.7.ext_ref, f32[46,8,128]{2,1,0:T(8,128)} %copy-done, f32[46,8,128]{2,1,0:T(8,128)} %copy-done.1, f32[14]{0:T(128)} %stoich_ref.1), custom_call_target="tpu_custom_call" | custom-call | tf_op jit(solution)/shard_map/pallas_call | solution.py:300
  67.3 9.3 %all_to_all.5 = f32[4,3,8,256]{3,2,1,0:T(8,128)S(1)} all-to-all(f32[4,3,8,256]{3,2,1,0:T(8,128)} %get-tuple-element.10), channel_id=1, replica_groups=mesh['comp'=4,'ty'=8,'tx'=32] {'comp'}, dimensions={0} | all-to-all | bytes 196608 | tf_op jit(solution)/shard_map/all_to_all | solution.py:310
  76.6 0.6 copy_bitcast_fusion
Async XLA Ops:
  3.6 12.7 %collective-permute-start.1 = (f32[45,8,128]{2,1,0:T(8,128)}, f32[45,8,128]{2,1,0:T(8,128)S(1)}, u32[]{:S(2)}, u32[]{:S(2)}) collective-permute-start(f32[45,8,128]{2,1,0:T(8,128)} %shard_map.59.own_ref), channel_id=1, source_target_pairs={{0,1},{1,0},{2,3},{3,2},{4,5},{5,4},{6,7},{7,6},{8,9},{9,8},{10,11... | collective-permute-start | bytes 552968 | tf_op jit(solution)/shard_map/ppermute | solution.py:286
  5.6 31.8 %collective-permute-start = (f32[45,8,128]{2,1,0:T(8,128)}, f32[45,8,128]{2,1,0:T(8,128)S(1)}, u32[]{:S(2)}, u32[]{:S(2)}) collective-permute-start(f32[45,8,128]{2,1,0:T(8,128)} %shard_map.59.own_ref), channel_id=1, source_target_pairs={{1,2},{2,1},{3,4},{4,3},{5,6},{6,5},{7,8},{8,7},{9,10},{10,9},{11,... | collective-permute-start | bytes 552968 | tf_op jit(solution)/shard_map/ppermute | solution.py:285
  16.3 21.0 %copy-start.2 = (f32[45,8,128]{2,1,0:T(8,128)}, f32[45,8,128]{2,1,0:T(8,128)S(1)}, u32[]{:S(2)}) copy-start(f32[45,8,128]{2,1,0:T(8,128)S(1)} %collective-permute-done.1.ee_ref) | copy-start | bytes 552964
  37.4 0.7 copy-start.3
  40.2 7.7 %collective-permute-start.2 = (f32[46,8,128]{2,1,0:T(8,128)}, f32[46,8,128]{2,1,0:T(8,128)S(1)}, u32[]{:S(2)}, u32[]{:S(2)}) collective-permute-start(f32[46,8,128]{2,1,0:T(8,128)} %get-tuple-element.8), channel_id=1, source_target_pairs={{0,256},{256,0},{512,768},{768,512},{32,288},{288,32},{544,800},{8... | collective-permute-start | bytes 565256 | tf_op jit(solution)/shard_map/ppermute | solution.py:298
  43.7 9.8 %collective-permute-start.3 = (f32[46,8,128]{2,1,0:T(8,128)}, f32[46,8,128]{2,1,0:T(8,128)S(1)}, u32[]{:S(2)}, u32[]{:S(2)}) collective-permute-start(f32[46,8,128]{2,1,0:T(8,128)} %get-tuple-element.9), channel_id=1, source_target_pairs={{256,512},{512,256},{768,32},{32,768},{288,544},{544,288},{800,64}... | collective-permute-start | bytes 565256 | tf_op jit(solution)/shard_map/ppermute | solution.py:299
  47.9 5.6 %copy-start = (f32[46,8,128]{2,1,0:T(8,128)}, f32[46,8,128]{2,1,0:T(8,128)S(1)}, u32[]{:S(2)}) copy-start(f32[46,8,128]{2,1,0:T(8,128)S(1)} %collective-permute-done.2.te_ref) | copy-start | bytes 565252
  53.5 0.7 copy-start.1

commit v2 on v1

v2 whole, which is shorter than its diff:
```python
import jax
import jax.numpy as jnp
from jax import lax
from jax.experimental import pallas as pl
from jax.experimental.pallas import tpu as pltpu
from jax.sharding import PartitionSpec as P


LEV = 64
NTR = 19
ROWS = 8
FIELDS = 22
U, V, T, WET = 19, 20, 21, 22
VMEM = pltpu.VMEM
TILE = (ROWS, 128)


def lanes():
    return lax.broadcasted_iota(jnp.int32, TILE, 1)


def subs():
    return lax.broadcasted_iota(jnp.int32, TILE, 0)


def half_turn(x):
    return pltpu.roll(x, LEV, 1)


def mix(a, b):
    return jnp.where(lanes() < LEV, a, b)


def narrow(x):
    return [mix(x[i + 2], x[i]) for i in range(len(x) - 2)]


def each(f, *lists):
    return [f(*args) for args in zip(*lists)]


def next_col(x):
    return x[1:] + [half_turn(x[0])]


def prev_col(x):
    return [half_turn(x[-1])] + x[:-1]


def next_row(o, h):
    edge = subs() == 0
    return (
        [pltpu.roll(jnp.where(edge, b, a), ROWS - 1, 0) for a, b in zip(o, h)],
        [pltpu.roll(jnp.where(edge, a, b), ROWS - 1, 0) for a, b in zip(o, h)],
    )


def prev_row(o, h):
    edge = subs() == ROWS - 1
    return (
        [pltpu.roll(jnp.where(edge, b, a), 1, 0) for a, b in zip(o, h)],
        [pltpu.roll(jnp.where(edge, a, b), 1, 0) for a, b in zip(o, h)],
    )


def minmod(a, b):
    return jnp.maximum(jnp.minimum(a, b), 0.0) + jnp.minimum(jnp.maximum(a, b), 0.0)


def upwind(fac, left, right):
    return fac * jnp.where(fac > 0.0, left, right)


def minus(x, y):
    return each(lambda a, b: a - b, x, y)


def col_divergence(q, fac):
    d = minus(next_col(q), q)
    m = each(minmod, d, prev_col(d))
    left = each(lambda a, b: (a + a) + b, q, m)
    right = each(lambda a, b: (a + a) - b, q, m)
    flux = each(upwind, fac, left, next_col(right))
    return minus(flux, prev_col(flux))


def row_divergence(o, h, fac_o, fac_h):
    n_o, n_h = next_row(o, h)
    d_o, d_h = minus(n_o, o), minus(n_h, h)
    b_o, b_h = prev_row(d_o, d_h)
    m_o, m_h = each(minmod, d_o, b_o), each(minmod, d_h, b_h)
    r_o = each(lambda a, b: (a + a) - b, o, m_o)
    r_h = each(lambda a, b: (a + a) - b, h, m_h)
    n_o, n_h = next_row(r_o, r_h)
    f_o = each(lambda f, a, b, c: upwind(f, (a + a) + b, c), fac_o, o, m_o, n_o)
    f_h = each(lambda f, a, b, c: upwind(f, (a + a) + b, c), fac_h, h, m_h, n_h)
    p_o, p_h = prev_row(f_o, f_h)
    return minus(f_o, p_o), minus(f_h, p_h)


def half_factor(vel, wet, next_vel, next_wet):
    return 0.5 * (0.08 * (0.5 * (vel + next_vel) * wet * next_wet))


def col_factor(vel, wet):
    return each(half_factor, vel, wet, next_col(vel), next_col(wet))


def row_factor(vel_o, vel_h, wet_o, wet_h):
    n_o, n_h = next_row(vel_o, vel_h)
    w_o, w_h = next_row(wet_o, wet_h)
    return each(half_factor, vel_o, wet_o, n_o, w_o), each(half_factor, vel_h, wet_h, n_h, w_h)


def level_sum(tiles, inclusive):
    r = lax.rem(lax.broadcasted_iota(jnp.int32, (256, 128), 0), 128)
    c = lax.broadcasted_iota(jnp.int32, (256, 128), 1)
    above = (r <= c) if inclusive else (r < c)
    ladder = jnp.where(((r < LEV) == (c < LEV)) & above, 1.0, 0.0).astype(jnp.bfloat16)
    x = jnp.concatenate(tiles, axis=0)
    major = x.astype(jnp.bfloat16)
    minor = (x - major.astype(jnp.float32)).astype(jnp.bfloat16)
    out = jnp.dot(
        jnp.concatenate([major, minor], axis=1), ladder, preferred_element_type=jnp.float32
    )
    return [out[ROWS * i : ROWS * (i + 1)] for i in range(len(tiles))]


def optics(chloro, wet):
    absorb = each(lambda a, w: (0.04 + 0.03 * jnp.maximum(a, 0.0)) * w, chloro, wet)
    sun = [jnp.exp(-s) for s in level_sum(absorb, False)]
    heat = each(lambda s, a, w: s * (1.0 - jnp.exp(-a)) * w, sun, absorb, wet)
    return sun, heat


def east_speed(u, v, p, w):
    return each(
        lambda u, v, e, b, w: w * (0.95 * u + 0.2 * (v - 0.5 * (e - b))),
        u, v, next_col(p), prev_col(p), w,
    )


def north_speed(u, v, n, b, w):
    return each(
        lambda u, v, n, b, w: w * (0.95 * v - 0.2 * (u + 0.5 * (n - b))), u, v, n, b, w
    )


def warmed(t, heat, n, s, e, b, w):
    return each(
        lambda t, heat, n, s, e, b, w: w
        * (t + 0.2 * (2.0 * heat + 0.2 * (n + s + e + b - 4.0 * t))),
        t, heat, n, s, e, b, w,
    )


def reaction(adv, sun, temp):
    n, p, c, z, d = [jnp.maximum(a, 0.0) for a in adv]
    uptake = sun / (sun + 0.2) * n / (n + 0.5) * jnp.exp(0.1 * temp)
    growth = uptake * p
    grazing = 0.8 * z * p * p / (p * p + 0.3)
    dying = 0.1 * p
    remin = 0.2 * d
    core = [
        remin - growth,
        growth - grazing - dying,
        0.3 * (0.5 * p - c) + 0.2 * growth,
        0.3 * grazing - 0.05 * z,
        dying + 0.7 * grazing + 0.05 * z - remin,
    ]
    return core, 0.2 * (growth - remin)


def odd(name):
    return lax.rem(lax.axis_index(name), 2) == 1


def pack_kernel(ocean_ref, tr_ref, bot_ref, out_ref):
    start = pl.multiple_of(lax.axis_index("comp") * ROWS, ROWS)
    rows = pl.ds(start, ROWS)
    for f in range(FIELDS):
        x = tr_ref[f, 0] if f < NTR else ocean_ref[f - NTR, rows, :]
        out_ref[2 * f] = x[:, :128]
        out_ref[2 * f + 1] = x[:, 128:]
    band = bot_ref.shape[1]
    row = lax.broadcasted_iota(jnp.int32, (ROWS, band), 0) + start
    pick = row == lax.broadcasted_iota(jnp.int32, (ROWS, band), 1)
    depth = jnp.zeros(TILE, jnp.float32)
    for c in range(4):
        line = bot_ref[c : c + 1, :].astype(jnp.float32)
        depth = jnp.where(
            lanes() == c, jnp.sum(jnp.where(pick, line, 0.0), axis=1, keepdims=True), depth
        )
    out_ref[2 * FIELDS] = depth


def wet_tiles(depth):
    level = lax.rem(lanes(), LEV).astype(jnp.float32)
    return [
        jnp.where(level < mix(depth[:, c : c + 1], depth[:, c + 1 : c + 2]), 1.0, 0.0)
        for c in (0, 2)
    ]


def mid_kernel(own_ref, eo_ref, ee_ref, ext_ref, ne_ref, no_ref):
    flip = odd("tx")
    keep = (subs() < 4) == odd("comp")

    def put(f, west, own, east):
        wide = []
        for low, high in ((west[0], own[1]), (west[1], east[0]), (own[0], east[1])):
            wide += [mix(low, half_turn(high)), mix(half_turn(low), high)]
        for i in range(6):
            ext_ref[f, i] = wide[i]
        m = narrow(wide)
        for k in range(2):
            turned = pltpu.roll(m[2 * k + 1], 4, 0)
            ne_ref[f, k] = jnp.where(keep, m[2 * k], turned)
            no_ref[f, k] = jnp.where(keep, turned, m[2 * k])

    def sides(t):
        a, b = eo_ref[t], ee_ref[t]
        return jnp.where(flip, b, a), own_ref[t], jnp.where(flip, a, b)

    def one(f, _):
        put(f, *zip(sides(2 * f), sides(2 * f + 1)))
        return 0

    lax.fori_loop(0, FIELDS, one, 0, unroll=2)
    put(WET, *[wet_tiles(x) for x in sides(2 * FIELDS)])


def main_kernel(
    ext_ref, te_ref, to_ref, stoich_ref, ocean_ref, out_ref, q_ref, co_ref, ch_ref, ro_ref,
    rh_ref, g_ref, w_ref, c2_ref, r2_ref, g2_ref,
):
    first = (subs() < 4) != odd("comp")

    def wide(f):
        return [ext_ref[f, i] for i in range(6)]

    def halo(f):
        out = []
        for k in range(2):
            te, to = te_ref[f, k], to_ref[f, k]
            out.append(jnp.where(first, te, to))
            out.append(pltpu.roll(jnp.where(first, to, te), 4, 0))
        return out

    def save(ref, tiles):
        for i, x in enumerate(tiles):
            ref[i] = x

    def load(ref):
        return [ref[i] for i in range(ref.shape[0])]

    u_w, v_w, t_w, w_w = [wide(f) for f in (U, V, T, WET)]
    u_h, v_h, t_h, w_h = [halo(f) for f in (U, V, T, WET)]
    u_m, v_m, t_m, w_m = [narrow(x) for x in (u_w, v_w, t_w, w_w)]
    w_six = w_m + narrow(w_h)
    save(w_ref, w_six)

    press = [0.05 * s for s in level_sum(t_w + t_h, True)]
    p_w, p_h = press[:6], press[6:]
    sun, heat = optics(narrow(wide(2)) + narrow(halo(2)), w_six)

    u1_w = east_speed(u_w, v_w, p_w, w_w)
    u1_h = east_speed(u_h, v_h, p_h, w_h)
    u1_m = narrow(u1_w)
    p_m = narrow(p_w)
    (n_m, n_h), (b_m, b_h) = next_row(p_m, p_h), prev_row(p_m, p_h)
    v1_m = north_speed(u_m, v_m, n_m, b_m, w_m)
    v1_h = north_speed(u_h, v_h, n_h, b_h, w_h)
    (n_m, n_h), (b_m, b_h) = next_row(t_m, t_h), prev_row(t_m, t_h)
    t1 = warmed(
        t_m + narrow(t_h),
        heat,
        n_m + narrow(n_h),
        b_m + narrow(b_h),
        narrow(next_col(t_w)) + narrow(next_col(t_h)),
        narrow(prev_col(t_w)) + narrow(prev_col(t_h)),
        w_six,
    )

    save(co_ref, col_factor(u1_w, w_w))
    save(ch_ref, col_factor(u1_h, w_h))
    fr_o, fr_h = row_factor(v1_m, v1_h, w_m, w_h)
    save(ro_ref, fr_o)
    save(rh_ref, fr_h)

    def advect1(f):
        q_w, q_h = wide(f), halo(f)
        q_m = narrow(q_w)
        r_m, r_h = row_divergence(q_m, q_h, load(ro_ref), load(rh_ref))
        a_m = minus(minus(q_m, narrow(col_divergence(q_w, load(co_ref)))), r_m)
        a_h = minus(minus(q_h, col_divergence(q_h, load(ch_ref))), r_h)
        return a_m + narrow(a_h)

    core_fields = [advect1(f) for f in range(5)]
    gain = []
    for i in range(6):
        core, g = reaction([core_fields[f][i] for f in range(5)], sun[i], t1[i])
        gain.append(g)
        for f in range(5):
            q_ref[f, i] = (core_fields[f][i] + 0.2 * core[f]) * w_six[i]
    save(g_ref, gain)

    def others1(f, _):
        s = stoich_ref[f - 5]
        out = each(lambda a, g, w: (a + s * g) * w, advect1(f), load(g_ref), load(w_ref))
        for i in range(6):
            q_ref[f, i] = out[i]
        return 0

    lax.fori_loop(5, NTR, others1, 0, unroll=2)

    t1_m, t1_o, t1_h = t1[:4], narrow(t1[:4]), t1[4:]
    w_o, w_oh = narrow(w_m), w_six[4:]
    p1 = [0.05 * s for s in level_sum(t1, True)]
    u2_m = east_speed(u1_m, v1_m, p1[:4], w_m)
    (n_o, n_h), (b_o, b_h) = next_row(narrow(p1[:4]), p1[4:]), prev_row(narrow(p1[:4]), p1[4:])
    v2_o = north_speed(narrow(u1_m), narrow(v1_m), n_o, b_o, w_o)
    v2_h = north_speed(narrow(u1_h), narrow(v1_h), n_h, b_h, w_oh)
    sun2, heat2 = optics(narrow([q_ref[2, i] for i in range(4)]), w_o)
    t2 = warmed(
        t1_o,
        heat2,
        next_row(t1_o, t1_h)[0],
        prev_row(t1_o, t1_h)[0],
        narrow(next_col(t1_m)),
        narrow(prev_col(t1_m)),
        w_o,
    )

    def plain(x):
        return [mix(x[0], half_turn(x[1])), mix(half_turn(x[0]), x[1])]

    for k, x in enumerate((narrow(u2_m), v2_o, t2)):
        for i, tile in enumerate(plain(x)):
            for peer in range(ocean_ref.shape[0]):
                ocean_ref[peer, k, :, 128 * i : 128 * (i + 1)] = tile

    save(c2_ref, col_factor(u2_m, w_m))
    fr_o, fr_h = row_factor(v2_o, v2_h, w_o, w_oh)
    save(r2_ref, fr_o + fr_h)

    def advect2(f):
        q_m = [q_ref[f, i] for i in range(4)]
        q_h = [q_ref[f, 4 + i] for i in range(2)]
        q_o = narrow(q_m)
        fr = load(r2_ref)
        row = row_divergence(q_o, q_h, fr[:2], fr[2:])[0]
        return minus(minus(q_o, narrow(col_divergence(q_m, load(c2_ref)))), row)

    def finish(f, tiles):
        for i, x in enumerate(plain(tiles)):
            out_ref[f, 0, :, 128 * i : 128 * (i + 1)] = x

    core_fields = [advect2(f) for f in range(5)]
    done = [[] for _ in range(5)]
    gain = []
    for i in range(2):
        core, g = reaction([core_fields[f][i] for f in range(5)], sun2[i], t2[i])
        gain.append(g)
        for f in range(5):
            done[f].append((core_fields[f][i] + 0.2 * core[f]) * w_o[i])
    for f in range(5):
        finish(f, done[f])
    save(g2_ref, gain + w_o)

    def others2(f, _):
        s = stoich_ref[f - 5]
        k = load(g2_ref)
        finish(f, each(lambda a, g, w: (a + s * g) * w, advect2(f), k[:2], k[2:]))
        return 0

    lax.fori_loop(5, NTR, others2, 0, unroll=2)


def swaps(count, first, place=lambda i: i):
    pairs = []
    for a in range(first, count - 1, 2):
        pairs += [(place(a), place(a + 1)), (place(a + 1), place(a))]
    return pairs


def shards(ocean, tracers, bottom, stoich):
    comps = lax.axis_size("comp")
    bands = lax.axis_size("ty")
    tiles = lax.axis_size("tx")
    vmem = pl.BlockSpec(memory_space=VMEM)

    def arr(*dims):
        return VMEM(dims, jnp.float32)

    def near(*args):
        return [pltpu.with_memory_space_constraint(a, VMEM) for a in args]

    def place(row):
        return (row % comps) * bands + row // comps

    packed = pl.pallas_call(
        pack_kernel,
        out_shape=arr(2 * FIELDS + 1, *TILE),
        in_specs=[vmem] * 3,
        out_specs=vmem,
    )(ocean, tracers, bottom.T)
    from_odd = lax.ppermute(packed, "tx", swaps(tiles, 1))
    from_even = lax.ppermute(packed, "tx", swaps(tiles, 0))
    ext, ne, no = pl.pallas_call(
        mid_kernel,
        out_shape=(
            arr(FIELDS + 1, 6, *TILE),
            arr(FIELDS + 1, 2, *TILE),
            arr(FIELDS + 1, 2, *TILE),
        ),
        in_specs=[vmem] * 3,
        out_specs=(vmem,) * 3,
    )(*near(packed, from_odd, from_even))
    axes = ("comp", "ty")
    te = lax.ppermute(ne, axes, swaps(comps * bands, 0, place))
    to = lax.ppermute(no, axes, swaps(comps * bands, 1, place))
    rows, tracers_out = pl.pallas_call(
        main_kernel,
        out_shape=(arr(comps, 3, ROWS, 256), jax.ShapeDtypeStruct((NTR, 1, ROWS, 256), jnp.float32)),
        in_specs=[vmem] * 3 + [pl.BlockSpec(memory_space=pltpu.SMEM)],
        out_specs=(vmem, vmem),
        scratch_shapes=[
            VMEM((n, *TILE) if isinstance(n, int) else (*n, *TILE), jnp.float32)
            for n in ((NTR, 6), 6, 4, 4, 4, 6, 6, 4, 4, 4)
        ],
    )(*near(ext, te, to), stoich)
    gathered = lax.all_to_all(rows, "comp", 0, 0, tiled=True)
    ocean_out = jnp.swapaxes(gathered, 0, 1).reshape(3, comps * ROWS, 256)
    return ocean_out, tracers_out


def solution(mesh):
    in_specs = (P(None, "ty", "tx"), P(None, "ty", "comp", "tx"), P("ty", "tx"), P())
    out_specs = (P(None, "ty", "tx"), P(None, "ty", "comp", "tx"))
    return jax.shard_map(shards, mesh=mesh, in_specs=in_specs, out_specs=out_specs, check_vma=False)
```

time: 77.6 us -> 66.8 us (0.86)
  the two profiles are of different devices: /device:TPU:800 before, /device:TPU:864 now
where the time goes in v2:
time: 66.8 us; the launch traced here: 66.6 us
  starting transfers between devices  25.1 us (38%)
  waiting for transfers between devices  19.7 us (29%)
  blocking collectives  11.6 us (17%)
  Pallas kernels  8.82 us (13%)
  between operations  0.68 us (1%)
    ppermute x1, waiting for transfers between devices, shards(): from_odd = lax.ppermute(packed, 'tx', swaps(tiles, 1))  16.2 us
    all_to_all x1, blocking collectives, shards(): gathered = lax.all_to_all(rows, 'comp', 0, 0, tiled=True)  11.6 us
    ppermute x1, starting transfers between devices, shards(): from_odd = lax.ppermute(packed, 'tx', swaps(tiles, 1))  10.7 us
    ppermute x1, starting transfers between devices, shards(): to = lax.ppermute(no, axes, swaps(comps * bands, 1, place))  8.97 us
    pallas_call x1, Pallas kernels, shards(): pl.pallas_call(main_kernel, out_shape=(arr(comps, 3, ROWS, 256), jax.Shap...  6.7 us
    ppermute x1, waiting for transfers between devices, shards(): to = lax.ppermute(no, axes, swaps(comps * bands, 1, place))  3.54 us
    ppermute x1, starting transfers between devices, shards(): te = lax.ppermute(ne, axes, swaps(comps * bands, 0, place))  3.48 us
    ppermute x1, starting transfers between devices, shards(): from_even = lax.ppermute(packed, 'tx', swaps(tiles, 0))  1.91 us
  transfers between devices with their start and end apart: 4, of which 2 were waited for; matrix products, arithmetic and copies ran while one was open for 0% of the time, Pallas kernels for 0%

profile of v2, /device:TPU:864, one launch (start us, length us, event | category | flops | bytes accessed | tf_op | source)
XLA Modules:
  0.0 66.6 jit_solution(9013607370074465873)
XLA Ops:
  0.6 1.1 %shard_map.59.own_ref = f32[45,8,128]{2,1,0:T(8,128)S(1)} custom-call(f32[3,32,256]{2,1,0:T(8,128)} %ocean_ref.1, f32[19,1,8,256]{3,2,1,0:T(8,128)} %tr_ref.1, s32[4,32]{1,0:T(4,128)} %bitcast.6), custom_call_target="tpu_custom_call" | custom-call | tf_op jit(solution)/shard_map/pallas_call | solution.py:402
  1.7 1.9 %collective-permute-start.1 = (f32[45,8,128]{2,1,0:T(8,128)S(1)}, f32[45,8,128]{2,1,0:T(8,128)S(1)}, u32[]{:S(2)}, u32[]{:S(2)}) collective-permute-start(f32[45,8,128]{2,1,0:T(8,128)S(1)} %shard_map.59.own_ref), channel_id=1, source_target_pairs={{0,1},{1,0},{2,3},{3,2},{4,5},{5,4},{6,7},{7,6},{8,9},{9,8},{10,11... | collective-permute-start | bytes 552968 | tf_op jit(solution)/shard_map/ppermute | solution.py:409
  3.6 10.7 %collective-permute-start = (f32[45,8,128]{2,1,0:T(8,128)S(1)}, f32[45,8,128]{2,1,0:T(8,128)S(1)}, u32[]{:S(2)}, u32[]{:S(2)}) collective-permute-start(f32[45,8,128]{2,1,0:T(8,128)S(1)} %shard_map.59.own_ref), channel_id=1, source_target_pairs={{1,2},{2,1},{3,4},{4,3},{5,6},{6,5},{7,8},{8,7},{9,10},{10,9},{11,... | collective-permute-start | bytes 552968 | tf_op jit(solution)/shard_map/ppermute | solution.py:408
  14.4 0.0 collective-permute-done.1.ee_ref
  14.4 16.2 %collective-permute-done.eo_ref = f32[45,8,128]{2,1,0:T(8,128)S(1)} collective-permute-done((f32[45,8,128]{2,1,0:T(8,128)S(1)}, f32[45,8,128]{2,1,0:T(8,128)S(1)}, u32[]{:S(2)}, u32[]{:S(2)}) %collective-permute-start) | collective-permute-done | bytes 184352 | tf_op jit(solution)/shard_map/ppermute | solution.py:408
  30.6 1.1 %shard_map.60 = (f32[23,6,8,128]{3,2,1,0:T(8,128)S(1)}, f32[23,2,8,128]{3,2,1,0:T(8,128)S(1)}, f32[23,2,8,128]{3,2,1,0:T(8,128)S(1)}) custom-call(f32[45,8,128]{2,1,0:T(8,128)S(1)} %shard_map.59.own_ref, f32[45,8,128]{2,1,0:T(8,128)S(1)} %collective-permute-done.eo_ref, f32[45,8,128]{2,1,0:T(8,128)S(1)} %collective-permute-done.1.ee_ref), custom_call_target="tpu_custom_call" | custom-call | tf_op jit(solution)/shard_map/pallas_call | solution.py:410
  31.6 3.5 %collective-permute-start.2 = (f32[23,2,8,128]{3,2,1,0:T(8,128)S(1)}, f32[23,2,8,128]{3,2,1,0:T(8,128)S(1)}, u32[]{:S(2)}, u32[]{:S(2)}) collective-permute-start(f32[23,2,8,128]{3,2,1,0:T(8,128)S(1)} %get-tuple-element.8), channel_id=1, source_target_pairs={{0,256},{256,0},{512,768},{768,512},{32,288},{288,32},{544,800},{8... | collective-permute-start | bytes 565256 | tf_op jit(solution)/shard_map/ppermute | solution.py:421
  35.1 9.0 %collective-permute-start.3 = (f32[23,2,8,128]{3,2,1,0:T(8,128)S(1)}, f32[23,2,8,128]{3,2,1,0:T(8,128)S(1)}, u32[]{:S(2)}, u32[]{:S(2)}) collective-permute-start(f32[23,2,8,128]{3,2,1,0:T(8,128)S(1)} %get-tuple-element.9), channel_id=1, source_target_pairs={{256,512},{512,256},{768,32},{32,768},{288,544},{544,288},{800,64}... | collective-permute-start | bytes 565256 | tf_op jit(solution)/shard_map/ppermute | solution.py:422
  44.1 0.0 collective-permute-done.2.te_ref
  44.1 3.5 %collective-permute-done.3.to_ref = f32[23,2,8,128]{3,2,1,0:T(8,128)S(1)} collective-permute-done((f32[23,2,8,128]{3,2,1,0:T(8,128)S(1)}, f32[23,2,8,128]{3,2,1,0:T(8,128)S(1)}, u32[]{:S(2)}, u32[]{:S(2)}) %collective-permute-start.3) | collective-permute-done | bytes 188448 | tf_op jit(solution)/shard_map/ppermute | solution.py:422
  47.6 6.7 %shard_map.61 = (f32[4,3,8,256]{3,2,1,0:T(8,128)S(1)}, f32[19,1,8,256]{3,2,1,0:T(8,128)}) custom-call(f32[23,6,8,128]{3,2,1,0:T(8,128)S(1)} %get-tuple-element.7.ext_ref, f32[23,2,8,128]{3,2,1,0:T(8,128)S(1)} %collective-permute-done.2.te_ref, f32[23,2,8,128]{3,2,1,0:T(8,128)S(1)} %collective-permute-done.3.to_ref, f32[14]{0:T(128)} %stoich_ref.1), custom_call_target="tpu_custom_call" | custom-call | tf_op jit(solution)/shard_map/pallas_call | solution.py:423
  54.3 11.6 %all_to_all.5 = f32[4,3,8,256]{3,2,1,0:T(8,128)S(1)} all-to-all(f32[4,3,8,256]{3,2,1,0:T(8,128)S(1)} %get-tuple-element.10), channel_id=1, replica_groups=mesh['comp'=4,'ty'=8,'tx'=32] {'comp'}, dimensions={0} | all-to-all | bytes 196608 | tf_op jit(solution)/shard_map/all_to_all | solution.py:433
  65.9 0.6 copy_bitcast_fusion
Async XLA Ops:
  1.7 12.7 %collective-permute-start.1 = (f32[45,8,128]{2,1,0:T(8,128)S(1)}, f32[45,8,128]{2,1,0:T(8,128)S(1)}, u32[]{:S(2)}, u32[]{:S(2)}) collective-permute-start(f32[45,8,128]{2,1,0:T(8,128)S(1)} %shard_map.59.own_ref), channel_id=1, source_target_pairs={{0,1},{1,0},{2,3},{3,2},{4,5},{5,4},{6,7},{7,6},{8,9},{9,8},{10,11... | collective-permute-start | bytes 552968 | tf_op jit(solution)/shard_map/ppermute | solution.py:409
  3.6 27.0 %collective-permute-start = (f32[45,8,128]{2,1,0:T(8,128)S(1)}, f32[45,8,128]{2,1,0:T(8,128)S(1)}, u32[]{:S(2)}, u32[]{:S(2)}) collective-permute-start(f32[45,8,128]{2,1,0:T(8,128)S(1)} %shard_map.59.own_ref), channel_id=1, source_target_pairs={{1,2},{2,1},{3,4},{4,3},{5,6},{6,5},{7,8},{8,7},{9,10},{10,9},{11,... | collective-permute-start | bytes 552968 | tf_op jit(solution)/shard_map/ppermute | solution.py:408
  31.6 12.5 %collective-permute-start.2 = (f32[23,2,8,128]{3,2,1,0:T(8,128)S(1)}, f32[23,2,8,128]{3,2,1,0:T(8,128)S(1)}, u32[]{:S(2)}, u32[]{:S(2)}) collective-permute-start(f32[23,2,8,128]{3,2,1,0:T(8,128)S(1)} %get-tuple-element.8), channel_id=1, source_target_pairs={{0,256},{256,0},{512,768},{768,512},{32,288},{288,32},{544,800},{8... | collective-permute-start | bytes 565256 | tf_op jit(solution)/shard_map/ppermute | solution.py:421
  35.1 12.5 %collective-permute-start.3 = (f32[23,2,8,128]{3,2,1,0:T(8,128)S(1)}, f32[23,2,8,128]{3,2,1,0:T(8,128)S(1)}, u32[]{:S(2)}, u32[]{:S(2)}) collective-permute-start(f32[23,2,8,128]{3,2,1,0:T(8,128)S(1)} %get-tuple-element.9), channel_id=1, source_target_pairs={{256,512},{512,256},{768,32},{32,768},{288,544},{544,288},{800,64}... | collective-permute-start | bytes 565256 | tf_op jit(solution)/shard_map/ppermute | solution.py:422

commit v3 on v2

--- a/solution.py
+++ b/solution.py
@@ -64,7 +64,7 @@
 
 
 def minmod(a, b):
-    return jnp.maximum(jnp.minimum(a, b), 0.0) + jnp.minimum(jnp.maximum(a, b), 0.0)
+    return jnp.maximum(jnp.minimum(a, b), jnp.minimum(jnp.maximum(a, b), 0.0))
 
 
 def upwind(fac, left, right):
@@ -175,13 +175,38 @@
     return lax.rem(lax.axis_index(name), 2) == 1
 
 
-def pack_kernel(ocean_ref, tr_ref, bot_ref, out_ref):
+def wet_tiles(depth):
+    level = lax.rem(lanes(), LEV).astype(jnp.float32)
+    return [
+        jnp.where(level < mix(depth[:, c : c + 1], depth[:, c + 1 : c + 2]), 1.0, 0.0)
+        for c in (0, 2)
+    ]
+
+
+def strips(keep, a, b):
+    turned = pltpu.roll(b, 4, 0)
+    return jnp.where(keep, a, turned), jnp.where(keep, turned, a)
+
+
+def unstrip(first, te, to):
+    return jnp.where(first, te, to), pltpu.roll(jnp.where(first, to, te), 4, 0)
+
+
+def pack_kernel(ocean_ref, tr_ref, bot_ref, out_ref, ne_ref, no_ref):
     start = pl.multiple_of(lax.axis_index("comp") * ROWS, ROWS)
     rows = pl.ds(start, ROWS)
+    keep = (subs() < 4) == odd("comp")
+
+    def strip(f, a, b):
+        pair = strips(keep, mix(a, half_turn(b)), mix(half_turn(a), b))
+        ne_ref[f], no_ref[f] = pair
+
     for f in range(FIELDS):
         x = tr_ref[f, 0] if f < NTR else ocean_ref[f - NTR, rows, :]
-        out_ref[2 * f] = x[:, :128]
-        out_ref[2 * f + 1] = x[:, 128:]
+        a, b = x[:, :128], x[:, 128:]
+        out_ref[2 * f] = a
+        out_ref[2 * f + 1] = b
+        strip(f, a, b)
     band = bot_ref.shape[1]
     row = lax.broadcasted_iota(jnp.int32, (ROWS, band), 0) + start
     pick = row == lax.broadcasted_iota(jnp.int32, (ROWS, band), 1)
@@ -192,14 +217,7 @@
             lanes() == c, jnp.sum(jnp.where(pick, line, 0.0), axis=1, keepdims=True), depth
         )
     out_ref[2 * FIELDS] = depth
-
-
-def wet_tiles(depth):
-    level = lax.rem(lanes(), LEV).astype(jnp.float32)
-    return [
-        jnp.where(level < mix(depth[:, c : c + 1], depth[:, c + 1 : c + 2]), 1.0, 0.0)
-        for c in (0, 2)
-    ]
+    strip(WET, *wet_tiles(depth))
 
 
 def mid_kernel(own_ref, eo_ref, ee_ref, ext_ref, ne_ref, no_ref):
@@ -212,11 +230,7 @@
             wide += [mix(low, half_turn(high)), mix(half_turn(low), high)]
         for i in range(6):
             ext_ref[f, i] = wide[i]
-        m = narrow(wide)
-        for k in range(2):
-            turned = pltpu.roll(m[2 * k + 1], 4, 0)
-            ne_ref[f, k] = jnp.where(keep, m[2 * k], turned)
-            no_ref[f, k] = jnp.where(keep, turned, m[2 * k])
+        ne_ref[f], no_ref[f] = strips(keep, wide[2], wide[3])
 
     def sides(t):
         a, b = eo_ref[t], ee_ref[t]
@@ -231,7 +245,7 @@
 
 
 def main_kernel(
-    ext_ref, te_ref, to_ref, stoich_ref, ocean_ref, out_ref, q_ref, co_ref, ch_ref, ro_ref,
+    ext_ref, se_ref, so_ref, te_ref, to_ref, stoich_ref, ocean_ref, out_ref, q_ref, co_ref, ch_ref, ro_ref,
     rh_ref, g_ref, w_ref, c2_ref, r2_ref, g2_ref,
 ):
     first = (subs() < 4) != odd("comp")
@@ -240,12 +254,9 @@
         return [ext_ref[f, i] for i in range(6)]
 
     def halo(f):
-        out = []
-        for k in range(2):
-            te, to = te_ref[f, k], to_ref[f, k]
-            out.append(jnp.where(first, te, to))
-            out.append(pltpu.roll(jnp.where(first, to, te), 4, 0))
-        return out
+        s0, s1 = unstrip(first, se_ref[f], so_ref[f])
+        c0, c1 = unstrip(first, te_ref[f], to_ref[f])
+        return [mix(c0, s0), mix(c1, s1), mix(s0, c0), mix(s1, c1)]
 
     def save(ref, tiles):
         for i, x in enumerate(tiles):
@@ -337,8 +348,8 @@
 
     for k, x in enumerate((narrow(u2_m), v2_o, t2)):
         for i, tile in enumerate(plain(x)):
-            for peer in range(ocean_ref.shape[0]):
-                ocean_ref[peer, k, :, 128 * i : 128 * (i + 1)] = tile
+            for peer in range(0, ocean_ref.shape[1], ROWS):
+                ocean_ref[k, peer : peer + ROWS, 128 * i : 128 * (i + 1)] = tile
 
     save(c2_ref, col_factor(u2_m, w_m))
     fr_o, fr_h = row_factor(v2_o, v2_h, w_o, w_oh)
@@ -399,40 +410,41 @@
     def place(row):
         return (row % comps) * bands + row // comps
 
-    packed = pl.pallas_call(
+    packed, strip_e, strip_o = pl.pallas_call(
         pack_kernel,
-        out_shape=arr(2 * FIELDS + 1, *TILE),
+        out_shape=(arr(2 * FIELDS + 1, *TILE), arr(FIELDS + 1, *TILE), arr(FIELDS + 1, *TILE)),
         in_specs=[vmem] * 3,
-        out_specs=vmem,
+        out_specs=(vmem,) * 3,
     )(ocean, tracers, bottom.T)
+    axes = ("comp", "ty")
+    even_rows = swaps(comps * bands, 0, place)
+    odd_rows = swaps(comps * bands, 1, place)
     from_odd = lax.ppermute(packed, "tx", swaps(tiles, 1))
     from_even = lax.ppermute(packed, "tx", swaps(tiles, 0))
+    so = lax.ppermute(strip_o, axes, odd_rows)
+    se = lax.ppermute(strip_e, axes, even_rows)
     ext, ne, no = pl.pallas_call(
         mid_kernel,
-        out_shape=(
-            arr(FIELDS + 1, 6, *TILE),
-            arr(FIELDS + 1, 2, *TILE),
-            arr(FIELDS + 1, 2, *TILE),
-        ),
+        out_shape=(arr(FIELDS + 1, 6, *TILE), arr(FIELDS + 1, *TILE), arr(FIELDS + 1, *TILE)),
         in_specs=[vmem] * 3,
         out_specs=(vmem,) * 3,
     )(*near(packed, from_odd, from_even))
-    axes = ("comp", "ty")
-    te = lax.ppermute(ne, axes, swaps(comps * bands, 0, place))
-    to = lax.ppermute(no, axes, swaps(comps * bands, 1, place))
+    to = lax.ppermute(no, axes, odd_rows)
+    te = lax.ppermute(ne, axes, even_rows)
     rows, tracers_out = pl.pallas_call(
         main_kernel,
-        out_shape=(arr(comps, 3, ROWS, 256), jax.ShapeDtypeStruct((NTR, 1, ROWS, 256), jnp.float32)),
-        in_specs=[vmem] * 3 + [pl.BlockSpec(memory_space=pltpu.SMEM)],
+        out_shape=(
+            arr(3, comps * ROWS, 256),
+            jax.ShapeDtypeStruct((NTR, 1, ROWS, 256), jnp.float32),
+        ),
+        in_specs=[vmem] * 5 + [pl.BlockSpec(memory_space=pltpu.SMEM)],
         out_specs=(vmem, vmem),
         scratch_shapes=[
             VMEM((n, *TILE) if isinstance(n, int) else (*n, *TILE), jnp.float32)
             for n in ((NTR, 6), 6, 4, 4, 4, 6, 6, 4, 4, 4)
         ],
-    )(*near(ext, te, to), stoich)
-    gathered = lax.all_to_all(rows, "comp", 0, 0, tiled=True)
-    ocean_out = jnp.swapaxes(gathered, 0, 1).reshape(3, comps * ROWS, 256)
-    return ocean_out, tracers_out
+    )(*near(ext, se, so, te, to), stoich)
+    return lax.all_to_all(rows, "comp", 1, 1, tiled=True), tracers_out
 
 
 def solution(mesh):

time: 66.8 us -> 66.1 us (0.990)
  the two profiles are of different devices: /device:TPU:864 before, /device:TPU:800 now
where the time goes in v3:
time: 66.1 us; the launch traced here: 65.8 us
  starting transfers between devices  27.4 us (41%)
  waiting for transfers between devices  18.1 us (27%)
  blocking collectives  9.93 us (15%)
  Pallas kernels  8.91 us (13%)
  local copies, waits for them, and re-layouts  0.73 us (1%)
  between operations  0.71 us (1%)
    ppermute x1, waiting for transfers between devices, shards(): from_odd = lax.ppermute(packed, 'tx', swaps(tiles, 1))  12.8 us
    ppermute x1, starting transfers between devices, shards(): from_odd = lax.ppermute(packed, 'tx', swaps(tiles, 1))  10.7 us
    all_to_all x1, blocking collectives, shards(): return (lax.all_to_all(rows, 'comp', 1, 1, tiled=True), tracers_out)  9.93 us
    pallas_call x1, Pallas kernels, shards(): pl.pallas_call(main_kernel, out_shape=(arr(3, comps * ROWS, 256), jax.Sha...  6.69 us
    ppermute x1, waiting for transfers between devices, shards(): to = lax.ppermute(no, axes, odd_rows)  5.26 us
    ppermute x1, starting transfers between devices, shards(): so = lax.ppermute(strip_o, axes, odd_rows)  4.53 us
    ppermute x1, starting transfers between devices, shards(): se = lax.ppermute(strip_e, axes, even_rows)  3.48 us
    ppermute x1, starting transfers between devices, shards(): te = lax.ppermute(ne, axes, even_rows)  3.48 us
  transfers between devices with their start and end apart: 6, of which 2 were waited for; matrix products, arithmetic and copies ran while one was open for 0% of the time, Pallas kernels for 2%

profile of v3, /device:TPU:800, one launch (start us, length us, event | category | flops | bytes accessed | tf_op | source)
XLA Modules:
  0.0 65.8 jit_solution(16377813624186544042)
XLA Ops:
  0.6 1.2 %shard_map.59 = (f32[45,8,128]{2,1,0:T(8,128)S(1)}, f32[23,8,128]{2,1,0:T(8,128)S(1)}, f32[23,8,128]{2,1,0:T(8,128)S(1)}) custom-call(f32[3,32,256]{2,1,0:T(8,128)} %ocean_ref.1, f32[19,1,8,256]{3,2,1,0:T(8,128)} %tr_ref.1, s32[4,32]{1,0:T(4,128)} %bitcast.1), custom_call_target="tpu_custom_call" | custom-call | tf_op jit(solution)/shard_map/pallas_call | solution.py:413
  1.8 1.9 %collective-permute-start.1 = (f32[45,8,128]{2,1,0:T(8,128)S(1)}, f32[45,8,128]{2,1,0:T(8,128)S(1)}, u32[]{:S(2)}, u32[]{:S(2)}) collective-permute-start(f32[45,8,128]{2,1,0:T(8,128)S(1)} %get-tuple-element.10.own_ref), channel_id=1, source_target_pairs={{0,1},{1,0},{2,3},{3,2},{4,5},{5,4},{6,7},{7,6},{8,9},{9,8},{10,11... | collective-permute-start | bytes 552968 | tf_op jit(solution)/shard_map/ppermute | solution.py:423
  3.8 10.7 %collective-permute-start = (f32[45,8,128]{2,1,0:T(8,128)S(1)}, f32[45,8,128]{2,1,0:T(8,128)S(1)}, u32[]{:S(2)}, u32[]{:S(2)}) collective-permute-start(f32[45,8,128]{2,1,0:T(8,128)S(1)} %get-tuple-element.10.own_ref), channel_id=1, source_target_pairs={{1,2},{2,1},{3,4},{4,3},{5,6},{6,5},{7,8},{8,7},{9,10},{10,9},{11,... | collective-permute-start | bytes 552968 | tf_op jit(solution)/shard_map/ppermute | solution.py:422
  14.5 3.5 %collective-permute-start.2 = (f32[23,8,128]{2,1,0:T(8,128)S(1)}, f32[23,8,128]{2,1,0:T(8,128)S(1)}, u32[]{:S(2)}, u32[]{:S(2)}) collective-permute-start(f32[23,8,128]{2,1,0:T(8,128)S(1)} %get-tuple-element.12), channel_id=1, source_target_pairs={{0,256},{256,0},{512,768},{768,512},{32,288},{288,32},{544,800},{8... | collective-permute-start | bytes 282632 | tf_op jit(solution)/shard_map/ppermute | solution.py:425
  18.0 4.5 %collective-permute-start.3 = (f32[23,8,128]{2,1,0:T(8,128)S(1)}, f32[23,8,128]{2,1,0:T(8,128)S(1)}, u32[]{:S(2)}, u32[]{:S(2)}) collective-permute-start(f32[23,8,128]{2,1,0:T(8,128)S(1)} %get-tuple-element.13), channel_id=1, source_target_pairs={{256,512},{512,256},{768,32},{32,768},{288,544},{544,288},{800,64}... | collective-permute-start | bytes 282632 | tf_op jit(solution)/shard_map/ppermute | solution.py:424
  22.5 0.0 collective-permute-done.1.ee_ref
  22.6 12.8 %collective-permute-done.eo_ref = f32[45,8,128]{2,1,0:T(8,128)S(1)} collective-permute-done((f32[45,8,128]{2,1,0:T(8,128)S(1)}, f32[45,8,128]{2,1,0:T(8,128)S(1)}, u32[]{:S(2)}, u32[]{:S(2)}) %collective-permute-start) | collective-permute-done | bytes 184352 | tf_op jit(solution)/shard_map/ppermute | solution.py:422
  35.4 1.0 %shard_map.60 = (f32[23,6,8,128]{3,2,1,0:T(8,128)S(1)}, f32[23,8,128]{2,1,0:T(8,128)S(1)}, f32[23,8,128]{2,1,0:T(8,128)S(1)}) custom-call(f32[45,8,128]{2,1,0:T(8,128)S(1)} %get-tuple-element.10.own_ref, f32[45,8,128]{2,1,0:T(8,128)S(1)} %collective-permute-done.eo_ref, f32[45,8,128]{2,1,0:T(8,128)S(1)} %collective-permute-done.1.ee_ref), custom_call_target="tpu_custom_call" | custom-call | tf_op jit(solution)/shard_map/pallas_call | solution.py:426
  36.4 3.5 %collective-permute-start.4 = (f32[23,8,128]{2,1,0:T(8,128)S(1)}, f32[23,8,128]{2,1,0:T(8,128)S(1)}, u32[]{:S(2)}, u32[]{:S(2)}) collective-permute-start(f32[23,8,128]{2,1,0:T(8,128)S(1)} %get-tuple-element.14), channel_id=1, source_target_pairs={{0,256},{256,0},{512,768},{768,512},{32,288},{288,32},{544,800},{8... | collective-permute-start | bytes 282632 | tf_op jit(solution)/shard_map/ppermute | solution.py:433
  39.9 3.3 %collective-permute-start.5 = (f32[23,8,128]{2,1,0:T(8,128)S(1)}, f32[23,8,128]{2,1,0:T(8,128)S(1)}, u32[]{:S(2)}, u32[]{:S(2)}) collective-permute-start(f32[23,8,128]{2,1,0:T(8,128)S(1)} %get-tuple-element.15), channel_id=1, source_target_pairs={{256,512},{512,256},{768,32},{32,768},{288,544},{544,288},{800,64}... | collective-permute-start | bytes 282632 | tf_op jit(solution)/shard_map/ppermute | solution.py:432
  43.1 0.0 collective-permute-done.2.se_ref
  43.1 0.0 collective-permute-done.3.so_ref
  43.2 0.0 collective-permute-done.4.te_ref
  43.2 5.3 %collective-permute-done.5.to_ref = f32[23,8,128]{2,1,0:T(8,128)S(1)} collective-permute-done((f32[23,8,128]{2,1,0:T(8,128)S(1)}, f32[23,8,128]{2,1,0:T(8,128)S(1)}, u32[]{:S(2)}, u32[]{:S(2)}) %collective-permute-start.5) | collective-permute-done | bytes 94240 | tf_op jit(solution)/shard_map/ppermute | solution.py:432
  48.4 6.7 %shard_map.61 = (f32[3,32,256]{2,1,0:T(8,128)S(1)}, f32[19,1,8,256]{3,2,1,0:T(8,128)}) custom-call(f32[23,6,8,128]{3,2,1,0:T(8,128)S(1)} %get-tuple-element.11.ext_ref, f32[23,8,128]{2,1,0:T(8,128)S(1)} %collective-permute-done.2.se_ref, f32[23,8,128]{2,1,0:T(8,128)S(1)} %collective-permute-done.3.so_ref, f32[23,8,128]{2,1,0:T(8,128)S(1)} %collective-permute-done.4.te_ref, ...), custom_call_target="tpu_custom_call" | custom-call | tf_op jit(solution)/shard_map/pallas_call | solution.py:434
  55.1 0.1 copy.6
  55.2 9.9 %all_to_all.5 = f32[3,32,256]{2,0,1:T(4,128)S(1)} all-to-all(f32[3,32,256]{2,0,1:T(4,128)S(1)} %copy.6), channel_id=1, replica_groups=mesh['comp'=4,'ty'=8,'tx'=32] {'comp'}, dimensions={1} | all-to-all | bytes 196608 | tf_op jit(solution)/shard_map/all_to_all | solution.py:447
  65.1 0.7 %copy.7 = f32[3,32,256]{2,1,0:T(8,128)} copy(f32[3,32,256]{2,0,1:T(4,128)S(1)} %all_to_all.5) | data formatting | bytes 196608
Async XLA Ops:
  1.8 20.7 %collective-permute-start.1 = (f32[45,8,128]{2,1,0:T(8,128)S(1)}, f32[45,8,128]{2,1,0:T(8,128)S(1)}, u32[]{:S(2)}, u32[]{:S(2)}) collective-permute-start(f32[45,8,128]{2,1,0:T(8,128)S(1)} %get-tuple-element.10.own_ref), channel_id=1, source_target_pairs={{0,1},{1,0},{2,3},{3,2},{4,5},{5,4},{6,7},{7,6},{8,9},{9,8},{10,11... | collective-permute-start | bytes 552968 | tf_op jit(solution)/shard_map/ppermute | solution.py:423
  3.8 31.6 %collective-permute-start = (f32[45,8,128]{2,1,0:T(8,128)S(1)}, f32[45,8,128]{2,1,0:T(8,128)S(1)}, u32[]{:S(2)}, u32[]{:S(2)}) collective-permute-start(f32[45,8,128]{2,1,0:T(8,128)S(1)} %get-tuple-element.10.own_ref), channel_id=1, source_target_pairs={{1,2},{2,1},{3,4},{4,3},{5,6},{6,5},{7,8},{8,7},{9,10},{10,9},{11,... | collective-permute-start | bytes 552968 | tf_op jit(solution)/shard_map/ppermute | solution.py:422
  14.5 28.6 %collective-permute-start.2 = (f32[23,8,128]{2,1,0:T(8,128)S(1)}, f32[23,8,128]{2,1,0:T(8,128)S(1)}, u32[]{:S(2)}, u32[]{:S(2)}) collective-permute-start(f32[23,8,128]{2,1,0:T(8,128)S(1)} %get-tuple-element.12), channel_id=1, source_target_pairs={{0,256},{256,0},{512,768},{768,512},{32,288},{288,32},{544,800},{8... | collective-permute-start | bytes 282632 | tf_op jit(solution)/shard_map/ppermute | solution.py:425
  18.0 25.1 %collective-permute-start.3 = (f32[23,8,128]{2,1,0:T(8,128)S(1)}, f32[23,8,128]{2,1,0:T(8,128)S(1)}, u32[]{:S(2)}, u32[]{:S(2)}) collective-permute-start(f32[23,8,128]{2,1,0:T(8,128)S(1)} %get-tuple-element.13), channel_id=1, source_target_pairs={{256,512},{512,256},{768,32},{32,768},{288,544},{544,288},{800,64}... | collective-permute-start | bytes 282632 | tf_op jit(solution)/shard_map/ppermute | solution.py:424
  36.4 6.8 %collective-permute-start.4 = (f32[23,8,128]{2,1,0:T(8,128)S(1)}, f32[23,8,128]{2,1,0:T(8,128)S(1)}, u32[]{:S(2)}, u32[]{:S(2)}) collective-permute-start(f32[23,8,128]{2,1,0:T(8,128)S(1)} %get-tuple-element.14), channel_id=1, source_target_pairs={{0,256},{256,0},{512,768},{768,512},{32,288},{288,32},{544,800},{8... | collective-permute-start | bytes 282632 | tf_op jit(solution)/shard_map/ppermute | solution.py:433
  39.9 8.6 %collective-permute-start.5 = (f32[23,8,128]{2,1,0:T(8,128)S(1)}, f32[23,8,128]{2,1,0:T(8,128)S(1)}, u32[]{:S(2)}, u32[]{:S(2)}) collective-permute-start(f32[23,8,128]{2,1,0:T(8,128)S(1)} %get-tuple-element.15), channel_id=1, source_target_pairs={{256,512},{512,256},{768,32},{32,768},{288,544},{544,288},{800,64}... | collective-permute-start | bytes 282632 | tf_op jit(solution)/shard_map/ppermute | solution.py:432

commit v4 on v3

v4 whole, which is shorter than its diff:
```python
import jax
import jax.numpy as jnp
from jax import lax
from jax.experimental import pallas as pl
from jax.experimental.pallas import tpu as pltpu
from jax.sharding import PartitionSpec as P


LEV = 64
NTR = 19
ROWS = 8
FIELDS = 22
U, V, T, WET = 19, 20, 21, 22
PAIRS = 12
AUX = (
    "w_s", "p_e", "p_h", "sun_e", "sun_h", "heat_e", "heat_h", "cols_e", "rows_h", "u1_s",
    "u1_e", "v1_s", "v1_h", "t1_s", "sun2", "heat2",
)
VMEM = pltpu.VMEM
TILE = (ROWS, 128)


def lanes():
    return lax.broadcasted_iota(jnp.int32, TILE, 1)


def subs():
    return lax.broadcasted_iota(jnp.int32, TILE, 0)


def half_turn(x):
    return pltpu.roll(x, LEV, 1)


def mix(a, b):
    return jnp.where(lanes() < LEV, a, b)


def own_of(w):
    return [mix(w[4], w[0]), mix(w[5], w[1])]


def edge_of(w):
    return [w[2], w[3]]


def each(f, *lists):
    return [f(*args) for args in zip(*lists)]


def next_col(x):
    return x[1:] + [half_turn(x[0])]


def prev_col(x):
    return [half_turn(x[-1])] + x[:-1]


def next_split(s, e):
    return [s[1], mix(half_turn(s[0]), e[0])], [e[1], s[0]]


def prev_split(s, e):
    return [mix(e[1], half_turn(s[1])), s[0]], [s[1], e[0]]


def next_row(o, h):
    edge = subs() == 0
    return (
        [pltpu.roll(jnp.where(edge, b, a), ROWS - 1, 0) for a, b in zip(o, h)],
        [pltpu.roll(jnp.where(edge, a, b), ROWS - 1, 0) for a, b in zip(o, h)],
    )


def prev_row(o, h):
    edge = subs() == ROWS - 1
    return (
        [pltpu.roll(jnp.where(edge, b, a), 1, 0) for a, b in zip(o, h)],
        [pltpu.roll(jnp.where(edge, a, b), 1, 0) for a, b in zip(o, h)],
    )


def minmod(a, b):
    return jnp.maximum(jnp.minimum(a, b), jnp.minimum(jnp.maximum(a, b), 0.0))


def upwind(fac, left, right):
    return fac * jnp.where(fac > 0.0, left, right)


def minus(x, y):
    return each(lambda a, b: a - b, x, y)


def col_divergence(q, fac):
    d = minus(next_col(q), q)
    m = each(minmod, d, prev_col(d))
    left = each(lambda a, b: (a + a) + b, q, m)
    right = each(lambda a, b: (a + a) - b, q, m)
    flux = each(upwind, fac, left, next_col(right))
    return minus(flux, prev_col(flux))


def split_divergence(s, e, fac_s, fac_e):
    n_s, n_e = next_split(s, e)
    d_s, d_e = minus(n_s, s), minus(n_e, e)
    b_s, b_e = prev_split(d_s, d_e)
    m_s, m_e = each(minmod, d_s, b_s), each(minmod, d_e, b_e)
    r_s = each(lambda a, b: (a + a) - b, s, m_s)
    r_e = each(lambda a, b: (a + a) - b, e, m_e)
    n_s, n_e = next_split(r_s, r_e)
    f_s = each(lambda f, a, b, c: upwind(f, (a + a) + b, c), fac_s, s, m_s, n_s)
    f_e = each(lambda f, a, b, c: upwind(f, (a + a) + b, c), fac_e, e, m_e, n_e)
    return minus(f_s, prev_split(f_s, f_e)[0])


def row_divergence(o, h, fac_o, fac_h):
    n_o, n_h = next_row(o, h)
    d_o, d_h = minus(n_o, o), minus(n_h, h)
    b_o, b_h = prev_row(d_o, d_h)
    m_o, m_h = each(minmod, d_o, b_o), each(minmod, d_h, b_h)
    r_o = each(lambda a, b: (a + a) - b, o, m_o)
    r_h = each(lambda a, b: (a + a) - b, h, m_h)
    n_o, n_h = next_row(r_o, r_h)
    f_o = each(lambda f, a, b, c: upwind(f, (a + a) + b, c), fac_o, o, m_o, n_o)
    f_h = each(lambda f, a, b, c: upwind(f, (a + a) + b, c), fac_h, h, m_h, n_h)
    p_o, p_h = prev_row(f_o, f_h)
    return minus(f_o, p_o), minus(f_h, p_h)


def half_factor(vel, wet, next_vel, next_wet):
    return 0.5 * (0.08 * (0.5 * (vel + next_vel) * wet * next_wet))


def col_factor(vel, wet):
    return each(half_factor, vel, wet, next_col(vel), next_col(wet))


def split_factor(vel_s, vel_e, wet_s, wet_e):
    n_s, n_e = next_split(vel_s, vel_e)
    w_s, w_e = next_split(wet_s, wet_e)
    return each(half_factor, vel_s, wet_s, n_s, w_s), each(half_factor, vel_e, wet_e, n_e, w_e)


def row_factor(vel_o, vel_h, wet_o, wet_h):
    n_o, n_h = next_row(vel_o, vel_h)
    w_o, w_h = next_row(wet_o, wet_h)
    return each(half_factor, vel_o, wet_o, n_o, w_o), each(half_factor, vel_h, wet_h, n_h, w_h)


def level_sum(tiles, inclusive):
    r = lax.rem(lax.broadcasted_iota(jnp.int32, (256, 128), 0), 128)
    c = lax.broadcasted_iota(jnp.int32, (256, 128), 1)
    above = (r <= c) if inclusive else (r < c)
    ladder = jnp.where(((r < LEV) == (c < LEV)) & above, 1.0, 0.0).astype(jnp.bfloat16)
    x = jnp.concatenate(tiles, axis=0)
    major = x.astype(jnp.bfloat16)
    minor = (x - major.astype(jnp.float32)).astype(jnp.bfloat16)
    out = jnp.dot(
        jnp.concatenate([major, minor], axis=1), ladder, preferred_element_type=jnp.float32
    )
    return [out[ROWS * i : ROWS * (i + 1)] for i in range(len(tiles))]


def optics(chloro, wet):
    absorb = each(lambda a, w: (0.04 + 0.03 * jnp.maximum(a, 0.0)) * w, chloro, wet)
    sun = [jnp.exp(-s) for s in level_sum(absorb, False)]
    heat = each(lambda s, a, w: s * (1.0 - jnp.exp(-a)) * w, sun, absorb, wet)
    return sun, heat


def east_speed(u, v, n, b, w):
    return each(
        lambda u, v, n, b, w: w * (0.95 * u + 0.2 * (v - 0.5 * (n - b))), u, v, n, b, w
    )


def north_speed(u, v, n, b, w):
    return each(
        lambda u, v, n, b, w: w * (0.95 * v - 0.2 * (u + 0.5 * (n - b))), u, v, n, b, w
    )


def plus(x, y):
    return each(lambda a, b: a + b, x, y)


def warmed(t, heat, rows, cols, w):
    return each(
        lambda t, heat, r, c, w: w * (t + 0.2 * (2.0 * heat + 0.2 * (r + c - 4.0 * t))),
        t, heat, rows, cols, w,
    )


def reaction(adv, sun, temp):
    n, p, c, z, d = [jnp.maximum(a, 0.0) for a in adv]
    uptake = sun / (sun + 0.2) * n / (n + 0.5) * jnp.exp(0.1 * temp)
    growth = uptake * p
    grazing = 0.8 * z * p * p / (p * p + 0.3)
    dying = 0.1 * p
    remin = 0.2 * d
    core = [
        remin - growth,
        growth - grazing - dying,
        0.3 * (0.5 * p - c) + 0.2 * growth,
        0.3 * grazing - 0.05 * z,
        dying + 0.7 * grazing + 0.05 * z - remin,
    ]
    return core, 0.2 * (growth - remin)


def odd(name):
    return lax.rem(lax.axis_index(name), 2) == 1


def wet_tiles(depth):
    level = lax.rem(lanes(), LEV).astype(jnp.float32)
    return [
        jnp.where(level < mix(depth[:, c : c + 1], depth[:, c + 1 : c + 2]), 1.0, 0.0)
        for c in (0, 2)
    ]


def unstrip(below, above):
    first = subs() < 4
    return [
        jnp.where(first, below, above),
        pltpu.roll(jnp.where(first, above, below), 4, 0),
    ]


def pack_kernel(ocean_ref, tr_ref, bot_ref, stoich_ref, out_ref, up_ref, down_ref, yield_ref):
    for j in range(NTR - 5):
        yield_ref[j] = jnp.full(TILE, stoich_ref[j], jnp.float32)
    start = pl.multiple_of(lax.axis_index("comp") * ROWS, ROWS)
    rows = pl.ds(start, ROWS)

    def strip(f, a, b):
        a, b = mix(a, half_turn(b)), pltpu.roll(mix(half_turn(a), b), 4, 0)
        up_ref[f] = jnp.where(subs() < 4, a, b)
        down_ref[f] = jnp.where(subs() < 4, b, a)

    for f in range(FIELDS):
        x = tr_ref[f, 0] if f < NTR else ocean_ref[f - NTR, rows, :]
        a, b = x[:, :128], x[:, 128:]
        out_ref[2 * f] = a
        out_ref[2 * f + 1] = b
        strip(f, a, b)
    band = bot_ref.shape[1]
    row = lax.broadcasted_iota(jnp.int32, (ROWS, band), 0) + start
    pick = row == lax.broadcasted_iota(jnp.int32, (ROWS, band), 1)
    depth = jnp.zeros(TILE, jnp.float32)
    for c in range(4):
        line = bot_ref[c : c + 1, :].astype(jnp.float32)
        depth = jnp.where(
            lanes() == c, jnp.sum(jnp.where(pick, line, 0.0), axis=1, keepdims=True), depth
        )
    out_ref[2 * FIELDS] = depth
    strip(WET, *wet_tiles(depth))


def sides(own_ref, eo_ref, ee_ref, t):
    flip = odd("tx")
    a, b = eo_ref[t], ee_ref[t]
    return jnp.where(flip, b, a), own_ref[t], jnp.where(flip, a, b)


def corner_kernel(own_ref, eo_ref, ee_ref, up_ref, down_ref):
    sub = subs()
    west, _, east = sides(own_ref, eo_ref, ee_ref, 2 * FIELDS)
    wet = wet_tiles(west)[1], wet_tiles(east)[0]

    def edge(f):
        if f < 0:
            return [jnp.zeros(TILE, jnp.float32)] * 2
        if f == WET:
            w, e = wet
        else:
            w = sides(own_ref, eo_ref, ee_ref, 2 * f + 1)[0]
            e = sides(own_ref, eo_ref, ee_ref, 2 * f)[2]
        return [mix(w, half_turn(e)), mix(half_turn(w), e)]

    for k in range(PAIRS):
        a, b, c, d = edge(2 * k - 1) + edge(2 * k)
        turned = pltpu.roll(c, 4, 0)
        up_ref[k] = jnp.where(
            sub < 4,
            jnp.where(sub < 2, a, pltpu.roll(b, 2, 0)),
            jnp.where(sub < 6, turned, pltpu.roll(d, 6, 0)),
        )
        down_ref[k] = jnp.where(
            sub < 4,
            jnp.where(sub < 2, pltpu.roll(d, 2, 0), turned),
            jnp.where(sub < 6, pltpu.roll(b, 6, 0), a),
        )


def save(ref, tiles):
    for i, x in enumerate(tiles):
        ref[i] = x


def load(ref, *names):
    if not names:
        return [ref[i] for i in range(ref.shape[0])]
    return [[ref[2 * AUX.index(n)], ref[2 * AUX.index(n) + 1]] for n in names]


def own_kernel(
    own_ref, eo_ref, ee_ref, below_ref, above_ref, stoich_ref, raw_ref, part_ref, q1_ref,
    aux_ref, fc_ref, fr_ref, g_ref,
):
    def arrange(a, b):
        pairs = ((a[0], b[1]), (b[0], a[2]), (a[1], b[2]))
        out = []
        for low, high in pairs:
            out += [mix(low, half_turn(high)), mix(half_turn(low), high)]
        return out

    def wide(f):
        return arrange(*[sides(own_ref, eo_ref, ee_ref, 2 * f + i) for i in range(2)])

    def halo(f):
        return unstrip(below_ref[f], above_ref[f])

    u_w, v_w, t_w = [wide(f) for f in (U, V, T)]
    depth = sides(own_ref, eo_ref, ee_ref, 2 * FIELDS)
    w_w = arrange(*zip(*[wet_tiles(x) for x in depth]))
    u_h, v_h, t_h, w_h = [halo(f) for f in (U, V, T, WET)]
    u_s, v_s, t_s, w_s = [own_of(x) for x in (u_w, v_w, t_w, w_w)]
    w_e = edge_of(w_w)
    for f, wd, h in ((U, u_w, u_h), (V, v_w, v_h), (T, t_w, t_h), (WET, w_w, w_h)):
        save(raw_ref.at[f], edge_of(wd) + h)

    press = [0.05 * s for s in level_sum(t_w + t_h, True)]
    p_w, p_h = press[:6], press[6:]
    p_s = own_of(p_w)
    q_w, q_h = wide(2), halo(2)
    sun, heat = optics(own_of(q_w) + edge_of(q_w) + q_h, w_s + w_e + w_h)
    u1_w = east_speed(u_w, v_w, next_col(p_w), prev_col(p_w), w_w)
    (n_s, n_h), (b_s, b_h) = next_row(p_s, p_h), prev_row(p_s, p_h)
    v1_s = north_speed(u_s, v_s, n_s, b_s, w_s)
    v1_h = north_speed(u_h, v_h, n_h, b_h, w_h)
    (n_s, n_h), (b_s, b_h) = next_row(t_s, t_h), prev_row(t_s, t_h)
    around = plus(next_col(t_w), prev_col(t_w))
    t1_s = warmed(t_s, heat[:2], plus(n_s, b_s), own_of(around), w_s)
    save(fc_ref, col_factor(u1_w, w_w))
    fr_s, fr_h = row_factor(v1_s, v1_h, w_s, w_h)
    save(fr_ref, fr_s + fr_h)

    def advect(f):
        q_w, q_h = wide(f), halo(f)
        q_s, q_e = own_of(q_w), edge_of(q_w)
        col = col_divergence(q_w, load(fc_ref))
        fr = load(fr_ref)
        r_s, r_h = row_divergence(q_s, q_h, fr[:2], fr[2:])
        save(raw_ref.at[f], q_e + q_h)
        save(part_ref.at[f], minus(q_e, edge_of(col)) + minus(q_h, r_h))
        return minus(minus(q_s, own_of(col)), r_s)

    first = [advect(f) for f in range(5)]
    gain, chloro = [], []
    for i in range(2):
        core, g = reaction([first[f][i] for f in range(5)], sun[i], t1_s[i])
        gain.append(g)
        for f in range(5):
            q1_ref[f, i] = (first[f][i] + 0.2 * core[f]) * w_s[i]
        chloro.append((first[2][i] + 0.2 * core[2]) * w_s[i])
    sun2, heat2 = optics(chloro, w_s)
    save(g_ref, gain + w_s)
    values = dict(
        w_s=w_s, p_e=edge_of(p_w), p_h=p_h, sun_e=sun[2:4], sun_h=sun[4:], heat_e=heat[2:4],
        heat_h=heat[4:], cols_e=edge_of(around), rows_h=plus(n_h, b_h), u1_s=own_of(u1_w),
        u1_e=edge_of(u1_w), v1_s=v1_s, v1_h=v1_h, t1_s=t1_s, sun2=sun2, heat2=heat2,
    )
    save(aux_ref, [x for n in AUX for x in values[n]])

    def others(f, _):
        s = stoich_ref[f - 5]
        k = load(g_ref)
        out = each(lambda a, g, w: (a + s * g) * w, advect(f), k[:2], k[2:])
        save(q1_ref.at[f], out)
        return 0

    lax.fori_loop(5, NTR, others, 0, unroll=2)


def plain(x):
    return [mix(x[0], half_turn(x[1])), mix(half_turn(x[0]), x[1])]


def edge_kernel(
    raw_ref, part_ref, aux_ref, below_ref, above_ref, stoich_ref, ocean_ref, q_ref, c2_ref,
    r2_ref, t2_ref, fc_ref, fr_ref, g_ref,
):
    sub4 = subs() < 4

    def corners(k):
        b, a = below_ref[k], above_ref[k]
        return (
            [
                jnp.where(sub4, b, a),
                jnp.where(sub4, pltpu.roll(b, 6, 0), pltpu.roll(a, 2, 0)),
            ],
            [
                pltpu.roll(jnp.where(sub4, a, b), 4, 0),
                jnp.where(sub4, pltpu.roll(b, 2, 0), pltpu.roll(a, 6, 0)),
            ],
        )

    def raw(f):
        x = load(raw_ref.at[f])
        return x[:2], x[2:]

    (u_c, v_c), (t_c, w_c) = corners((U + 1) // 2), corners((T + 1) // 2)
    (u_e, u_h), (v_e, v_h), (t_e, t_h), (w_e, w_h) = [raw(f) for f in (U, V, T, WET)]
    w_s, p_e, p_h = load(aux_ref, "w_s", "p_e", "p_h")
    p_c = [0.05 * s for s in level_sum(t_c, True)]

    (n_h, n_c), (b_h, b_c) = next_split(p_h, p_c), prev_split(p_h, p_c)
    u1_h = east_speed(u_h, v_h, n_h, b_h, w_h)
    u1_c = east_speed(u_c, v_c, n_c, b_c, w_c)
    (n_e, n_c), (b_e, b_c) = next_row(p_e, p_c), prev_row(p_e, p_c)
    v1_e = north_speed(u_e, v_e, n_e, b_e, w_e)
    v1_c = north_speed(u_c, v_c, n_c, b_c, w_c)
    heat_e, heat_h, cols_e, rows_h = load(aux_ref, "heat_e", "heat_h", "cols_e", "rows_h")
    rows_e = plus(next_row(t_e, t_c)[0], prev_row(t_e, t_c)[0])
    t1_e = warmed(t_e, heat_e, rows_e, cols_e, w_e)
    cols_h = plus(next_split(t_h, t_c)[0], prev_split(t_h, t_c)[0])
    t1_h = warmed(t_h, heat_h, rows_h, cols_h, w_h)
    fc_h, fc_c = split_factor(u1_h, u1_c, w_h, w_c)
    save(fc_ref, fc_h + fc_c)
    fr_e, fr_c = row_factor(v1_e, v1_c, w_e, w_c)
    save(fr_ref, fr_e + fr_c)

    def advect1(f, q_c):
        q_e, q_h = raw(f)
        fc, fr = load(fc_ref), load(fr_ref)
        row = row_divergence(q_e, q_c, fr[:2], fr[2:])[0]
        col = split_divergence(q_h, q_c, fc[:2], fc[2:])
        return minus(load(part_ref.at[f]), row + col)

    c = [corners(k) for k in range(3)]
    core_corners = [c[0][1], c[1][0], c[1][1], c[2][0], c[2][1]]
    first = [advect1(f, core_corners[f]) for f in range(5)]
    sun_e, sun_h = load(aux_ref, "sun_e", "sun_h")
    w_four, sun, t1_four, gain = w_e + w_h, sun_e + sun_h, t1_e + t1_h, []
    for i in range(4):
        core, g = reaction([first[f][i] for f in range(5)], sun[i], t1_four[i])
        gain.append(g)
        for f in range(5):
            q_ref[f, i] = (first[f][i] + 0.2 * core[f]) * w_four[i]
    save(g_ref, gain + w_four)

    def others1(k, _):
        both = corners(k)
        for j in range(2):
            f = 2 * k - 1 + j
            s = stoich_ref[f - 5]
            g = load(g_ref)
            out = each(lambda a, g, w: (a + s * g) * w, advect1(f, both[j]), g[:4], g[4:])
            save(q_ref.at[f], out)
        return 0

    lax.fori_loop(3, 10, others1, 0)

    u1_s, u1_e, v1_s, v1_h, t1_s, _, heat2 = load(
        aux_ref, "u1_s", "u1_e", "v1_s", "v1_h", "t1_s", "sun2", "heat2"
    )
    p1 = [0.05 * s for s in level_sum(t1_s + t1_e + t1_h, True)]
    p_s, p_e, p_h = p1[:2], p1[2:4], p1[4:]
    (n_s, n_e), (b_s, b_e) = next_split(p_s, p_e), prev_split(p_s, p_e)
    u2_s = east_speed(u1_s, v1_s, n_s, b_s, w_s)
    u2_e = east_speed(u1_e, v1_e, n_e, b_e, w_e)
    (n_s, n_h), (b_s, b_h) = next_row(p_s, p_h), prev_row(p_s, p_h)
    v2_s = north_speed(u1_s, v1_s, n_s, b_s, w_s)
    v2_h = north_speed(u1_h, v1_h, n_h, b_h, w_h)
    rows = plus(next_row(t1_s, t1_h)[0], prev_row(t1_s, t1_h)[0])
    cols = plus(next_split(t1_s, t1_e)[0], prev_split(t1_s, t1_e)[0])
    t2 = warmed(t1_s, heat2, rows, cols, w_s)

    save(t2_ref, t2)
    for k, x in enumerate((u2_s, v2_s, t2)):
        for i, tile in enumerate(plain(x)):
            for peer in range(ocean_ref.shape[0]):
                ocean_ref[peer, k, :, 128 * i : 128 * (i + 1)] = tile

    fc_s, fc_e = split_factor(u2_s, u2_e, w_s, w_e)
    save(c2_ref, fc_s + fc_e)
    fr_s, fr_h = row_factor(v2_s, v2_h, w_s, w_h)
    save(r2_ref, fr_s + fr_h)


def last_kernel(
    q1_ref, aux_ref, q_ref, c2_ref, r2_ref, t2_ref, stoich_ref, out_ref, g2_ref
):
    w_s, sun2 = load(aux_ref, "w_s", "sun2")
    t2 = load(t2_ref)

    def advect2(f):
        q_s, x = load(q1_ref.at[f]), load(q_ref.at[f])
        fc, fr = load(c2_ref), load(r2_ref)
        row = row_divergence(q_s, x[2:], fr[:2], fr[2:])[0]
        return minus(minus(q_s, split_divergence(q_s, x[:2], fc[:2], fc[2:])), row)

    def finish(f, tiles):
        for i, x in enumerate(plain(tiles)):
            out_ref[f, 0, :, 128 * i : 128 * (i + 1)] = x

    first = [advect2(f) for f in range(5)]
    done = [[] for _ in range(5)]
    gain = []
    for i in range(2):
        core, g = reaction([first[f][i] for f in range(5)], sun2[i], t2[i])
        gain.append(g)
        for f in range(5):
            done[f].append((first[f][i] + 0.2 * core[f]) * w_s[i])
    for f in range(5):
        finish(f, done[f])
    save(g2_ref, gain + w_s)

    def others2(f, _):
        s = stoich_ref[f - 5]
        k = load(g2_ref)
        finish(f, each(lambda a, g, w: (a + s * g) * w, advect2(f), k[:2], k[2:]))
        return 0

    lax.fori_loop(5, NTR, others2, 0, unroll=2)


def swaps(count, first, place=lambda i: i):
    pairs = []
    for a in range(first, count - 1, 2):
        pairs += [(place(a), place(a + 1)), (place(a + 1), place(a))]
    return pairs


def shards(ocean, tracers, bottom, stoich):
    comps = lax.axis_size("comp")
    bands = lax.axis_size("ty")
    tiles = lax.axis_size("tx")
    vmem = pl.BlockSpec(memory_space=VMEM)

    def arr(*dims):
        return VMEM(dims, jnp.float32)

    def near(*args):
        return [pltpu.with_memory_space_constraint(a, VMEM) for a in args]

    def place(row):
        return (row % comps) * bands + row // comps

    axes = ("comp", "ty")
    count = comps * bands
    ups = [(place(r), place(r - 1)) for r in range(1, count)]
    downs = [(b, a) for a, b in ups]

    def kernel(body, outs, ins, scratch=(), scalars=False):
        return pl.pallas_call(
            body,
            out_shape=tuple(outs),
            in_specs=[vmem] * ins + [pl.BlockSpec(memory_space=pltpu.SMEM)] * scalars,
            out_specs=(vmem,) * len(outs),
            scratch_shapes=[VMEM((*n, *TILE), jnp.float32) for n in scratch],
        )

    packed, strip_up, strip_down, yields = kernel(
        pack_kernel,
        [arr(n, *TILE) for n in (2 * FIELDS + 1, FIELDS + 1, FIELDS + 1, NTR - 5)],
        3,
        scalars=True,
    )(ocean, tracers, bottom.T, stoich)
    from_odd = lax.ppermute(packed, "tx", swaps(tiles, 1))
    from_even = lax.ppermute(packed, "tx", swaps(tiles, 0))
    below = lax.ppermute(strip_up, axes, ups)
    above = lax.ppermute(strip_down, axes, downs)
    blocks = near(packed, from_odd, from_even)
    corner_up, corner_down = kernel(
        corner_kernel, [arr(PAIRS, *TILE), arr(PAIRS, *TILE)], 3
    )(*blocks)
    corner_below = lax.ppermute(corner_up, axes, ups)
    corner_above = lax.ppermute(corner_down, axes, downs)
    state = kernel(
        own_kernel,
        [
            arr(FIELDS + 1, 4, *TILE),
            arr(NTR, 4, *TILE),
            arr(NTR, 2, *TILE),
            arr(2 * len(AUX), *TILE),
        ],
        6,
        [(6,), (4,), (4,)],
    )(*blocks, *near(below, above, yields))
    raw, part, q1_own, aux = near(*state)
    rows, *rest = kernel(
        edge_kernel,
        [arr(comps, 3, ROWS, 256), arr(NTR, 4, *TILE)] + [arr(n, *TILE) for n in (4, 4, 2)],
        6,
        [(4,), (4,), (8,)],
    )(raw, part, aux, *near(corner_below, corner_above, yields))
    gathered = lax.all_to_all(rows, "comp", 0, 0, tiled=True)
    (tracers_out,) = kernel(
        last_kernel, [jax.ShapeDtypeStruct((NTR, 1, ROWS, 256), jnp.float32)], 7, [(4,)]
    )(q1_own, aux, *near(*rest, yields))
    return jnp.swapaxes(gathered, 0, 1).reshape(3, comps * ROWS, 256), tracers_out


def solution(mesh):
    in_specs = (P(None, "ty", "tx"), P(None, "ty", "comp", "tx"), P("ty", "tx"), P())
    out_specs = (P(None, "ty", "tx"), P(None, "ty", "comp", "tx"))
    return jax.shard_map(shards, mesh=mesh, in_specs=in_specs, out_specs=out_specs, check_vma=False)
```

time: 66.1 us -> 60.7 us (0.918)
  the two profiles are of different devices: /device:TPU:800 before, /device:TPU:576 now
where the time goes in v4:
time: 60.7 us; the launch traced here: 60.4 us
  starting transfers between devices  35.5 us (58%)
  waiting for transfers between devices  12.2 us (20%)
  Pallas kernels  11.3 us (19%)
  between operations  0.71 us (1%)
  local copies, waits for them, and re-layouts  0.65 us (1%)
    ppermute x1, starting transfers between devices, shards(): corner_below = lax.ppermute(corner_up, axes, ups)  17.6 us
    ppermute x1, waiting for transfers between devices, shards(): from_odd = lax.ppermute(packed, 'tx', swaps(tiles, 1))  7.02 us
    ppermute x1, starting transfers between devices, shards(): below = lax.ppermute(strip_up, axes, ups)  5.37 us
    pallas_call x1, Pallas kernels, shards(): kernel(last_kernel, [jax.ShapeDtypeStruct((NTR, 1, ROWS, 256), jnp.float3...  3.53 us
    all_to_all x1, starting transfers between devices, shards(): gathered = lax.all_to_all(rows, 'comp', 0, 0, tiled=True)  3.3 us
    pallas_call x1, Pallas kernels, shards(): kernel(edge_kernel, [arr(comps, 3, ROWS, 256), arr(NTR, 4, *TILE)] + [arr...  3.24 us
    pallas_call x1, Pallas kernels, shards(): kernel(own_kernel, [arr(FIELDS + 1, 4, *TILE), arr(NTR, 4, *TILE), arr(NT...  3.17 us
    ppermute x1, starting transfers between devices, shards(): from_even = lax.ppermute(packed, 'tx', swaps(tiles, 0))  3.16 us
  transfers between devices with their start and end apart: 7, of which 3 were waited for; matrix products, arithmetic and copies ran while one was open for 0% of the time, Pallas kernels for 11%

profile of v4, /device:TPU:576, one launch (start us, length us, event | category | flops | bytes accessed | tf_op | source)
XLA Modules:
  0.0 60.4 jit_solution(14272433713265873440)
XLA Ops:
  0.6 1.2 %shard_map.59 = (f32[45,8,128]{2,1,0:T(8,128)S(1)}, f32[23,8,128]{2,1,0:T(8,128)S(1)}, f32[23,8,128]{2,1,0:T(8,128)S(1)}, f32[14,8,128]{2,1,0:T(8,128)S(1)}) custom-call(f32[3,32,256]{2,1,0:T(8,128)} %ocean_ref.1, f32[19,1,8,256]{3,2,1,0:T(8,128)} %tr_ref.1, s32[4,32]{1,0:T(4,128)} %bitcast.6, f32[14]{0:T(128)} %stoich_ref.1), custom_call_target="tpu_custom_call" | custom-call | tf_op jit(solution)/shard_map/pallas_call | solution.py:567
  1.9 2.3 %collective-permute-start = (f32[45,8,128]{2,1,0:T(8,128)S(1)}, f32[45,8,128]{2,1,0:T(8,128)S(1)}, u32[]{:S(2)}, u32[]{:S(2)}) collective-permute-start(f32[45,8,128]{2,1,0:T(8,128)S(1)} %get-tuple-element.17.own_ref), channel_id=1, source_target_pairs={{1,2},{2,1},{3,4},{4,3},{5,6},{6,5},{7,8},{8,7},{9,10},{10,9},{11,... | collective-permute-start | bytes 552968 | tf_op jit(solution)/shard_map/ppermute | solution.py:573
  4.1 3.2 %collective-permute-start.1 = (f32[45,8,128]{2,1,0:T(8,128)S(1)}, f32[45,8,128]{2,1,0:T(8,128)S(1)}, u32[]{:S(2)}, u32[]{:S(2)}) collective-permute-start(f32[45,8,128]{2,1,0:T(8,128)S(1)} %get-tuple-element.17.own_ref), channel_id=1, source_target_pairs={{0,1},{1,0},{2,3},{3,2},{4,5},{5,4},{6,7},{7,6},{8,9},{9,8},{10,11... | collective-permute-start | bytes 552968 | tf_op jit(solution)/shard_map/ppermute | solution.py:574
  7.3 5.4 %collective-permute-start.2 = (f32[23,8,128]{2,1,0:T(8,128)S(1)}, f32[23,8,128]{2,1,0:T(8,128)S(1)}, u32[]{:S(2)}, u32[]{:S(2)}) collective-permute-start(f32[23,8,128]{2,1,0:T(8,128)S(1)} %get-tuple-element.18), channel_id=1, source_target_pairs={{256,0},{512,256},{768,512},{32,768},{288,32},{544,288},{800,544},... | collective-permute-start | bytes 282632 | tf_op jit(solution)/shard_map/ppermute | solution.py:575
  12.7 1.9 %collective-permute-start.3 = (f32[23,8,128]{2,1,0:T(8,128)S(1)}, f32[23,8,128]{2,1,0:T(8,128)S(1)}, u32[]{:S(2)}, u32[]{:S(2)}) collective-permute-start(f32[23,8,128]{2,1,0:T(8,128)S(1)} %get-tuple-element.19), channel_id=1, source_target_pairs={{0,256},{256,512},{512,768},{768,32},{32,288},{288,544},{544,800},... | collective-permute-start | bytes 282632 | tf_op jit(solution)/shard_map/ppermute | solution.py:576
  14.6 7.0 %collective-permute-done.eo_ref = f32[45,8,128]{2,1,0:T(8,128)S(1)} collective-permute-done((f32[45,8,128]{2,1,0:T(8,128)S(1)}, f32[45,8,128]{2,1,0:T(8,128)S(1)}, u32[]{:S(2)}, u32[]{:S(2)}) %collective-permute-start) | collective-permute-done | bytes 184352 | tf_op jit(solution)/shard_map/ppermute | solution.py:573
  21.6 0.0 collective-permute-done.1.ee_ref
  21.6 0.2 shard_map.61
  21.8 17.6 %collective-permute-start.4 = (f32[12,8,128]{2,1,0:T(8,128)S(1)}, f32[12,8,128]{2,1,0:T(8,128)S(1)}, u32[]{:S(2)}, u32[]{:S(2)}) collective-permute-start(f32[12,8,128]{2,1,0:T(8,128)S(1)} %get-tuple-element.24), channel_id=1, source_target_pairs={{256,0},{512,256},{768,512},{32,768},{288,32},{544,288},{800,544},... | collective-permute-start | bytes 147464 | tf_op jit(solution)/shard_map/ppermute | solution.py:581
  39.3 1.9 %collective-permute-start.5 = (f32[12,8,128]{2,1,0:T(8,128)S(1)}, f32[12,8,128]{2,1,0:T(8,128)S(1)}, u32[]{:S(2)}, u32[]{:S(2)}) collective-permute-start(f32[12,8,128]{2,1,0:T(8,128)S(1)} %get-tuple-element.25), channel_id=1, source_target_pairs={{0,256},{256,512},{512,768},{768,32},{32,288},{288,544},{544,800},... | collective-permute-start | bytes 147464 | tf_op jit(solution)/shard_map/ppermute | solution.py:582
  41.3 0.0 collective-permute-done.2.below_ref
  41.3 0.0 collective-permute-done.3.above_ref
  41.3 3.2 %shard_map.60 = (f32[23,4,8,128]{3,2,1,0:T(8,128)S(1)}, f32[19,4,8,128]{3,2,1,0:T(8,128)S(1)}, f32[19,2,8,128]{3,2,1,0:T(8,128)S(1)}, f32[32,8,128]{2,1,0:T(8,128)S(1)}) custom-call(f32[45,8,128]{2,1,0:T(8,128)S(1)} %get-tuple-element.17.own_ref, f32[45,8,128]{2,1,0:T(8,128)S(1)} %collective-permute-done.eo_ref, ...), custom_call_target="tpu_custom_call" | custom-call | tf_op jit(solution)/shard_map/pallas_call | solution.py:583
  44.4 0.0 collective-permute-done.4.below_ref
  44.4 3.0 %collective-permute-done.5.above_ref = f32[12,8,128]{2,1,0:T(8,128)S(1)} collective-permute-done((f32[12,8,128]{2,1,0:T(8,128)S(1)}, f32[12,8,128]{2,1,0:T(8,128)S(1)}, u32[]{:S(2)}, u32[]{:S(2)}) %collective-permute-start.5) | collective-permute-done | bytes 49184 | tf_op jit(solution)/shard_map/ppermute | solution.py:582
  47.4 3.2 %shard_map.62 = (f32[4,3,8,256]{3,2,1,0:T(8,128)}, f32[19,4,8,128]{3,2,1,0:T(8,128)S(1)}, f32[4,8,128]{2,1,0:T(8,128)S(1)}, f32[4,8,128]{2,1,0:T(8,128)S(1)}, f32[2,8,128]{2,1,0:T(8,128)S(1)}) custom-call(f32[23,4,8,128]{3,2,1,0:T(8,128)S(1)} %get-tuple-element.21.raw_ref, f32[19,4,8,128]{3,2,1,0:T(8,128)S(1)} %get-tuple-element.22.part_ref, ...), custom_call_target="tpu_custom_call" | custom-call | tf_op jit(solution)/shard_map/pallas_call | solution.py:595
  50.7 3.3 %all-to-all-start = ((f32[4,3,8,256]{3,2,1,0:T(8,128)}), f32[4,3,8,256]{3,2,1,0:T(8,128)S(1)}, u32[]{:S(2)}, u32[]{:S(2)}) async-start(f32[4,3,8,256]{3,2,1,0:T(8,128)} %get-tuple-element.26), calls=%async_computation | async-start | bytes 196608 | tf_op jit(solution)/shard_map/all_to_all | solution.py:601
  54.0 3.5 %shard_map.63 = f32[19,1,8,256]{3,2,1,0:T(8,128)} custom-call(f32[19,2,8,128]{3,2,1,0:T(8,128)S(1)} %get-tuple-element.27.q1_ref, f32[32,8,128]{2,1,0:T(8,128)S(1)} %get-tuple-element.23.aux_ref, f32[19,4,8,128]{3,2,1,0:T(8,128)S(1)} %get-tuple-element.28.q_ref, f32[4,8,128]{2,1,0:T(8,128)S(1)} %get-tuple-element.29.c2_ref, ...), custom_call_target="tpu_custom_call" | custom-call | tf_op jit(solution)/shard_map/pallas_call | solution.py:602
  57.5 2.2 %all-to-all-done = f32[4,3,8,256]{3,2,1,0:T(8,128)S(1)} async-done(((f32[4,3,8,256]{3,2,1,0:T(8,128)}), f32[4,3,8,256]{3,2,1,0:T(8,128)S(1)}, u32[]{:S(2)}, u32[]{:S(2)}) %all-to-all-start) | async-done | bytes 98336 | tf_op jit(solution)/shard_map/all_to_all | solution.py:601
  59.7 0.6 %copy_bitcast_fusion = f32[3,32,256]{2,1,0:T(8,128)} fusion(f32[4,3,8,256]{3,2,1,0:T(8,128)S(1)} %all-to-all-done), kind=kLoop, calls=%fused_computation | loop fusion | bytes 196608 | tf_op jit(solution)/shard_map/reshape | solution.py:605
Async XLA Ops:
  1.9 19.8 %collective-permute-start = (f32[45,8,128]{2,1,0:T(8,128)S(1)}, f32[45,8,128]{2,1,0:T(8,128)S(1)}, u32[]{:S(2)}, u32[]{:S(2)}) collective-permute-start(f32[45,8,128]{2,1,0:T(8,128)S(1)} %get-tuple-element.17.own_ref), channel_id=1, source_target_pairs={{1,2},{2,1},{3,4},{4,3},{5,6},{6,5},{7,8},{8,7},{9,10},{10,9},{11,... | collective-permute-start | bytes 552968 | tf_op jit(solution)/shard_map/ppermute | solution.py:573
  4.1 17.5 %collective-permute-start.1 = (f32[45,8,128]{2,1,0:T(8,128)S(1)}, f32[45,8,128]{2,1,0:T(8,128)S(1)}, u32[]{:S(2)}, u32[]{:S(2)}) collective-permute-start(f32[45,8,128]{2,1,0:T(8,128)S(1)} %get-tuple-element.17.own_ref), channel_id=1, source_target_pairs={{0,1},{1,0},{2,3},{3,2},{4,5},{5,4},{6,7},{7,6},{8,9},{9,8},{10,11... | collective-permute-start | bytes 552968 | tf_op jit(solution)/shard_map/ppermute | solution.py:574
  7.3 34.0 %collective-permute-start.2 = (f32[23,8,128]{2,1,0:T(8,128)S(1)}, f32[23,8,128]{2,1,0:T(8,128)S(1)}, u32[]{:S(2)}, u32[]{:S(2)}) collective-permute-start(f32[23,8,128]{2,1,0:T(8,128)S(1)} %get-tuple-element.18), channel_id=1, source_target_pairs={{256,0},{512,256},{768,512},{32,768},{288,32},{544,288},{800,544},... | collective-permute-start | bytes 282632 | tf_op jit(solution)/shard_map/ppermute | solution.py:575
  12.7 28.6 %collective-permute-start.3 = (f32[23,8,128]{2,1,0:T(8,128)S(1)}, f32[23,8,128]{2,1,0:T(8,128)S(1)}, u32[]{:S(2)}, u32[]{:S(2)}) collective-permute-start(f32[23,8,128]{2,1,0:T(8,128)S(1)} %get-tuple-element.19), channel_id=1, source_target_pairs={{0,256},{256,512},{512,768},{768,32},{32,288},{288,544},{544,800},... | collective-permute-start | bytes 282632 | tf_op jit(solution)/shard_map/ppermute | solution.py:576
  21.8 22.7 %collective-permute-start.4 = (f32[12,8,128]{2,1,0:T(8,128)S(1)}, f32[12,8,128]{2,1,0:T(8,128)S(1)}, u32[]{:S(2)}, u32[]{:S(2)}) collective-permute-start(f32[12,8,128]{2,1,0:T(8,128)S(1)} %get-tuple-element.24), channel_id=1, source_target_pairs={{256,0},{512,256},{768,512},{32,768},{288,32},{544,288},{800,544},... | collective-permute-start | bytes 147464 | tf_op jit(solution)/shard_map/ppermute | solution.py:581
  39.3 8.1 %collective-permute-start.5 = (f32[12,8,128]{2,1,0:T(8,128)S(1)}, f32[12,8,128]{2,1,0:T(8,128)S(1)}, u32[]{:S(2)}, u32[]{:S(2)}) collective-permute-start(f32[12,8,128]{2,1,0:T(8,128)S(1)} %get-tuple-element.25), channel_id=1, source_target_pairs={{0,256},{256,512},{512,768},{768,32},{32,288},{288,544},{544,800},... | collective-permute-start | bytes 147464 | tf_op jit(solution)/shard_map/ppermute | solution.py:582
  50.7 9.1 %all-to-all-start = ((f32[4,3,8,256]{3,2,1,0:T(8,128)}), f32[4,3,8,256]{3,2,1,0:T(8,128)S(1)}, u32[]{:S(2)}, u32[]{:S(2)}) async-start(f32[4,3,8,256]{3,2,1,0:T(8,128)} %get-tuple-element.26), calls=%async_computation | async-start | bytes 196608 | tf_op jit(solution)/shard_map/all_to_all | solution.py:601

commit v5 on v4

--- a/solution.py
+++ b/solution.py
@@ -221,31 +221,17 @@
     ]
 
 
-def unstrip(below, above):
-    first = subs() < 4
-    return [
-        jnp.where(first, below, above),
-        pltpu.roll(jnp.where(first, above, below), 4, 0),
-    ]
-
-
-def pack_kernel(ocean_ref, tr_ref, bot_ref, stoich_ref, out_ref, up_ref, down_ref, yield_ref):
+def middle():
+    return (subs() >= 2) & (subs() < 6)
+
+
+def pack_kernel(
+    ocean_ref, tr_ref, bot_ref, stoich_ref, out_ref, first_ref, rest_ref, yield_ref
+):
     for j in range(NTR - 5):
         yield_ref[j] = jnp.full(TILE, stoich_ref[j], jnp.float32)
     start = pl.multiple_of(lax.axis_index("comp") * ROWS, ROWS)
     rows = pl.ds(start, ROWS)
-
-    def strip(f, a, b):
-        a, b = mix(a, half_turn(b)), pltpu.roll(mix(half_turn(a), b), 4, 0)
-        up_ref[f] = jnp.where(subs() < 4, a, b)
-        down_ref[f] = jnp.where(subs() < 4, b, a)
-
-    for f in range(FIELDS):
-        x = tr_ref[f, 0] if f < NTR else ocean_ref[f - NTR, rows, :]
-        a, b = x[:, :128], x[:, 128:]
-        out_ref[2 * f] = a
-        out_ref[2 * f + 1] = b
-        strip(f, a, b)
     band = bot_ref.shape[1]
     row = lax.broadcasted_iota(jnp.int32, (ROWS, band), 0) + start
     pick = row == lax.broadcasted_iota(jnp.int32, (ROWS, band), 1)
@@ -256,40 +242,63 @@
             lanes() == c, jnp.sum(jnp.where(pick, line, 0.0), axis=1, keepdims=True), depth
         )
     out_ref[2 * FIELDS] = depth
-    strip(WET, *wet_tiles(depth))
-
-
-def sides(own_ref, eo_ref, ee_ref, t):
+    rest_ref[PAIRS + FIELDS] = depth
     flip = odd("tx")
-    a, b = eo_ref[t], ee_ref[t]
-    return jnp.where(flip, b, a), own_ref[t], jnp.where(flip, a, b)
-
-
-def corner_kernel(own_ref, eo_ref, ee_ref, up_ref, down_ref):
+    wet = wet_tiles(depth)
+
+    def near_tile(f):
+        if f < 0:
+            return jnp.zeros(TILE, jnp.float32)
+        if f == WET:
+            return jnp.where(flip, wet[1], wet[0])
+        x = tr_ref[f, 0] if f < NTR else ocean_ref[f - NTR, rows, :]
+        a, b = x[:, :128], x[:, 128:]
+        out_ref[2 * f] = a
+        out_ref[2 * f + 1] = b
+        rest_ref[PAIRS + f] = jnp.where(flip, a, b)
+        return jnp.where(flip, b, a)
+
+    for k in range(PAIRS):
+        x, y = near_tile(2 * k - 1), pltpu.roll(near_tile(2 * k), 4, 0)
+        first_ref[k] = jnp.where(middle(), y, x)
+        rest_ref[k] = jnp.where(middle(), x, y)
+
+
+def row_kernel(own_ref, chip_ref, ca_ref, cb_ref, up_ref, down_ref, first_ref):
+    flip = odd("tx")
     sub = subs()
-    west, _, east = sides(own_ref, eo_ref, ee_ref, 2 * FIELDS)
-    wet = wet_tiles(west)[1], wet_tiles(east)[0]
-
-    def edge(f):
+    upper = sub < 4
+
+    def strip(f, a, b):
+        a, b = mix(a, half_turn(b)), pltpu.roll(mix(half_turn(a), b), 4, 0)
+        up_ref[f] = jnp.where(upper, a, b)
+        down_ref[f] = jnp.where(upper, b, a)
+
+    for f in range(FIELDS):
+        strip(f, own_ref[2 * f], own_ref[2 * f + 1])
+    strip(WET, *wet_tiles(own_ref[2 * FIELDS]))
+    wet = wet_tiles(chip_ref[2 * FIELDS])
+
+    def edge(f, far):
         if f < 0:
-            return [jnp.zeros(TILE, jnp.float32)] * 2
-        if f == WET:
-            w, e = wet
-        else:
-            w = sides(own_ref, eo_ref, ee_ref, 2 * f + 1)[0]
-            e = sides(own_ref, eo_ref, ee_ref, 2 * f)[2]
+            return [far, far]
+        west, east = wet if f == WET else (chip_ref[2 * f], chip_ref[2 * f + 1])
+        w = jnp.where(flip, east, far)
+        e = jnp.where(flip, far, west)
         return [mix(w, half_turn(e)), mix(half_turn(w), e)]
 
     for k in range(PAIRS):
-        a, b, c, d = edge(2 * k - 1) + edge(2 * k)
+        far = ca_ref[k] + cb_ref[k]
+        first_ref[k] = far
+        a, b, c, d = edge(2 * k - 1, far) + edge(2 * k, pltpu.roll(far, 4, 0))
         turned = pltpu.roll(c, 4, 0)
-        up_ref[k] = jnp.where(
-            sub < 4,
+        up_ref[WET + 1 + k] = jnp.where(
+            upper,
             jnp.where(sub < 2, a, pltpu.roll(b, 2, 0)),
             jnp.where(sub < 6, turned, pltpu.roll(d, 6, 0)),
         )
-        down_ref[k] = jnp.where(
-            sub < 4,
+        down_ref[WET + 1 + k] = jnp.where(
+            upper,
             jnp.where(sub < 2, pltpu.roll(d, 2, 0), turned),
             jnp.where(sub < 6, pltpu.roll(b, 6, 0), a),
         )
@@ -307,9 +316,18 @@
 
 
 def own_kernel(
-    own_ref, eo_ref, ee_ref, below_ref, above_ref, stoich_ref, raw_ref, part_ref, q1_ref,
-    aux_ref, fc_ref, fr_ref, g_ref,
+    own_ref, chip_ref, first_ref, ra_ref, rb_ref, te_ref, to_ref, stoich_ref, raw_ref, part_ref,
+    q1_ref, aux_ref, near_ref, fc_ref, fr_ref, g_ref,
 ):
+    flip = odd("tx")
+    even = jnp.logical_not(odd("comp"))
+    mid = middle()
+    for k in range(PAIRS):
+        c, r = first_ref[k], ra_ref[k] + rb_ref[k]
+        if k:
+            near_ref[2 * k - 1] = jnp.where(mid, r, c)
+        near_ref[2 * k] = pltpu.roll(jnp.where(mid, c, r), 4, 0)
+
     def arrange(a, b):
         pairs = ((a[0], b[1]), (b[0], a[2]), (a[1], b[2]))
         out = []
@@ -317,15 +335,28 @@
             out += [mix(low, half_turn(high)), mix(half_turn(low), high)]
         return out
 
+    def blocks(f):
+        n, d = near_ref[f], ra_ref[PAIRS + f] + rb_ref[PAIRS + f]
+        c0, c1 = chip_ref[2 * f], chip_ref[2 * f + 1]
+        west = jnp.where(flip, c0, d), jnp.where(flip, c1, n)
+        east = jnp.where(flip, n, c0), jnp.where(flip, d, c1)
+        return west, (own_ref[2 * f], own_ref[2 * f + 1]), east
+
     def wide(f):
-        return arrange(*[sides(own_ref, eo_ref, ee_ref, 2 * f + i) for i in range(2)])
+        return arrange(*zip(*blocks(f)))
 
     def halo(f):
-        return unstrip(below_ref[f], above_ref[f])
+        first = (subs() < 4) == even
+        te, to = te_ref[f], to_ref[f]
+        return [jnp.where(first, te, to), pltpu.roll(jnp.where(first, to, te), 4, 0)]
 
     u_w, v_w, t_w = [wide(f) for f in (U, V, T)]
-    depth = sides(own_ref, eo_ref, ee_ref, 2 * FIELDS)
-    w_w = arrange(*zip(*[wet_tiles(x) for x in depth]))
+    far = wet_tiles(ra_ref[PAIRS + FIELDS] + rb_ref[PAIRS + FIELDS])
+    close = wet_tiles(chip_ref[2 * FIELDS])
+    own = wet_tiles(own_ref[2 * FIELDS])
+    west = [jnp.where(flip, c, d) for c, d in zip(close, far)]
+    east = [jnp.where(flip, d, c) for c, d in zip(close, far)]
+    w_w = arrange(*zip(west, own, east))
     u_h, v_h, t_h, w_h = [halo(f) for f in (U, V, T, WET)]
     u_s, v_s, t_s, w_s = [own_of(x) for x in (u_w, v_w, t_w, w_w)]
     w_e = edge_of(w_w)
@@ -390,13 +421,15 @@
 
 
 def edge_kernel(
-    raw_ref, part_ref, aux_ref, below_ref, above_ref, stoich_ref, ocean_ref, q_ref, c2_ref,
+    raw_ref, part_ref, aux_ref, te_ref, to_ref, stoich_ref, ocean_ref, q_ref, c2_ref,
     r2_ref, t2_ref, fc_ref, fr_ref, g_ref,
 ):
     sub4 = subs() < 4
+    swapped = odd("comp")
 
     def corners(k):
-        b, a = below_ref[k], above_ref[k]
+        te, to = te_ref[WET + 1 + k], to_ref[WET + 1 + k]
+        b, a = jnp.where(swapped, to, te), jnp.where(swapped, te, to)
         return (
             [
                 jnp.where(sub4, b, a),
@@ -535,6 +568,25 @@
     return pairs
 
 
+def far_pairs(bands, tiles):
+    group = 8
+    length = bands * (tiles // group)
+
+    def steps(tx, ty):
+        z = tx // group * bands + ty
+        return min(z, length - z)
+
+    later, sooner = [], []
+    for ty in range(bands):
+        for a in range(1, tiles - 1, 2):
+            pair = (ty * tiles + a, ty * tiles + a + 1)
+            if steps(a, ty) < steps(a + 1, ty):
+                pair = pair[::-1]
+            later.append(pair)
+            sooner.append(pair[::-1])
+    return later, sooner
+
+
 def shards(ocean, tracers, bottom, stoich):
     comps = lax.axis_size("comp")
     bands = lax.axis_size("ty")
@@ -552,8 +604,6 @@
 
     axes = ("comp", "ty")
     count = comps * bands
-    ups = [(place(r), place(r - 1)) for r in range(1, count)]
-    downs = [(b, a) for a, b in ups]
 
     def kernel(body, outs, ins, scratch=(), scalars=False):
         return pl.pallas_call(
@@ -564,22 +614,26 @@
             scratch_shapes=[VMEM((*n, *TILE), jnp.float32) for n in scratch],
         )
 
-    packed, strip_up, strip_down, yields = kernel(
+    packed, first, rest, yields = kernel(
         pack_kernel,
-        [arr(n, *TILE) for n in (2 * FIELDS + 1, FIELDS + 1, FIELDS + 1, NTR - 5)],
+        [arr(n, *TILE) for n in (2 * FIELDS + 1, PAIRS, PAIRS + FIELDS + 1, NTR - 5)],
         3,
         scalars=True,
     )(ocean, tracers, bottom.T, stoich)
-    from_odd = lax.ppermute(packed, "tx", swaps(tiles, 1))
-    from_even = lax.ppermute(packed, "tx", swaps(tiles, 0))
-    below = lax.ppermute(strip_up, axes, ups)
-    above = lax.ppermute(strip_down, axes, downs)
-    blocks = near(packed, from_odd, from_even)
-    corner_up, corner_down = kernel(
-        corner_kernel, [arr(PAIRS, *TILE), arr(PAIRS, *TILE)], 3
-    )(*blocks)
-    corner_below = lax.ppermute(corner_up, axes, ups)
-    corner_above = lax.ppermute(corner_down, axes, downs)
+    later, sooner = far_pairs(bands, tiles)
+
+    grid = ("ty", "tx")
+    first_a = lax.ppermute(first, grid, later)
+    rest_a = lax.ppermute(rest, grid, later)
+    first_b = lax.ppermute(first, grid, sooner)
+    rest_b = lax.ppermute(rest, grid, sooner)
+    chip = lax.ppermute(packed, "tx", swaps(tiles, 0))
+    up, down, first = kernel(
+        row_kernel, [arr(n, *TILE) for n in (WET + 1 + PAIRS, WET + 1 + PAIRS, PAIRS)], 4
+    )(*near(packed, chip, first_a, first_b))
+    is_odd = odd("comp")
+    to = lax.ppermute(jnp.where(is_odd, down, up), axes, swaps(count, 1, place))
+    te = lax.ppermute(jnp.where(is_odd, up, down), axes, swaps(count, 0, place))
     state = kernel(
         own_kernel,
         [
@@ -588,16 +642,16 @@
             arr(NTR, 2, *TILE),
             arr(2 * len(AUX), *TILE),
         ],
-        6,
-        [(6,), (4,), (4,)],
-    )(*blocks, *near(below, above, yields))
+        8,
+        [(FIELDS + 1,), (6,), (4,), (4,)],
+    )(*near(packed, chip, first, rest_a, rest_b, te, to, yields))
     raw, part, q1_own, aux = near(*state)
     rows, *rest = kernel(
         edge_kernel,
         [arr(comps, 3, ROWS, 256), arr(NTR, 4, *TILE)] + [arr(n, *TILE) for n in (4, 4, 2)],
         6,
         [(4,), (4,), (8,)],
-    )(raw, part, aux, *near(corner_below, corner_above, yields))
+    )(raw, part, aux, *near(te, to, yields))
     gathered = lax.all_to_all(rows, "comp", 0, 0, tiled=True)
     (tracers_out,) = kernel(
         last_kernel, [jax.ShapeDtypeStruct((NTR, 1, ROWS, 256), jnp.float32)], 7, [(4,)]

time: 60.7 us -> 76 us (1.25)
  the two profiles are of different devices: /device:TPU:576 before, /device:TPU:864 now
where the time goes in v5:
time: 76 us; the launch traced here: 75.7 us
  starting transfers between devices  41.8 us (55%)
  waiting for transfers between devices  21.2 us (28%)
  Pallas kernels  11.3 us (15%)
    ppermute x1, waiting for transfers between devices, shards(): rest_a = lax.ppermute(rest, grid, later)  17.2 us
    ppermute x1, starting transfers between devices, shards(): rest_b = lax.ppermute(rest, grid, sooner)  15.1 us
    ppermute x1, starting transfers between devices, shards(): first_b = lax.ppermute(first, grid, sooner)  10.7 us
    ppermute x1, starting transfers between devices, shards(): to = lax.ppermute(jnp.where(is_odd, down, up), axes, swaps(count, 1, place))  4.78 us
    all_to_all x1, starting transfers between devices, shards(): gathered = lax.all_to_all(rows, 'comp', 0, 0, tiled=True)  4.46 us
    pallas_call x1, Pallas kernels, shards(): kernel(last_kernel, [jax.ShapeDtypeStruct((NTR, 1, ROWS, 256), jnp.float3...  3.53 us
    pallas_call x1, Pallas kernels, shards(): kernel(edge_kernel, [arr(comps, 3, ROWS, 256), arr(NTR, 4, *TILE)] + [arr...  3.25 us
    pallas_call x1, Pallas kernels, shards(): kernel(own_kernel, [arr(FIELDS + 1, 4, *TILE), arr(NTR, 4, *TILE), arr(NT...  3.17 us
  transfers between devices with their start and end apart: 8, of which 3 were waited for; matrix products, arithmetic and copies ran while one was open for 0% of the time, Pallas kernels for 5%

profile of v5, /device:TPU:864, one launch (start us, length us, event | category | flops | bytes accessed | tf_op | source)
XLA Modules:
  0.0 75.7 jit_solution(10980597918190498002)
XLA Ops:
  0.6 1.1 %shard_map.59 = (f32[45,8,128]{2,1,0:T(8,128)S(1)}, f32[12,8,128]{2,1,0:T(8,128)S(1)}, f32[35,8,128]{2,1,0:T(8,128)S(1)}, f32[14,8,128]{2,1,0:T(8,128)S(1)}) custom-call(f32[3,32,256]{2,1,0:T(8,128)} %ocean_ref.1, f32[19,1,8,256]{3,2,1,0:T(8,128)} %tr_ref.1, s32[4,32]{1,0:T(4,128)} %bitcast.6, f32[14]{0:T(128)} %stoich_ref.1), custom_call_target="tpu_custom_call" | custom-call | tf_op jit(solution)/shard_map/pallas_call | solution.py:617
  1.8 1.9 %collective-permute-start = (f32[45,8,128]{2,1,0:T(8,128)S(1)}, f32[45,8,128]{2,1,0:T(8,128)S(1)}, u32[]{:S(2)}, u32[]{:S(2)}) collective-permute-start(f32[45,8,128]{2,1,0:T(8,128)S(1)} %get-tuple-element.18.own_ref), channel_id=1, source_target_pairs={{0,1},{1,0},{2,3},{3,2},{4,5},{5,4},{6,7},{7,6},{8,9},{9,8},{10,11... | collective-permute-start | bytes 552968 | tf_op jit(solution)/shard_map/ppermute | solution.py:630
  3.7 10.7 %collective-permute-start.2 = (f32[12,8,128]{2,1,0:T(8,128)S(1)}, f32[12,8,128]{2,1,0:T(8,128)S(1)}, u32[]{:S(2)}, u32[]{:S(2)}) collective-permute-start(f32[12,8,128]{2,1,0:T(8,128)S(1)} %get-tuple-element.19), channel_id=1, source_target_pairs={{2,1},{4,3},{6,5},{7,8},{10,9},{12,11},{14,13},{15,16},{18,17},{20... | collective-permute-start | bytes 147464 | tf_op jit(solution)/shard_map/ppermute | solution.py:628
  14.4 1.3 %collective-permute-start.1 = (f32[12,8,128]{2,1,0:T(8,128)S(1)}, f32[12,8,128]{2,1,0:T(8,128)S(1)}, u32[]{:S(2)}, u32[]{:S(2)}) collective-permute-start(f32[12,8,128]{2,1,0:T(8,128)S(1)} %get-tuple-element.19), channel_id=1, source_target_pairs={{1,2},{3,4},{5,6},{8,7},{9,10},{11,12},{13,14},{16,15},{17,18},{19... | collective-permute-start | bytes 147464 | tf_op jit(solution)/shard_map/ppermute | solution.py:626
  15.7 15.1 %collective-permute-start.4 = (f32[35,8,128]{2,1,0:T(8,128)S(1)}, f32[35,8,128]{2,1,0:T(8,128)S(1)}, u32[]{:S(2)}, u32[]{:S(2)}) collective-permute-start(f32[35,8,128]{2,1,0:T(8,128)S(1)} %get-tuple-element.21), channel_id=1, source_target_pairs={{2,1},{4,3},{6,5},{7,8},{10,9},{12,11},{14,13},{15,16},{18,17},{20... | collective-permute-start | bytes 430088 | tf_op jit(solution)/shard_map/ppermute | solution.py:629
  30.9 1.3 %collective-permute-start.3 = (f32[35,8,128]{2,1,0:T(8,128)S(1)}, f32[35,8,128]{2,1,0:T(8,128)S(1)}, u32[]{:S(2)}, u32[]{:S(2)}) collective-permute-start(f32[35,8,128]{2,1,0:T(8,128)S(1)} %get-tuple-element.21), channel_id=1, source_target_pairs={{1,2},{3,4},{5,6},{8,7},{9,10},{11,12},{13,14},{16,15},{17,18},{19... | collective-permute-start | bytes 430088 | tf_op jit(solution)/shard_map/ppermute | solution.py:627
  32.2 0.0 collective-permute-done.2.cb_ref
  32.2 1.7 %collective-permute-done.1.ca_ref = f32[12,8,128]{2,1,0:T(8,128)S(1)} collective-permute-done((f32[12,8,128]{2,1,0:T(8,128)S(1)}, f32[12,8,128]{2,1,0:T(8,128)S(1)}, u32[]{:S(2)}, u32[]{:S(2)}) %collective-permute-start.1) | collective-permute-done | bytes 49184 | tf_op jit(solution)/shard_map/ppermute | solution.py:626
  33.9 0.0 collective-permute-done.chip_ref
  33.9 0.2 shard_map.60
  34.2 4.8 %collective-permute-start.6 = (f32[35,8,128]{2,1,0:T(8,128)S(1)}, f32[35,8,128]{2,1,0:T(8,128)S(1)}, u32[]{:S(2)}, u32[]{:S(2)}) collective-permute-start(f32[35,8,128]{2,1,0:T(8,128)S(1)} %get-tuple-element.34), channel_id=1, source_target_pairs={{256,512},{512,256},{768,32},{32,768},{288,544},{544,288},{800,64}... | collective-permute-start | bytes 430088 | tf_op jit(solution)/shard_map/ppermute | solution.py:635
  39.0 2.2 %collective-permute-start.5 = (f32[35,8,128]{2,1,0:T(8,128)S(1)}, f32[35,8,128]{2,1,0:T(8,128)S(1)}, u32[]{:S(2)}, u32[]{:S(2)}) collective-permute-start(f32[35,8,128]{2,1,0:T(8,128)S(1)} %get-tuple-element.35), channel_id=1, source_target_pairs={{0,256},{256,0},{512,768},{768,512},{32,288},{288,32},{544,800},{8... | collective-permute-start | bytes 430088 | tf_op jit(solution)/shard_map/ppermute | solution.py:636
  41.1 0.0 collective-permute-done.4.rb_ref
  41.2 17.2 %collective-permute-done.3.ra_ref = f32[35,8,128]{2,1,0:T(8,128)S(1)} collective-permute-done((f32[35,8,128]{2,1,0:T(8,128)S(1)}, f32[35,8,128]{2,1,0:T(8,128)S(1)}, u32[]{:S(2)}, u32[]{:S(2)}) %collective-permute-start.3) | collective-permute-done | bytes 143392 | tf_op jit(solution)/shard_map/ppermute | solution.py:627
  58.4 0.0 collective-permute-done.6.to_ref
  58.4 0.0 collective-permute-done.5.te_ref
  58.4 3.2 %shard_map.61 = (f32[23,4,8,128]{3,2,1,0:T(8,128)S(1)}, f32[19,4,8,128]{3,2,1,0:T(8,128)S(1)}, f32[19,2,8,128]{3,2,1,0:T(8,128)S(1)}, f32[32,8,128]{2,1,0:T(8,128)S(1)}) custom-call(f32[45,8,128]{2,1,0:T(8,128)S(1)} %get-tuple-element.18.own_ref, f32[45,8,128]{2,1,0:T(8,128)S(1)} %collective-permute-done.chip_ref, ...), custom_call_target="tpu_custom_call" | custom-call | tf_op jit(solution)/shard_map/pallas_call | solution.py:637
  61.5 3.2 %shard_map.62 = (f32[4,3,8,256]{3,2,1,0:T(8,128)}, f32[19,4,8,128]{3,2,1,0:T(8,128)S(1)}, f32[4,8,128]{2,1,0:T(8,128)S(1)}, f32[4,8,128]{2,1,0:T(8,128)S(1)}, f32[2,8,128]{2,1,0:T(8,128)S(1)}) custom-call(f32[23,4,8,128]{3,2,1,0:T(8,128)S(1)} %get-tuple-element.25.raw_ref, f32[19,4,8,128]{3,2,1,0:T(8,128)S(1)} %get-tuple-element.26.part_ref, ...), custom_call_target="tpu_custom_call" | custom-call | tf_op jit(solution)/shard_map/pallas_call | solution.py:649
  64.8 4.5 %all-to-all-start = ((f32[4,3,8,256]{3,2,1,0:T(8,128)}), f32[4,3,8,256]{3,2,1,0:T(8,128)S(1)}, u32[]{:S(2)}, u32[]{:S(2)}) async-start(f32[4,3,8,256]{3,2,1,0:T(8,128)} %get-tuple-element.28), calls=%async_computation | async-start | bytes 196608 | tf_op jit(solution)/shard_map/all_to_all | solution.py:655
  69.3 3.5 %shard_map.63 = f32[19,1,8,256]{3,2,1,0:T(8,128)} custom-call(f32[19,2,8,128]{3,2,1,0:T(8,128)S(1)} %get-tuple-element.29.q1_ref, f32[32,8,128]{2,1,0:T(8,128)S(1)} %get-tuple-element.27.aux_ref, f32[19,4,8,128]{3,2,1,0:T(8,128)S(1)} %get-tuple-element.30.q_ref, f32[4,8,128]{2,1,0:T(8,128)S(1)} %get-tuple-element.31.c2_ref, ...), custom_call_target="tpu_custom_call" | custom-call | tf_op jit(solution)/shard_map/pallas_call | solution.py:656
  72.8 2.3 %all-to-all-done = f32[4,3,8,256]{3,2,1,0:T(8,128)S(1)} async-done(((f32[4,3,8,256]{3,2,1,0:T(8,128)}), f32[4,3,8,256]{3,2,1,0:T(8,128)S(1)}, u32[]{:S(2)}, u32[]{:S(2)}) %all-to-all-start) | async-done | bytes 98336 | tf_op jit(solution)/shard_map/all_to_all | solution.py:655
  75.1 0.6 copy_bitcast_fusion
  (1 shorter events, 0.0 us)
Async XLA Ops:
  1.8 32.1 %collective-permute-start = (f32[45,8,128]{2,1,0:T(8,128)S(1)}, f32[45,8,128]{2,1,0:T(8,128)S(1)}, u32[]{:S(2)}, u32[]{:S(2)}) collective-permute-start(f32[45,8,128]{2,1,0:T(8,128)S(1)} %get-tuple-element.18.own_ref), channel_id=1, source_target_pairs={{0,1},{1,0},{2,3},{3,2},{4,5},{5,4},{6,7},{7,6},{8,9},{9,8},{10,11... | collective-permute-start | bytes 552968 | tf_op jit(solution)/shard_map/ppermute | solution.py:630
  3.7 28.5 %collective-permute-start.2 = (f32[12,8,128]{2,1,0:T(8,128)S(1)}, f32[12,8,128]{2,1,0:T(8,128)S(1)}, u32[]{:S(2)}, u32[]{:S(2)}) collective-permute-start(f32[12,8,128]{2,1,0:T(8,128)S(1)} %get-tuple-element.19), channel_id=1, source_target_pairs={{2,1},{4,3},{6,5},{7,8},{10,9},{12,11},{14,13},{15,16},{18,17},{20... | collective-permute-start | bytes 147464 | tf_op jit(solution)/shard_map/ppermute | solution.py:628
  14.4 19.4 %collective-permute-start.1 = (f32[12,8,128]{2,1,0:T(8,128)S(1)}, f32[12,8,128]{2,1,0:T(8,128)S(1)}, u32[]{:S(2)}, u32[]{:S(2)}) collective-permute-start(f32[12,8,128]{2,1,0:T(8,128)S(1)} %get-tuple-element.19), channel_id=1, source_target_pairs={{1,2},{3,4},{5,6},{8,7},{9,10},{11,12},{13,14},{16,15},{17,18},{19... | collective-permute-start | bytes 147464 | tf_op jit(solution)/shard_map/ppermute | solution.py:626
  15.7 25.4 %collective-permute-start.4 = (f32[35,8,128]{2,1,0:T(8,128)S(1)}, f32[35,8,128]{2,1,0:T(8,128)S(1)}, u32[]{:S(2)}, u32[]{:S(2)}) collective-permute-start(f32[35,8,128]{2,1,0:T(8,128)S(1)} %get-tuple-element.21), channel_id=1, source_target_pairs={{2,1},{4,3},{6,5},{7,8},{10,9},{12,11},{14,13},{15,16},{18,17},{20... | collective-permute-start | bytes 430088 | tf_op jit(solution)/shard_map/ppermute | solution.py:629
  30.9 27.5 %collective-permute-start.3 = (f32[35,8,128]{2,1,0:T(8,128)S(1)}, f32[35,8,128]{2,1,0:T(8,128)S(1)}, u32[]{:S(2)}, u32[]{:S(2)}) collective-permute-start(f32[35,8,128]{2,1,0:T(8,128)S(1)} %get-tuple-element.21), channel_id=1, source_target_pairs={{1,2},{3,4},{5,6},{8,7},{9,10},{11,12},{13,14},{16,15},{17,18},{19... | collective-permute-start | bytes 430088 | tf_op jit(solution)/shard_map/ppermute | solution.py:627
  34.2 24.2 %collective-permute-start.6 = (f32[35,8,128]{2,1,0:T(8,128)S(1)}, f32[35,8,128]{2,1,0:T(8,128)S(1)}, u32[]{:S(2)}, u32[]{:S(2)}) collective-permute-start(f32[35,8,128]{2,1,0:T(8,128)S(1)} %get-tuple-element.34), channel_id=1, source_target_pairs={{256,512},{512,256},{768,32},{32,768},{288,544},{544,288},{800,64}... | collective-permute-start | bytes 430088 | tf_op jit(solution)/shard_map/ppermute | solution.py:635
  39.0 19.4 %collective-permute-start.5 = (f32[35,8,128]{2,1,0:T(8,128)S(1)}, f32[35,8,128]{2,1,0:T(8,128)S(1)}, u32[]{:S(2)}, u32[]{:S(2)}) collective-permute-start(f32[35,8,128]{2,1,0:T(8,128)S(1)} %get-tuple-element.35), channel_id=1, source_target_pairs={{0,256},{256,0},{512,768},{768,512},{32,288},{288,32},{544,800},{8... | collective-permute-start | bytes 430088 | tf_op jit(solution)/shard_map/ppermute | solution.py:636
  64.8 10.3 %all-to-all-start = ((f32[4,3,8,256]{3,2,1,0:T(8,128)}), f32[4,3,8,256]{3,2,1,0:T(8,128)S(1)}, u32[]{:S(2)}, u32[]{:S(2)}) async-start(f32[4,3,8,256]{3,2,1,0:T(8,128)} %get-tuple-element.28), calls=%async_computation | async-start | bytes 196608 | tf_op jit(solution)/shard_map/all_to_all | solution.py:655

commit v6 on v5

--- a/solution.py
+++ b/solution.py
@@ -420,33 +420,30 @@
     return [mix(x[0], half_turn(x[1])), mix(half_turn(x[0]), x[1])]
 
 
-def edge_kernel(
-    raw_ref, part_ref, aux_ref, te_ref, to_ref, stoich_ref, ocean_ref, q_ref, c2_ref,
-    r2_ref, t2_ref, fc_ref, fr_ref, g_ref,
-):
+def corners(te_ref, to_ref, k):
     sub4 = subs() < 4
     swapped = odd("comp")
-
-    def corners(k):
-        te, to = te_ref[WET + 1 + k], to_ref[WET + 1 + k]
-        b, a = jnp.where(swapped, to, te), jnp.where(swapped, te, to)
-        return (
-            [
-                jnp.where(sub4, b, a),
-                jnp.where(sub4, pltpu.roll(b, 6, 0), pltpu.roll(a, 2, 0)),
-            ],
-            [
-                pltpu.roll(jnp.where(sub4, a, b), 4, 0),
-                jnp.where(sub4, pltpu.roll(b, 2, 0), pltpu.roll(a, 6, 0)),
-            ],
-        )
-
-    def raw(f):
-        x = load(raw_ref.at[f])
-        return x[:2], x[2:]
-
-    (u_c, v_c), (t_c, w_c) = corners((U + 1) // 2), corners((T + 1) // 2)
-    (u_e, u_h), (v_e, v_h), (t_e, t_h), (w_e, w_h) = [raw(f) for f in (U, V, T, WET)]
+    te, to = te_ref[WET + 1 + k], to_ref[WET + 1 + k]
+    b, a = jnp.where(swapped, to, te), jnp.where(swapped, te, to)
+    return (
+        [jnp.where(sub4, b, a), jnp.where(sub4, pltpu.roll(b, 6, 0), pltpu.roll(a, 2, 0))],
+        [
+            pltpu.roll(jnp.where(sub4, a, b), 4, 0),
+            jnp.where(sub4, pltpu.roll(b, 2, 0), pltpu.roll(a, 6, 0)),
+        ],
+    )
+
+
+def halves(ref, f):
+    x = load(ref.at[f])
+    return x[:2], x[2:]
+
+
+def ocean_kernel(
+    raw_ref, aux_ref, te_ref, to_ref, ocean_ref, fc_ref, fr_ref, t1_ref, c2_ref, r2_ref, t2_ref
+):
+    (u_c, v_c), (t_c, w_c) = corners(te_ref, to_ref, (U + 1) // 2), corners(te_ref, to_ref, (T + 1) // 2)
+    (u_e, u_h), (v_e, v_h), (t_e, t_h), (w_e, w_h) = [halves(raw_ref, f) for f in (U, V, T, WET)]
     w_s, p_e, p_h = load(aux_ref, "w_s", "p_e", "p_h")
     p_c = [0.05 * s for s in level_sum(t_c, True)]
 
@@ -466,37 +463,6 @@
     fr_e, fr_c = row_factor(v1_e, v1_c, w_e, w_c)
     save(fr_ref, fr_e + fr_c)
 
-    def advect1(f, q_c):
-        q_e, q_h = raw(f)
-        fc, fr = load(fc_ref), load(fr_ref)
-        row = row_divergence(q_e, q_c, fr[:2], fr[2:])[0]
-        col = split_divergence(q_h, q_c, fc[:2], fc[2:])
-        return minus(load(part_ref.at[f]), row + col)
-
-    c = [corners(k) for k in range(3)]
-    core_corners = [c[0][1], c[1][0], c[1][1], c[2][0], c[2][1]]
-    first = [advect1(f, core_corners[f]) for f in range(5)]
-    sun_e, sun_h = load(aux_ref, "sun_e", "sun_h")
-    w_four, sun, t1_four, gain = w_e + w_h, sun_e + sun_h, t1_e + t1_h, []
-    for i in range(4):
-        core, g = reaction([first[f][i] for f in range(5)], sun[i], t1_four[i])
-        gain.append(g)
-        for f in range(5):
-            q_ref[f, i] = (first[f][i] + 0.2 * core[f]) * w_four[i]
-    save(g_ref, gain + w_four)
-
-    def others1(k, _):
-        both = corners(k)
-        for j in range(2):
-            f = 2 * k - 1 + j
-            s = stoich_ref[f - 5]
-            g = load(g_ref)
-            out = each(lambda a, g, w: (a + s * g) * w, advect1(f, both[j]), g[:4], g[4:])
-            save(q_ref.at[f], out)
-        return 0
-
-    lax.fori_loop(3, 10, others1, 0)
-
     u1_s, u1_e, v1_s, v1_h, t1_s, _, heat2 = load(
         aux_ref, "u1_s", "u1_e", "v1_s", "v1_h", "t1_s", "sun2", "heat2"
     )
@@ -512,6 +478,7 @@
     cols = plus(next_split(t1_s, t1_e)[0], prev_split(t1_s, t1_e)[0])
     t2 = warmed(t1_s, heat2, rows, cols, w_s)
 
+    save(t1_ref, t1_e + t1_h)
     save(t2_ref, t2)
     for k, x in enumerate((u2_s, v2_s, t2)):
         for i, tile in enumerate(plain(x)):
@@ -525,8 +492,41 @@
 
 
 def last_kernel(
-    q1_ref, aux_ref, q_ref, c2_ref, r2_ref, t2_ref, stoich_ref, out_ref, g2_ref
+    raw_ref, part_ref, aux_ref, te_ref, to_ref, stoich_ref, fc_ref, fr_ref, t1_ref, q1_ref,
+    c2_ref, r2_ref, t2_ref, out_ref, q_ref, g_ref, g2_ref,
 ):
+    def advect1(f, q_c):
+        q_e, q_h = halves(raw_ref, f)
+        fc, fr = load(fc_ref), load(fr_ref)
+        row = row_divergence(q_e, q_c, fr[:2], fr[2:])[0]
+        col = split_divergence(q_h, q_c, fc[:2], fc[2:])
+        return minus(load(part_ref.at[f]), row + col)
+
+    c = [corners(te_ref, to_ref, k) for k in range(3)]
+    core_corners = [c[0][1], c[1][0], c[1][1], c[2][0], c[2][1]]
+    first = [advect1(f, core_corners[f]) for f in range(5)]
+    sun_e, sun_h = load(aux_ref, "sun_e", "sun_h")
+    w_e, w_h = halves(raw_ref, WET)
+    w_four, sun, t1_four, gain = w_e + w_h, sun_e + sun_h, load(t1_ref), []
+    for i in range(4):
+        core, g = reaction([first[f][i] for f in range(5)], sun[i], t1_four[i])
+        gain.append(g)
+        for f in range(5):
+            q_ref[f, i] = (first[f][i] + 0.2 * core[f]) * w_four[i]
+    save(g_ref, gain + w_four)
+
+    def others1(k, _):
+        both = corners(te_ref, to_ref, k)
+        for j in range(2):
+            f = 2 * k - 1 + j
+            s = stoich_ref[f - 5]
+            g = load(g_ref)
+            out = each(lambda a, g, w: (a + s * g) * w, advect1(f, both[j]), g[:4], g[4:])
+            save(q_ref.at[f], out)
+        return 0
+
+    lax.fori_loop(3, 10, others1, 0)
+
     w_s, sun2 = load(aux_ref, "w_s", "sun2")
     t2 = load(t2_ref)
 
@@ -569,18 +569,12 @@
 
 
 def far_pairs(bands, tiles):
-    group = 8
-    length = bands * (tiles // group)
-
-    def steps(tx, ty):
-        z = tx // group * bands + ty
-        return min(z, length - z)
-
     later, sooner = [], []
     for ty in range(bands):
         for a in range(1, tiles - 1, 2):
             pair = (ty * tiles + a, ty * tiles + a + 1)
-            if steps(a, ty) < steps(a + 1, ty):
+            part = 4 * (a + 1) // tiles
+            if part == 1 or (part == 2 and 4 * ty < 3 * bands):
                 pair = pair[::-1]
             later.append(pair)
             sooner.append(pair[::-1])
@@ -646,16 +640,18 @@
         [(FIELDS + 1,), (6,), (4,), (4,)],
     )(*near(packed, chip, first, rest_a, rest_b, te, to, yields))
     raw, part, q1_own, aux = near(*state)
-    rows, *rest = kernel(
-        edge_kernel,
-        [arr(comps, 3, ROWS, 256), arr(NTR, 4, *TILE)] + [arr(n, *TILE) for n in (4, 4, 2)],
-        6,
-        [(4,), (4,), (8,)],
-    )(raw, part, aux, *near(te, to, yields))
+    rows, fc, fr, t1, c2, r2, t2 = kernel(
+        ocean_kernel,
+        [arr(comps, 3, ROWS, 256)] + [arr(n, *TILE) for n in (4, 4, 4, 4, 4, 2)],
+        4,
+    )(raw, aux, *near(te, to))
     gathered = lax.all_to_all(rows, "comp", 0, 0, tiled=True)
     (tracers_out,) = kernel(
-        last_kernel, [jax.ShapeDtypeStruct((NTR, 1, ROWS, 256), jnp.float32)], 7, [(4,)]
-    )(q1_own, aux, *near(*rest, yields))
+        last_kernel,
+        [jax.ShapeDtypeStruct((NTR, 1, ROWS, 256), jnp.float32)],
+        13,
+        [(NTR, 4), (8,), (4,)],
+    )(raw, part, aux, *near(te, to, yields, fc, fr, t1), q1_own, *near(c2, r2, t2))
     return jnp.swapaxes(gathered, 0, 1).reshape(3, comps * ROWS, 256), tracers_out
 
 

time: 76 us -> 76.2 us (level)
  the two profiles are of different devices: /device:TPU:864 before, /device:TPU:271 now
where the time goes in v6:
time: 76.2 us; the launch traced here: 75.8 us
  starting transfers between devices  45 us (59%)
  waiting for transfers between devices  18.2 us (24%)
  Pallas kernels  11.3 us (15%)
    ppermute x1, starting transfers between devices, shards(): first_b = lax.ppermute(first, grid, sooner)  15.3 us
    ppermute x1, starting transfers between devices, shards(): rest_b = lax.ppermute(rest, grid, sooner)  15.1 us
    ppermute x1, waiting for transfers between devices, shards(): rest_a = lax.ppermute(rest, grid, later)  14.3 us
    pallas_call x1, Pallas kernels, shards(): kernel(last_kernel, [jax.ShapeDtypeStruct((NTR, 1, ROWS, 256), jnp.float3...  5.78 us
    all_to_all x1, starting transfers between devices, shards(): gathered = lax.all_to_all(rows, 'comp', 0, 0, tiled=True)  4.35 us
    ppermute x1, waiting for transfers between devices, shards(): rest_b = lax.ppermute(rest, grid, sooner)  3.92 us
    ppermute x1, starting transfers between devices, shards(): to = lax.ppermute(jnp.where(is_odd, down, up), axes, swaps(count, 1, place))  3.2 us
    pallas_call x1, Pallas kernels, shards(): kernel(own_kernel, [arr(FIELDS + 1, 4, *TILE), arr(NTR, 4, *TILE), arr(NT...  3.17 us
  transfers between devices with their start and end apart: 8, of which 2 were waited for; matrix products, arithmetic and copies ran while one was open for 0% of the time, Pallas kernels for 8%

profile of v6, /device:TPU:271, one launch (start us, length us, event | category | flops | bytes accessed | tf_op | source)
XLA Modules:
  0.0 75.8 jit_solution(1682200633871135655)
XLA Ops:
  0.6 1.1 %shard_map.59 = (f32[45,8,128]{2,1,0:T(8,128)S(1)}, f32[12,8,128]{2,1,0:T(8,128)S(1)}, f32[35,8,128]{2,1,0:T(8,128)S(1)}, f32[14,8,128]{2,1,0:T(8,128)S(1)}) custom-call(f32[3,32,256]{2,1,0:T(8,128)} %ocean_ref.1, f32[19,1,8,256]{3,2,1,0:T(8,128)} %tr_ref.1, s32[4,32]{1,0:T(4,128)} %bitcast.6, f32[14]{0:T(128)} %stoich_ref.1), custom_call_target="tpu_custom_call" | custom-call | tf_op jit(solution)/shard_map/pallas_call | solution.py:611
  1.8 2.6 %collective-permute-start = (f32[45,8,128]{2,1,0:T(8,128)S(1)}, f32[45,8,128]{2,1,0:T(8,128)S(1)}, u32[]{:S(2)}, u32[]{:S(2)}) collective-permute-start(f32[45,8,128]{2,1,0:T(8,128)S(1)} %get-tuple-element.20.own_ref), channel_id=1, source_target_pairs={{0,1},{1,0},{2,3},{3,2},{4,5},{5,4},{6,7},{7,6},{8,9},{9,8},{10,11... | collective-permute-start | bytes 552968 | tf_op jit(solution)/shard_map/ppermute | solution.py:624
  4.4 15.3 %collective-permute-start.2 = (f32[12,8,128]{2,1,0:T(8,128)S(1)}, f32[12,8,128]{2,1,0:T(8,128)S(1)}, u32[]{:S(2)}, u32[]{:S(2)}) collective-permute-start(f32[12,8,128]{2,1,0:T(8,128)S(1)} %get-tuple-element.21), channel_id=1, source_target_pairs={{2,1},{4,3},{6,5},{7,8},{9,10},{11,12},{13,14},{15,16},{17,18},{19... | collective-permute-start | bytes 147464 | tf_op jit(solution)/shard_map/ppermute | solution.py:622
  19.6 1.3 %collective-permute-start.1 = (f32[12,8,128]{2,1,0:T(8,128)S(1)}, f32[12,8,128]{2,1,0:T(8,128)S(1)}, u32[]{:S(2)}, u32[]{:S(2)}) collective-permute-start(f32[12,8,128]{2,1,0:T(8,128)S(1)} %get-tuple-element.21), channel_id=1, source_target_pairs={{1,2},{3,4},{5,6},{8,7},{10,9},{12,11},{14,13},{16,15},{18,17},{20... | collective-permute-start | bytes 147464 | tf_op jit(solution)/shard_map/ppermute | solution.py:620
  20.9 15.1 %collective-permute-start.4 = (f32[35,8,128]{2,1,0:T(8,128)S(1)}, f32[35,8,128]{2,1,0:T(8,128)S(1)}, u32[]{:S(2)}, u32[]{:S(2)}) collective-permute-start(f32[35,8,128]{2,1,0:T(8,128)S(1)} %get-tuple-element.23), channel_id=1, source_target_pairs={{2,1},{4,3},{6,5},{7,8},{9,10},{11,12},{13,14},{15,16},{17,18},{19... | collective-permute-start | bytes 430088 | tf_op jit(solution)/shard_map/ppermute | solution.py:623
  36.0 1.3 %collective-permute-start.3 = (f32[35,8,128]{2,1,0:T(8,128)S(1)}, f32[35,8,128]{2,1,0:T(8,128)S(1)}, u32[]{:S(2)}, u32[]{:S(2)}) collective-permute-start(f32[35,8,128]{2,1,0:T(8,128)S(1)} %get-tuple-element.23), channel_id=1, source_target_pairs={{1,2},{3,4},{5,6},{8,7},{10,9},{12,11},{14,13},{16,15},{18,17},{20... | collective-permute-start | bytes 430088 | tf_op jit(solution)/shard_map/ppermute | solution.py:621
  37.3 0.0 collective-permute-done.2.cb_ref
  37.3 0.0 collective-permute-done.1.ca_ref
  37.4 0.0 collective-permute-done.chip_ref
  37.4 0.2 shard_map.60
  37.6 3.2 %collective-permute-start.6 = (f32[35,8,128]{2,1,0:T(8,128)S(1)}, f32[35,8,128]{2,1,0:T(8,128)S(1)}, u32[]{:S(2)}, u32[]{:S(2)}) collective-permute-start(f32[35,8,128]{2,1,0:T(8,128)S(1)} %get-tuple-element.38), channel_id=1, source_target_pairs={{256,512},{512,256},{768,32},{32,768},{288,544},{544,288},{800,64}... | collective-permute-start | bytes 430088 | tf_op jit(solution)/shard_map/ppermute | solution.py:629
  40.9 1.9 %collective-permute-start.5 = (f32[35,8,128]{2,1,0:T(8,128)S(1)}, f32[35,8,128]{2,1,0:T(8,128)S(1)}, u32[]{:S(2)}, u32[]{:S(2)}) collective-permute-start(f32[35,8,128]{2,1,0:T(8,128)S(1)} %get-tuple-element.39), channel_id=1, source_target_pairs={{0,256},{256,0},{512,768},{768,512},{32,288},{288,32},{544,800},{8... | collective-permute-start | bytes 430088 | tf_op jit(solution)/shard_map/ppermute | solution.py:630
  42.8 3.9 %collective-permute-done.4.rb_ref = f32[35,8,128]{2,1,0:T(8,128)S(1)} collective-permute-done((f32[35,8,128]{2,1,0:T(8,128)S(1)}, f32[35,8,128]{2,1,0:T(8,128)S(1)}, u32[]{:S(2)}, u32[]{:S(2)}) %collective-permute-start.4) | collective-permute-done | bytes 143392 | tf_op jit(solution)/shard_map/ppermute | solution.py:623
  46.7 14.3 %collective-permute-done.3.ra_ref = f32[35,8,128]{2,1,0:T(8,128)S(1)} collective-permute-done((f32[35,8,128]{2,1,0:T(8,128)S(1)}, f32[35,8,128]{2,1,0:T(8,128)S(1)}, u32[]{:S(2)}, u32[]{:S(2)}) %collective-permute-start.3) | collective-permute-done | bytes 143392 | tf_op jit(solution)/shard_map/ppermute | solution.py:621
  60.9 0.0 collective-permute-done.6.to_ref
  61.0 0.0 collective-permute-done.5.te_ref
  61.0 3.2 %shard_map.61 = (f32[23,4,8,128]{3,2,1,0:T(8,128)S(1)}, f32[19,4,8,128]{3,2,1,0:T(8,128)S(1)}, f32[19,2,8,128]{3,2,1,0:T(8,128)S(1)}, f32[32,8,128]{2,1,0:T(8,128)S(1)}) custom-call(f32[45,8,128]{2,1,0:T(8,128)S(1)} %get-tuple-element.20.own_ref, f32[45,8,128]{2,1,0:T(8,128)S(1)} %collective-permute-done.chip_ref, ...), custom_call_target="tpu_custom_call" | custom-call | tf_op jit(solution)/shard_map/pallas_call | solution.py:631
  64.1 0.9 %shard_map.62 = (f32[4,3,8,256]{3,2,1,0:T(8,128)}, f32[4,8,128]{2,1,0:T(8,128)S(1)}, f32[4,8,128]{2,1,0:T(8,128)S(1)}, f32[4,8,128]{2,1,0:T(8,128)S(1)}, f32[4,8...) custom-call(f32[23,4,8,128]{3,2,1,0:T(8,128)S(1)} %get-tuple-element.27.raw_ref, ...), custom_call_target="tpu_custom_call" | custom-call | tf_op jit(solution)/shard_map/pallas_call | solution.py:643
  65.1 4.3 %all-to-all-start = ((f32[4,3,8,256]{3,2,1,0:T(8,128)}), f32[4,3,8,256]{3,2,1,0:T(8,128)S(1)}, u32[]{:S(2)}, u32[]{:S(2)}) async-start(f32[4,3,8,256]{3,2,1,0:T(8,128)} %get-tuple-element.29), calls=%async_computation | async-start | bytes 196608 | tf_op jit(solution)/shard_map/all_to_all | solution.py:648
  69.4 5.8 %shard_map.63 = f32[19,1,8,256]{3,2,1,0:T(8,128)} custom-call(f32[23,4,8,128]{3,2,1,0:T(8,128)S(1)} %get-tuple-element.27.raw_ref, f32[19,4,8,128]{3,2,1,0:T(8,128)S(1)} %get-tuple-element.30.part_ref, f32[32,8,128]{2,1,0:T(8,128)S(1)} %get-tuple-element.28.aux_ref, f32[35,8,128]{2,1,0:T(8,128)S(1)} %collective-permute-done.5.te_ref, ...), custom_call_target="tpu_custom_call" | custom-call | tf_op jit(solution)/shard_map/pallas_call | solution.py:649
  75.2 0.0 all-to-all-done
  75.2 0.6 copy_bitcast_fusion
  (1 shorter events, 0.0 us)
Async XLA Ops:
  1.8 35.6 %collective-permute-start = (f32[45,8,128]{2,1,0:T(8,128)S(1)}, f32[45,8,128]{2,1,0:T(8,128)S(1)}, u32[]{:S(2)}, u32[]{:S(2)}) collective-permute-start(f32[45,8,128]{2,1,0:T(8,128)S(1)} %get-tuple-element.20.own_ref), channel_id=1, source_target_pairs={{0,1},{1,0},{2,3},{3,2},{4,5},{5,4},{6,7},{7,6},{8,9},{9,8},{10,11... | collective-permute-start | bytes 552968 | tf_op jit(solution)/shard_map/ppermute | solution.py:624
  4.4 33.0 %collective-permute-start.2 = (f32[12,8,128]{2,1,0:T(8,128)S(1)}, f32[12,8,128]{2,1,0:T(8,128)S(1)}, u32[]{:S(2)}, u32[]{:S(2)}) collective-permute-start(f32[12,8,128]{2,1,0:T(8,128)S(1)} %get-tuple-element.21), channel_id=1, source_target_pairs={{2,1},{4,3},{6,5},{7,8},{9,10},{11,12},{13,14},{15,16},{17,18},{19... | collective-permute-start | bytes 147464 | tf_op jit(solution)/shard_map/ppermute | solution.py:622
  19.6 17.7 %collective-permute-start.1 = (f32[12,8,128]{2,1,0:T(8,128)S(1)}, f32[12,8,128]{2,1,0:T(8,128)S(1)}, u32[]{:S(2)}, u32[]{:S(2)}) collective-permute-start(f32[12,8,128]{2,1,0:T(8,128)S(1)} %get-tuple-element.21), channel_id=1, source_target_pairs={{1,2},{3,4},{5,6},{8,7},{10,9},{12,11},{14,13},{16,15},{18,17},{20... | collective-permute-start | bytes 147464 | tf_op jit(solution)/shard_map/ppermute | solution.py:620
  20.9 25.8 %collective-permute-start.4 = (f32[35,8,128]{2,1,0:T(8,128)S(1)}, f32[35,8,128]{2,1,0:T(8,128)S(1)}, u32[]{:S(2)}, u32[]{:S(2)}) collective-permute-start(f32[35,8,128]{2,1,0:T(8,128)S(1)} %get-tuple-element.23), channel_id=1, source_target_pairs={{2,1},{4,3},{6,5},{7,8},{9,10},{11,12},{13,14},{15,16},{17,18},{19... | collective-permute-start | bytes 430088 | tf_op jit(solution)/shard_map/ppermute | solution.py:623
  36.0 24.9 %collective-permute-start.3 = (f32[35,8,128]{2,1,0:T(8,128)S(1)}, f32[35,8,128]{2,1,0:T(8,128)S(1)}, u32[]{:S(2)}, u32[]{:S(2)}) collective-permute-start(f32[35,8,128]{2,1,0:T(8,128)S(1)} %get-tuple-element.23), channel_id=1, source_target_pairs={{1,2},{3,4},{5,6},{8,7},{10,9},{12,11},{14,13},{16,15},{18,17},{20... | collective-permute-start | bytes 430088 | tf_op jit(solution)/shard_map/ppermute | solution.py:621
  37.6 23.3 %collective-permute-start.6 = (f32[35,8,128]{2,1,0:T(8,128)S(1)}, f32[35,8,128]{2,1,0:T(8,128)S(1)}, u32[]{:S(2)}, u32[]{:S(2)}) collective-permute-start(f32[35,8,128]{2,1,0:T(8,128)S(1)} %get-tuple-element.38), channel_id=1, source_target_pairs={{256,512},{512,256},{768,32},{32,768},{288,544},{544,288},{800,64}... | collective-permute-start | bytes 430088 | tf_op jit(solution)/shard_map/ppermute | solution.py:629
  40.9 20.1 %collective-permute-start.5 = (f32[35,8,128]{2,1,0:T(8,128)S(1)}, f32[35,8,128]{2,1,0:T(8,128)S(1)}, u32[]{:S(2)}, u32[]{:S(2)}) collective-permute-start(f32[35,8,128]{2,1,0:T(8,128)S(1)} %get-tuple-element.39), channel_id=1, source_target_pairs={{0,256},{256,0},{512,768},{768,512},{32,288},{288,32},{544,800},{8... | collective-permute-start | bytes 430088 | tf_op jit(solution)/shard_map/ppermute | solution.py:630
  65.1 10.1 %all-to-all-start = ((f32[4,3,8,256]{3,2,1,0:T(8,128)}), f32[4,3,8,256]{3,2,1,0:T(8,128)S(1)}, u32[]{:S(2)}, u32[]{:S(2)}) async-start(f32[4,3,8,256]{3,2,1,0:T(8,128)} %get-tuple-element.29), calls=%async_computation | async-start | bytes 196608 | tf_op jit(solution)/shard_map/all_to_all | solution.py:648

commit v7 on v6

--- a/solution.py
+++ b/solution.py
@@ -315,12 +315,11 @@
     return [[ref[2 * AUX.index(n)], ref[2 * AUX.index(n) + 1]] for n in names]
 
 
-def own_kernel(
-    own_ref, chip_ref, first_ref, ra_ref, rb_ref, te_ref, to_ref, stoich_ref, raw_ref, part_ref,
-    q1_ref, aux_ref, near_ref, fc_ref, fr_ref, g_ref,
+def cols_kernel(
+    own_ref, chip_ref, first_ref, ra_ref, rb_ref, s_ref, e_ref, part_ref, aux_ref, near_ref,
+    fc_ref,
 ):
     flip = odd("tx")
-    even = jnp.logical_not(odd("comp"))
     mid = middle()
     for k in range(PAIRS):
         c, r = first_ref[k], ra_ref[k] + rb_ref[k]
@@ -344,11 +343,6 @@
 
     def wide(f):
         return arrange(*zip(*blocks(f)))
-
-    def halo(f):
-        first = (subs() < 4) == even
-        te, to = te_ref[f], to_ref[f]
-        return [jnp.where(first, te, to), pltpu.roll(jnp.where(first, to, te), 4, 0)]
 
     u_w, v_w, t_w = [wide(f) for f in (U, V, T)]
     far = wet_tiles(ra_ref[PAIRS + FIELDS] + rb_ref[PAIRS + FIELDS])
@@ -357,37 +351,63 @@
     west = [jnp.where(flip, c, d) for c, d in zip(close, far)]
     east = [jnp.where(flip, d, c) for c, d in zip(close, far)]
     w_w = arrange(*zip(west, own, east))
+    for f, x in ((U, u_w), (V, v_w), (T, t_w), (WET, w_w)):
+        save(s_ref.at[f], own_of(x))
+        save(e_ref.at[f], edge_of(x))
+    p_w = [0.05 * s for s in level_sum(t_w, True)]
+    u1_w = east_speed(u_w, v_w, next_col(p_w), prev_col(p_w), w_w)
+    around = plus(next_col(t_w), prev_col(t_w))
+    both = [own_of(x) + edge_of(x) for x in (p_w, u1_w, around)]
+    save(aux_ref, both[0] + both[1] + both[2])
+    save(fc_ref, col_factor(u1_w, w_w))
+
+    def one(f, _):
+        q_w = wide(f)
+        q_s, q_e = own_of(q_w), edge_of(q_w)
+        col = col_divergence(q_w, load(fc_ref))
+        save(s_ref.at[f], q_s)
+        save(e_ref.at[f], q_e)
+        save(part_ref.at[f], minus(q_s, own_of(col)) + minus(q_e, edge_of(col)))
+        return 0
+
+    one(0, 0)
+    lax.fori_loop(1, NTR, one, 0, unroll=6)
+
+
+def own_kernel(
+    s_ref, e_ref, cols_ref, caux_ref, te_ref, to_ref, stoich_ref, raw_ref, part_ref, q1_ref,
+    aux_ref, fr_ref, g_ref,
+):
+    even = jnp.logical_not(odd("comp"))
+
+    def halo(f):
+        first = (subs() < 4) == even
+        te, to = te_ref[f], to_ref[f]
+        return [jnp.where(first, te, to), pltpu.roll(jnp.where(first, to, te), 4, 0)]
+
+    u_s, v_s, t_s, w_s = [load(s_ref.at[f]) for f in (U, V, T, WET)]
     u_h, v_h, t_h, w_h = [halo(f) for f in (U, V, T, WET)]
-    u_s, v_s, t_s, w_s = [own_of(x) for x in (u_w, v_w, t_w, w_w)]
-    w_e = edge_of(w_w)
-    for f, wd, h in ((U, u_w, u_h), (V, v_w, v_h), (T, t_w, t_h), (WET, w_w, w_h)):
-        save(raw_ref.at[f], edge_of(wd) + h)
-
-    press = [0.05 * s for s in level_sum(t_w + t_h, True)]
-    p_w, p_h = press[:6], press[6:]
-    p_s = own_of(p_w)
-    q_w, q_h = wide(2), halo(2)
-    sun, heat = optics(own_of(q_w) + edge_of(q_w) + q_h, w_s + w_e + w_h)
-    u1_w = east_speed(u_w, v_w, next_col(p_w), prev_col(p_w), w_w)
+    w_e = load(e_ref.at[WET])
+    for f, h in ((U, u_h), (V, v_h), (T, t_h), (WET, w_h)):
+        save(raw_ref.at[f], load(e_ref.at[f]) + h)
+    c = load(caux_ref)
+    p_s, p_e, u1_s, u1_e, cols_s, cols_e = [c[i : i + 2] for i in range(0, 12, 2)]
+    p_h = [0.05 * s for s in level_sum(t_h, True)]
+    sun, heat = optics(load(s_ref.at[2]) + load(e_ref.at[2]) + halo(2), w_s + w_e + w_h)
     (n_s, n_h), (b_s, b_h) = next_row(p_s, p_h), prev_row(p_s, p_h)
     v1_s = north_speed(u_s, v_s, n_s, b_s, w_s)
     v1_h = north_speed(u_h, v_h, n_h, b_h, w_h)
     (n_s, n_h), (b_s, b_h) = next_row(t_s, t_h), prev_row(t_s, t_h)
-    around = plus(next_col(t_w), prev_col(t_w))
-    t1_s = warmed(t_s, heat[:2], plus(n_s, b_s), own_of(around), w_s)
-    save(fc_ref, col_factor(u1_w, w_w))
+    t1_s = warmed(t_s, heat[:2], plus(n_s, b_s), cols_s, w_s)
     fr_s, fr_h = row_factor(v1_s, v1_h, w_s, w_h)
     save(fr_ref, fr_s + fr_h)
 
     def advect(f):
-        q_w, q_h = wide(f), halo(f)
-        q_s, q_e = own_of(q_w), edge_of(q_w)
-        col = col_divergence(q_w, load(fc_ref))
-        fr = load(fr_ref)
-        r_s, r_h = row_divergence(q_s, q_h, fr[:2], fr[2:])
-        save(raw_ref.at[f], q_e + q_h)
-        save(part_ref.at[f], minus(q_e, edge_of(col)) + minus(q_h, r_h))
-        return minus(minus(q_s, own_of(col)), r_s)
+        q_h, c, fr = halo(f), load(cols_ref.at[f]), load(fr_ref)
+        r_s, r_h = row_divergence(load(s_ref.at[f]), q_h, fr[:2], fr[2:])
+        save(raw_ref.at[f], load(e_ref.at[f]) + q_h)
+        save(part_ref.at[f], c[2:] + minus(q_h, r_h))
+        return minus(c[:2], r_s)
 
     first = [advect(f) for f in range(5)]
     gain, chloro = [], []
@@ -400,9 +420,9 @@
     sun2, heat2 = optics(chloro, w_s)
     save(g_ref, gain + w_s)
     values = dict(
-        w_s=w_s, p_e=edge_of(p_w), p_h=p_h, sun_e=sun[2:4], sun_h=sun[4:], heat_e=heat[2:4],
-        heat_h=heat[4:], cols_e=edge_of(around), rows_h=plus(n_h, b_h), u1_s=own_of(u1_w),
-        u1_e=edge_of(u1_w), v1_s=v1_s, v1_h=v1_h, t1_s=t1_s, sun2=sun2, heat2=heat2,
+        w_s=w_s, p_e=p_e, p_h=p_h, sun_e=sun[2:4], sun_h=sun[4:], heat_e=heat[2:4],
+        heat_h=heat[4:], cols_e=cols_e, rows_h=plus(n_h, b_h), u1_s=u1_s,
+        u1_e=u1_e, v1_s=v1_s, v1_h=v1_h, t1_s=t1_s, sun2=sun2, heat2=heat2,
     )
     save(aux_ref, [x for n in AUX for x in values[n]])
 
@@ -525,7 +545,7 @@
             save(q_ref.at[f], out)
         return 0
 
-    lax.fori_loop(3, 10, others1, 0)
+    lax.fori_loop(3, 10, others1, 0, unroll=7)
 
     w_s, sun2 = load(aux_ref, "w_s", "sun2")
     t2 = load(t2_ref)
@@ -558,7 +578,7 @@
         finish(f, each(lambda a, g, w: (a + s * g) * w, advect2(f), k[:2], k[2:]))
         return 0
 
-    lax.fori_loop(5, NTR, others2, 0, unroll=2)
+    lax.fori_loop(5, NTR, others2, 0, unroll=7)
 
 
 def swaps(count, first, place=lambda i: i):
@@ -628,6 +648,12 @@
     is_odd = odd("comp")
     to = lax.ppermute(jnp.where(is_odd, down, up), axes, swaps(count, 1, place))
     te = lax.ppermute(jnp.where(is_odd, up, down), axes, swaps(count, 0, place))
+    columns = kernel(
+        cols_kernel,
+        [arr(FIELDS + 1, 2, *TILE), arr(FIELDS + 1, 2, *TILE), arr(NTR, 4, *TILE), arr(12, *TILE)],
+        5,
+        [(FIELDS + 1,), (6,)],
+    )(*near(packed, chip, first, rest_a, rest_b))
     state = kernel(
         own_kernel,
         [
@@ -636,9 +662,9 @@
             arr(NTR, 2, *TILE),
             arr(2 * len(AUX), *TILE),
         ],
-        8,
-        [(FIELDS + 1,), (6,), (4,), (4,)],
-    )(*near(packed, chip, first, rest_a, rest_b, te, to, yields))
+        7,
+        [(4,), (4,)],
+    )(*near(*columns, te, to, yields))
     raw, part, q1_own, aux = near(*state)
     rows, fc, fr, t1, c2, r2, t2 = kernel(
         ocean_kernel,

time: 76.2 us -> 73.8 us (0.969)
  the two profiles are of different devices: /device:TPU:271 before, /device:TPU:263 now
where the time goes in v7:
time: 73.8 us; the launch traced here: 73.5 us
  starting transfers between devices  46 us (62%)
  waiting for transfers between devices  19.7 us (27%)
  Pallas kernels  6.33 us (9%)
  between operations  0.75 us (1%)
    ppermute x1, starting transfers between devices, shards(): first_b = lax.ppermute(first, grid, sooner)  15.3 us
    ppermute x1, starting transfers between devices, shards(): rest_b = lax.ppermute(rest, grid, sooner)  15.1 us
    ppermute x1, waiting for transfers between devices, shards(): rest_a = lax.ppermute(rest, grid, later)  14.4 us
    ppermute x1, starting transfers between devices, shards(): te = lax.ppermute(jnp.where(is_odd, up, down), axes, swaps(count, 0, place))  5.74 us
    all_to_all x1, starting transfers between devices, shards(): gathered = lax.all_to_all(rows, 'comp', 0, 0, tiled=True)  4.08 us
    all_to_all x1, waiting for transfers between devices, shards(): gathered = lax.all_to_all(rows, 'comp', 0, 0, tiled=True)  2.71 us
    ppermute x1, waiting for transfers between devices, shards(): rest_b = lax.ppermute(rest, grid, sooner)  2.64 us
    ppermute x1, starting transfers between devices, shards(): chip = lax.ppermute(packed, 'tx', swaps(tiles, 0))  2.58 us
  transfers between devices with their start and end apart: 8, of which 3 were waited for; matrix products, arithmetic and copies ran while one was open for 0% of the time, Pallas kernels for 5%

profile of v7, /device:TPU:263, one launch (start us, length us, event | category | flops | bytes accessed | tf_op | source)
XLA Modules:
  0.0 73.5 jit_solution(15492329221400735716)
XLA Ops:
  0.6 1.1 %shard_map.59 = (f32[45,8,128]{2,1,0:T(8,128)S(1)}, f32[12,8,128]{2,1,0:T(8,128)S(1)}, f32[35,8,128]{2,1,0:T(8,128)S(1)}, f32[14,8,128]{2,1,0:T(8,128)S(1)}) custom-call(f32[3,32,256]{2,1,0:T(8,128)} %ocean_ref.1, f32[19,1,8,256]{3,2,1,0:T(8,128)} %tr_ref.1, s32[4,32]{1,0:T(4,128)} %bitcast.6, f32[14]{0:T(128)} %stoich_ref.1), custom_call_target="tpu_custom_call" | custom-call | tf_op jit(solution)/shard_map/pallas_call | solution.py:631
  1.8 2.6 %collective-permute-start = (f32[45,8,128]{2,1,0:T(8,128)S(1)}, f32[45,8,128]{2,1,0:T(8,128)S(1)}, u32[]{:S(2)}, u32[]{:S(2)}) collective-permute-start(f32[45,8,128]{2,1,0:T(8,128)S(1)} %get-tuple-element.24.own_ref), channel_id=1, source_target_pairs={{0,1},{1,0},{2,3},{3,2},{4,5},{5,4},{6,7},{7,6},{8,9},{9,8},{10,11... | collective-permute-start | bytes 552968 | tf_op jit(solution)/shard_map/ppermute | solution.py:644
  4.4 15.3 %collective-permute-start.2 = (f32[12,8,128]{2,1,0:T(8,128)S(1)}, f32[12,8,128]{2,1,0:T(8,128)S(1)}, u32[]{:S(2)}, u32[]{:S(2)}) collective-permute-start(f32[12,8,128]{2,1,0:T(8,128)S(1)} %get-tuple-element.25), channel_id=1, source_target_pairs={{2,1},{4,3},{6,5},{7,8},{9,10},{11,12},{13,14},{15,16},{17,18},{19... | collective-permute-start | bytes 147464 | tf_op jit(solution)/shard_map/ppermute | solution.py:642
  19.6 1.3 %collective-permute-start.1 = (f32[12,8,128]{2,1,0:T(8,128)S(1)}, f32[12,8,128]{2,1,0:T(8,128)S(1)}, u32[]{:S(2)}, u32[]{:S(2)}) collective-permute-start(f32[12,8,128]{2,1,0:T(8,128)S(1)} %get-tuple-element.25), channel_id=1, source_target_pairs={{1,2},{3,4},{5,6},{8,7},{10,9},{12,11},{14,13},{16,15},{18,17},{20... | collective-permute-start | bytes 147464 | tf_op jit(solution)/shard_map/ppermute | solution.py:640
  20.9 15.1 %collective-permute-start.4 = (f32[35,8,128]{2,1,0:T(8,128)S(1)}, f32[35,8,128]{2,1,0:T(8,128)S(1)}, u32[]{:S(2)}, u32[]{:S(2)}) collective-permute-start(f32[35,8,128]{2,1,0:T(8,128)S(1)} %get-tuple-element.27), channel_id=1, source_target_pairs={{2,1},{4,3},{6,5},{7,8},{9,10},{11,12},{13,14},{15,16},{17,18},{19... | collective-permute-start | bytes 430088 | tf_op jit(solution)/shard_map/ppermute | solution.py:643
  36.0 1.3 %collective-permute-start.3 = (f32[35,8,128]{2,1,0:T(8,128)S(1)}, f32[35,8,128]{2,1,0:T(8,128)S(1)}, u32[]{:S(2)}, u32[]{:S(2)}) collective-permute-start(f32[35,8,128]{2,1,0:T(8,128)S(1)} %get-tuple-element.27), channel_id=1, source_target_pairs={{1,2},{3,4},{5,6},{8,7},{10,9},{12,11},{14,13},{16,15},{18,17},{20... | collective-permute-start | bytes 430088 | tf_op jit(solution)/shard_map/ppermute | solution.py:641
  37.3 0.0 collective-permute-done.2.cb_ref
  37.3 0.0 collective-permute-done.1.ca_ref
  37.4 0.0 collective-permute-done.chip_ref
  37.4 0.2 shard_map.60
  37.6 0.7 collective-permute-start.6
  38.3 5.7 %collective-permute-start.5 = (f32[35,8,128]{2,1,0:T(8,128)S(1)}, f32[35,8,128]{2,1,0:T(8,128)S(1)}, u32[]{:S(2)}, u32[]{:S(2)}) collective-permute-start(f32[35,8,128]{2,1,0:T(8,128)S(1)} %get-tuple-element.47), channel_id=1, source_target_pairs={{0,256},{256,0},{512,768},{768,512},{32,288},{288,32},{544,800},{8... | collective-permute-start | bytes 430088 | tf_op jit(solution)/shard_map/ppermute | solution.py:650
  44.1 2.6 %collective-permute-done.4.rb_ref = f32[35,8,128]{2,1,0:T(8,128)S(1)} collective-permute-done((f32[35,8,128]{2,1,0:T(8,128)S(1)}, f32[35,8,128]{2,1,0:T(8,128)S(1)}, u32[]{:S(2)}, u32[]{:S(2)}) %collective-permute-start.4) | collective-permute-done | bytes 143392 | tf_op jit(solution)/shard_map/ppermute | solution.py:643
  46.7 14.4 %collective-permute-done.3.ra_ref = f32[35,8,128]{2,1,0:T(8,128)S(1)} collective-permute-done((f32[35,8,128]{2,1,0:T(8,128)S(1)}, f32[35,8,128]{2,1,0:T(8,128)S(1)}, u32[]{:S(2)}, u32[]{:S(2)}) %collective-permute-start.3) | collective-permute-done | bytes 143392 | tf_op jit(solution)/shard_map/ppermute | solution.py:641
  61.0 1.5 %shard_map.61 = (f32[23,2,8,128]{3,2,1,0:T(8,128)S(1)}, f32[23,2,8,128]{3,2,1,0:T(8,128)S(1)}, f32[19,4,8,128]{3,2,1,0:T(8,128)S(1)}, f32[12,8,128]{2,1,0:T(8,128)S(1)}) custom-call(f32[45,8,128]{2,1,0:T(8,128)S(1)} %get-tuple-element.24.own_ref, f32[45,8,128]{2,1,0:T(8,128)S(1)} %collective-permute-done.chip_ref, ...), custom_call_target="tpu_custom_call" | custom-call | tf_op jit(solution)/shard_map/pallas_call | solution.py:651
  62.5 0.0 collective-permute-done.6.to_ref
  62.6 0.0 collective-permute-done.5.te_ref
  62.6 0.6 shard_map.62
  63.2 0.9 %shard_map.63 = (f32[4,3,8,256]{3,2,1,0:T(8,128)}, f32[4,8,128]{2,1,0:T(8,128)S(1)}, f32[4,8,128]{2,1,0:T(8,128)S(1)}, f32[4,8,128]{2,1,0:T(8,128)S(1)}, f32[4,8...) custom-call(f32[23,4,8,128]{3,2,1,0:T(8,128)S(1)} %get-tuple-element.35.raw_ref, ...), custom_call_target="tpu_custom_call" | custom-call | tf_op jit(solution)/shard_map/pallas_call | solution.py:669
  64.1 4.1 %all-to-all-start = ((f32[4,3,8,256]{3,2,1,0:T(8,128)}), f32[4,3,8,256]{3,2,1,0:T(8,128)S(1)}, u32[]{:S(2)}, u32[]{:S(2)}) async-start(f32[4,3,8,256]{3,2,1,0:T(8,128)} %get-tuple-element.37), calls=%async_computation | async-start | bytes 196608 | tf_op jit(solution)/shard_map/all_to_all | solution.py:674
  68.2 1.9 %shard_map.64 = f32[19,1,8,256]{3,2,1,0:T(8,128)} custom-call(f32[23,4,8,128]{3,2,1,0:T(8,128)S(1)} %get-tuple-element.35.raw_ref, f32[19,4,8,128]{3,2,1,0:T(8,128)S(1)} %get-tuple-element.38.part_ref, f32[32,8,128]{2,1,0:T(8,128)S(1)} %get-tuple-element.36.aux_ref, f32[35,8,128]{2,1,0:T(8,128)S(1)} %collective-permute-done.5.te_ref, ...), custom_call_target="tpu_custom_call" | custom-call | tf_op jit(solution)/shard_map/pallas_call | solution.py:675
  70.1 2.7 %all-to-all-done = f32[4,3,8,256]{3,2,1,0:T(8,128)S(1)} async-done(((f32[4,3,8,256]{3,2,1,0:T(8,128)}), f32[4,3,8,256]{3,2,1,0:T(8,128)S(1)}, u32[]{:S(2)}, u32[]{:S(2)}) %all-to-all-start) | async-done | bytes 98336 | tf_op jit(solution)/shard_map/all_to_all | solution.py:674
  72.8 0.6 copy_bitcast_fusion
  (1 shorter events, 0.0 us)
Async XLA Ops:
  1.8 35.6 %collective-permute-start = (f32[45,8,128]{2,1,0:T(8,128)S(1)}, f32[45,8,128]{2,1,0:T(8,128)S(1)}, u32[]{:S(2)}, u32[]{:S(2)}) collective-permute-start(f32[45,8,128]{2,1,0:T(8,128)S(1)} %get-tuple-element.24.own_ref), channel_id=1, source_target_pairs={{0,1},{1,0},{2,3},{3,2},{4,5},{5,4},{6,7},{7,6},{8,9},{9,8},{10,11... | collective-permute-start | bytes 552968 | tf_op jit(solution)/shard_map/ppermute | solution.py:644
  4.4 33.0 %collective-permute-start.2 = (f32[12,8,128]{2,1,0:T(8,128)S(1)}, f32[12,8,128]{2,1,0:T(8,128)S(1)}, u32[]{:S(2)}, u32[]{:S(2)}) collective-permute-start(f32[12,8,128]{2,1,0:T(8,128)S(1)} %get-tuple-element.25), channel_id=1, source_target_pairs={{2,1},{4,3},{6,5},{7,8},{9,10},{11,12},{13,14},{15,16},{17,18},{19... | collective-permute-start | bytes 147464 | tf_op jit(solution)/shard_map/ppermute | solution.py:642
  19.6 17.7 %collective-permute-start.1 = (f32[12,8,128]{2,1,0:T(8,128)S(1)}, f32[12,8,128]{2,1,0:T(8,128)S(1)}, u32[]{:S(2)}, u32[]{:S(2)}) collective-permute-start(f32[12,8,128]{2,1,0:T(8,128)S(1)} %get-tuple-element.25), channel_id=1, source_target_pairs={{1,2},{3,4},{5,6},{8,7},{10,9},{12,11},{14,13},{16,15},{18,17},{20... | collective-permute-start | bytes 147464 | tf_op jit(solution)/shard_map/ppermute | solution.py:640
  20.9 25.8 %collective-permute-start.4 = (f32[35,8,128]{2,1,0:T(8,128)S(1)}, f32[35,8,128]{2,1,0:T(8,128)S(1)}, u32[]{:S(2)}, u32[]{:S(2)}) collective-permute-start(f32[35,8,128]{2,1,0:T(8,128)S(1)} %get-tuple-element.27), channel_id=1, source_target_pairs={{2,1},{4,3},{6,5},{7,8},{9,10},{11,12},{13,14},{15,16},{17,18},{19... | collective-permute-start | bytes 430088 | tf_op jit(solution)/shard_map/ppermute | solution.py:643
  36.0 25.0 %collective-permute-start.3 = (f32[35,8,128]{2,1,0:T(8,128)S(1)}, f32[35,8,128]{2,1,0:T(8,128)S(1)}, u32[]{:S(2)}, u32[]{:S(2)}) collective-permute-start(f32[35,8,128]{2,1,0:T(8,128)S(1)} %get-tuple-element.27), channel_id=1, source_target_pairs={{1,2},{3,4},{5,6},{8,7},{10,9},{12,11},{14,13},{16,15},{18,17},{20... | collective-permute-start | bytes 430088 | tf_op jit(solution)/shard_map/ppermute | solution.py:641
  37.6 24.9 %collective-permute-start.6 = (f32[35,8,128]{2,1,0:T(8,128)S(1)}, f32[35,8,128]{2,1,0:T(8,128)S(1)}, u32[]{:S(2)}, u32[]{:S(2)}) collective-permute-start(f32[35,8,128]{2,1,0:T(8,128)S(1)} %get-tuple-element.46), channel_id=1, source_target_pairs={{256,512},{512,256},{768,32},{32,768},{288,544},{544,288},{800,64}... | collective-permute-start | bytes 430088 | tf_op jit(solution)/shard_map/ppermute | solution.py:649
  38.3 24.2 %collective-permute-start.5 = (f32[35,8,128]{2,1,0:T(8,128)S(1)}, f32[35,8,128]{2,1,0:T(8,128)S(1)}, u32[]{:S(2)}, u32[]{:S(2)}) collective-permute-start(f32[35,8,128]{2,1,0:T(8,128)S(1)} %get-tuple-element.47), channel_id=1, source_target_pairs={{0,256},{256,0},{512,768},{768,512},{32,288},{288,32},{544,800},{8... | collective-permute-start | bytes 430088 | tf_op jit(solution)/shard_map/ppermute | solution.py:650
  64.1 8.7 %all-to-all-start = ((f32[4,3,8,256]{3,2,1,0:T(8,128)}), f32[4,3,8,256]{3,2,1,0:T(8,128)S(1)}, u32[]{:S(2)}, u32[]{:S(2)}) async-start(f32[4,3,8,256]{3,2,1,0:T(8,128)} %get-tuple-element.37), calls=%async_computation | async-start | bytes 196608 | tf_op jit(solution)/shard_map/all_to_all | solution.py:674
